TPU v7x, 32 devices: a whole 2x2x4 slice. The times are simulated.
32 devices in a mesh: dp: 8 (over y, x, core), mp: 4 (over z).
Axes of the slice: x: 2, y: 2, z: 4, core: 2. Of those that a mesh axis runs over, the one named last changes fastest.
Arguments:
- tokens: bfloat16 [8, 2048, 768], P('dp', 'mp'), may hold values from -6 to 6
- gain_first: float32 [768], replicated, may hold values from 0.5 to 1.5
- input_weight: bfloat16 [768, 3, 768], P(None, None, 'mp'), may hold values from -0.21875 to 0.21875
- kernel: float32 [768, 2048], P('mp'), may hold values from -0.25 to 0.25
- pad_len: int32 [768], P('mp'), may hold values from 0 to 1023
- output_weight: bfloat16 [768, 768], P('mp'), may hold values from -0.21875 to 0.21875
- gain_second: float32 [768], replicated, may hold values from 0.5 to 1.5
- up_weight: bfloat16 [768, 3072], P(None, 'mp'), may hold values from -0.21875 to 0.21875
- down_weight: bfloat16 [3072, 768], P('mp'), may hold values from -0.109375 to 0.109375
- cotangent: bfloat16 [8, 2048, 768], P('dp', 'mp'), may hold values from -6 to 6
Outputs:
- block_out: bfloat16 [8, 2048, 768], P('dp', 'mp')
- grad_tokens: float32 [8, 2048, 768], P('dp', 'mp')
- grad_gain_first: float32 [768], replicated
- grad_w_in: float32 [768, 3, 768], P(None, None, 'mp')
- grad_kernel: float32 [768, 2048], P('mp')
- grad_w_out: float32 [768, 768], P('mp')
- grad_gain_second: float32 [768], replicated
- grad_w_up: float32 [768, 3072], P(None, 'mp')
- grad_w_down: float32 [3072, 768], P('mp')
All inputs are finite; a program needn't handle non-finite values.
Results may differ from a plain program's by a relative error of at most 0.008.
Values may be sent and summed in bfloat16 or wider, within the bound.
No kernel may reach another device: no remote copies, remote signals or barrier semaphores. Data moves between devices by JAX's collectives and lax.ppermute only.
A program may use at most 640 MiB of HBM per device.

v0:
```python
import math
from functools import partial

import jax
import jax.numpy as jnp
import numpy as np
from jax import lax
from jax.experimental import pallas as pl
from jax.experimental.pallas import tpu as pltpu
from jax.sharding import PartitionSpec as P

LANES = 128
ROWS = 16
BASE = 256
f32 = jnp.float32
bf16 = jnp.bfloat16


def dft_tables(length):
    radix = length // BASE
    spot = lax.iota(jnp.int32, BASE)
    angle = (spot[:, None] * spot[None] % BASE).astype(f32) * (2 * math.pi / BASE)
    cos, sin = jnp.cos(angle), jnp.sin(angle)
    matrix = jnp.concatenate(
        [jnp.concatenate([cos, -sin], axis=1), jnp.concatenate([sin, cos], axis=1)], axis=0
    )
    high = matrix.astype(bf16)
    low = (matrix - high.astype(f32)).astype(bf16)
    turn = 2 * np.pi * np.outer(np.arange(radix) + 0.25, np.arange(BASE)) / length
    twiddle = np.stack([np.cos(turn), np.sin(turn)]).astype(np.float32)
    return high, low, jnp.asarray(twiddle)


def times(re, im, angle):
    c, s = math.cos(angle), math.sin(angle)
    if abs(s) < 1e-12:
        return (re, im) if c > 0 else (-re, -im)
    if abs(c) < 1e-12:
        return (-im, re) if s > 0 else (im, -re)
    if abs(abs(c) - abs(s)) < 1e-12:
        a = abs(c)
        sc, ss = (a if c > 0 else -a), (1.0 if (s > 0) == (c > 0) else -1.0)
        if ss > 0:
            return (re - im) * sc, (re + im) * sc
        return (re + im) * sc, (im - re) * sc
    return re * c - im * s, re * s + im * c


def radix_dft(re, im, sign):
    n = len(re)
    if n == 1:
        return re, im
    er, ei = radix_dft(re[0::2], im[0::2], sign)
    odr, odi = radix_dft(re[1::2], im[1::2], sign)
    lo_r, lo_i, hi_r, hi_i = [], [], [], []
    for k in range(n // 2):
        tr, ti = times(odr[k], odi[k], sign * 2 * math.pi * k / n)
        lo_r.append(er[k] + tr)
        lo_i.append(ei[k] + ti)
        hi_r.append(er[k] - tr)
        hi_i.append(ei[k] - ti)
    return lo_r + hi_r, lo_i + hi_i


def split_in(load, twiddle_ref, store, radix, channels):
    def step(tile, carry):
        rows = pl.ds(pl.multiple_of(tile * ROWS, ROWS), ROWS)
        for half in range(BASE // LANES):
            lanes = slice(half * LANES, (half + 1) * LANES)
            re, im = [], []
            for block in range(radix):
                x = load(rows, block, half)
                angle = -2 * math.pi * block * 0.25 / radix
                re.append(x * math.cos(angle))
                im.append(x * math.sin(angle))
            re, im = radix_dft(re, im, -1)
            for k in range(radix):
                c = twiddle_ref[0, k : k + 1, lanes]
                s = twiddle_ref[1, k : k + 1, lanes]
                store(rows, k, half, re[k] * c + im[k] * s, im[k] * c - re[k] * s)
        return carry

    lax.fori_loop(0, channels // ROWS, step, 0)


def split_out(load, twiddle_ref, store, radix, channels, length):
    def step(tile, carry):
        rows = pl.ds(pl.multiple_of(tile * ROWS, ROWS), ROWS)
        for half in range(BASE // LANES):
            lanes = slice(half * LANES, (half + 1) * LANES)
            re, im = [], []
            for k in range(radix):
                vr, vi = load(rows, k, half)
                c = twiddle_ref[0, k : k + 1, lanes]
                s = twiddle_ref[1, k : k + 1, lanes]
                re.append(vr * c - vi * s)
                im.append(vr * s + vi * c)
            re, im = radix_dft(re, im, 1)
            for block in range(radix):
                angle = 2 * math.pi * block * 0.25 / radix
                store(
                    rows,
                    block,
                    half,
                    re[block] * (math.cos(angle) / length) - im[block] * (math.sin(angle) / length),
                )
        return carry

    lax.fori_loop(0, channels // ROWS, step, 0)


def forward_dot(z, matrix):
    return jnp.dot(z, matrix, preferred_element_type=f32)


def inverse_dot(y, matrix):
    return lax.dot_general(y, matrix, (((1,), (1,)), ((), ())), preferred_element_type=f32)


def product_loop(a_load, b_load, store, total_rows, conj):
    def step(tile, carry):
        rows = pl.ds(pl.multiple_of(tile * ROWS, ROWS), ROWS)
        for half in range(BASE // LANES):
            cr = slice(half * LANES, (half + 1) * LANES)
            ci = slice(BASE + half * LANES, BASE + (half + 1) * LANES)
            ar, ai = a_load(rows, cr), a_load(rows, ci)
            br, bi = b_load(rows, cr), b_load(rows, ci)
            if conj:
                store(rows, cr, ar * br + ai * bi)
                store(rows, ci, ai * br - ar * bi)
            else:
                store(rows, cr, ar * br - ai * bi)
                store(rows, ci, ai * br + ar * bi)
        return carry

    lax.fori_loop(0, total_rows // ROWS, step, 0)


def cut(ref, here, rows, block, half):
    width = ref.shape[-1]
    start = block * BASE + half * LANES
    return ref[(start // width) ^ here, rows, start % width : start % width + LANES].astype(f32)


def put(ref, here, rows, block, half, value):
    width = ref.shape[-1]
    start = block * BASE + half * LANES
    ref[(start // width) ^ here, rows, start % width : start % width + LANES] = value.astype(ref.dtype)


def rowshift(rows, k, channels):
    return pl.ds(pl.multiple_of(rows.start + k * channels, ROWS), ROWS)


def into_scratch(ref, channels):
    def store(rows, k, half, re, im):
        at = rowshift(rows, k, channels)
        ref[at, half * LANES : (half + 1) * LANES] = re.astype(ref.dtype)
        ref[at, BASE + half * LANES : BASE + (half + 1) * LANES] = im.astype(ref.dtype)

    return store


def from_scratch(ref, channels):
    def load(rows, k, half):
        at = rowshift(rows, k, channels)
        return (
            ref[at, half * LANES : (half + 1) * LANES].astype(f32),
            ref[at, BASE + half * LANES : BASE + (half + 1) * LANES].astype(f32),
        )

    return load


def filter_kernel(f_ref, high_ref, low_ref, twiddle_ref, spec_ref, zh, zl, *, radix, channels):
    def store(rows, k, half, re, im):
        at = rowshift(rows, k, channels)
        for value, base in ((re, 0), (im, BASE)):
            lanes = slice(base + half * LANES, base + (half + 1) * LANES)
            top = value.astype(bf16)
            zh[at, lanes] = top
            zl[at, lanes] = (value - top.astype(f32)).astype(bf16)

    split_in(partial(cut, f_ref, 0), twiddle_ref, store, radix, channels)
    spec_ref[...] = (
        forward_dot(zh[...], high_ref[...])
        + forward_dot(zl[...], high_ref[...])
        + forward_dot(zh[...], low_ref[...])
    )


def tile_load(ref):
    return lambda rows, lanes: ref[rows, lanes].astype(f32)


def tile_store(ref):
    def store(rows, lanes, value):
        ref[rows, lanes] = value.astype(ref.dtype)

    return store


def conv_kernel(here_ref, *refs, parts, radix, channels, length):
    sent, (fspec_ref, high_ref, twiddle_ref) = refs[:parts], refs[parts : parts + 3]
    outs, (uspec_ref, z, y, big, turned) = refs[parts + 3 : 2 * parts + 3], refs[2 * parts + 3 :]
    here = here_ref[0]
    for i, ref in enumerate(sent):
        turned[i ^ here] = ref[...]
    split_in(partial(cut, turned, 0), twiddle_ref, into_scratch(z, channels), radix, channels)
    big[...] = forward_dot(z[...], high_ref[...])
    uspec_ref[...] = big[...].astype(uspec_ref.dtype)
    product_loop(tile_load(big), tile_load(fspec_ref), tile_store(y), radix * channels, False)
    big[...] = inverse_dot(y[...], high_ref[...])
    split_out(from_scratch(big, channels), twiddle_ref, partial(put, turned, 0), radix, channels, length)
    for i, ref in enumerate(outs):
        ref[...] = turned[i ^ here]


def conv_mixed_kernel(here_ref, *refs, parts, radix, channels, length):
    sent, (fspec_ref, high_ref, twiddle_ref) = refs[:parts], refs[parts : parts + 3]
    mixed, (spec_ref, z, y, big, turned) = refs[parts + 3 : 2 * parts + 3], refs[2 * parts + 3 :]
    here = here_ref[0]
    for i, ref in enumerate(sent):
        turned[i ^ here] = ref[...]
    split_in(partial(cut, turned, 0), twiddle_ref, into_scratch(z, channels), radix, channels)
    spec_ref[...] = forward_dot(z[...], high_ref[...])
    product_loop(tile_load(spec_ref), tile_load(fspec_ref), tile_store(y), radix * channels, True)
    big[...] = inverse_dot(y[...], high_ref[...])
    split_out(from_scratch(big, channels), twiddle_ref, partial(put, turned, 0), radix, channels, length)
    for i, ref in enumerate(mixed):
        ref[...] = turned[i ^ here]


def conv_filt_kernel(
    gspec_ref, uspec_ref, high_ref, twiddle_ref, filt_ref, y, big, *, radix, channels, length, taps
):
    product_loop(tile_load(gspec_ref), tile_load(uspec_ref), tile_store(y), radix * channels, True)
    big[...] = inverse_dot(y[...], high_ref[...])
    filt_ref[filt_ref.shape[0] - 1] = jnp.zeros(filt_ref.shape[1:], filt_ref.dtype)

    def store(rows, block, half, value):
        if block * BASE + half * LANES < taps:
            put(filt_ref, 0, rows, block, half, value)

    split_out(from_scratch(big, channels), twiddle_ref, store, radix, channels, length)


VM = pl.BlockSpec(memory_space=pltpu.VMEM)
SM = pl.BlockSpec(memory_space=pltpu.SMEM)


def filter_spectrum(filt, tables):
    high, low, twiddle = tables
    channels, length = filt.shape[1], filt.shape[0] * filt.shape[2]
    radix = length // BASE
    rows = radix * channels
    return pl.pallas_call(
        partial(filter_kernel, radix=radix, channels=channels),
        out_shape=jax.ShapeDtypeStruct((rows, 2 * BASE), f32),
        in_specs=[VM] * 4,
        out_specs=VM,
        scratch_shapes=[pltpu.VMEM((rows, 2 * BASE), bf16)] * 2,
        name="filter_spectrum",
    )(filt, high, low, twiddle)


def conv_forward(here, pieces, fspec, tables):
    high, _, twiddle = tables
    parts = len(pieces)
    channels, width = pieces[0].shape
    length = parts * width
    radix = length // BASE
    rows = radix * channels
    return pl.pallas_call(
        partial(conv_kernel, parts=parts, radix=radix, channels=channels, length=length),
        out_shape=[jax.ShapeDtypeStruct((channels, width), bf16)] * parts + [pltpu.HBM((rows, 2 * BASE), bf16)],
        in_specs=[SM] + [VM] * (parts + 3),
        out_specs=[VM] * (parts + 1),
        scratch_shapes=[pltpu.VMEM((rows, 2 * BASE), bf16)] * 2
        + [pltpu.VMEM((rows, 2 * BASE), f32), pltpu.VMEM((parts, channels, width), bf16)],
        compiler_params=pltpu.CompilerParams(vmem_limit_bytes=16 << 20),
        name="conv_forward",
    )(here, *pieces, fspec, high, twiddle)


def conv_mixed(here, pieces, fspec, tables):
    high, _, twiddle = tables
    parts = len(pieces)
    channels, width = pieces[0].shape
    length = parts * width
    radix = length // BASE
    rows = radix * channels
    return pl.pallas_call(
        partial(conv_mixed_kernel, parts=parts, radix=radix, channels=channels, length=length),
        out_shape=[jax.ShapeDtypeStruct((channels, width), bf16)] * parts
        + [jax.ShapeDtypeStruct((rows, 2 * BASE), f32)],
        in_specs=[SM] + [VM] * (parts + 3),
        out_specs=[VM] * (parts + 1),
        scratch_shapes=[pltpu.VMEM((rows, 2 * BASE), bf16)] * 2
        + [pltpu.VMEM((rows, 2 * BASE), f32), pltpu.VMEM((parts, channels, width), bf16)],
        compiler_params=pltpu.CompilerParams(vmem_limit_bytes=16 << 20),
        name="conv_mixed",
    )(here, *pieces, fspec, high, twiddle)


def conv_filt(gspec, uspec, tables, taps, width, length):
    high, _, twiddle = tables
    rows = gspec.shape[0]
    radix = length // BASE
    channels = rows // radix
    return pl.pallas_call(
        partial(conv_filt_kernel, radix=radix, channels=channels, length=length, taps=taps),
        out_shape=jax.ShapeDtypeStruct((-(-taps // width), channels, width), f32),
        in_specs=[VM] * 4,
        out_specs=VM,
        scratch_shapes=[pltpu.VMEM((rows, 2 * BASE), bf16), pltpu.VMEM((rows, 2 * BASE), f32)],
        compiler_params=pltpu.CompilerParams(vmem_limit_bytes=16 << 20),
        name="conv_filt",
    )(gspec, uspec, high, twiddle)


thresh = 0.003
epsilon = 1e-05
gelu_scale = math.sqrt(2 / math.pi)
gelu_cube = 0.044715


def norm(values):
    centered = values - jnp.mean(values, axis=-1, keepdims=True)
    inverse = lax.rsqrt(jnp.mean(centered * centered, axis=-1, keepdims=True) + epsilon)
    return centered * inverse, inverse


def norm_back(unit, inverse, gain, grad):
    scaled = grad * gain
    mean = jnp.mean(scaled, axis=-1, keepdims=True)
    along = jnp.mean(scaled * unit, axis=-1, keepdims=True)
    return inverse * (scaled - mean - unit * along), jnp.sum(grad * unit, axis=0)


def shrink_pool(kernel, pad_len):
    shrunk = jax.nn.relu(kernel - thresh) - jax.nn.relu(-kernel - thresh)
    padded = jnp.pad(shrunk, ((0, 0), (1, 1)))
    pooled = (padded[:, :-2] + padded[:, 1:-1] + padded[:, 2:]) / 3.0
    positions = lax.broadcasted_iota(jnp.int32, pooled.shape, 1)
    return jnp.where(positions < (pooled.shape[1] - pad_len)[:, None], pooled, 0.0)


def gelu_both(values):
    cubic = gelu_cube * values * values
    turn = jnp.tanh(gelu_scale * (values + cubic * values))
    half = 0.5 * (1 + turn)
    slope = half + 0.5 * values * (1 - turn * turn) * (gelu_scale * (1 + 3 * cubic))
    return values * half, slope


def dot(a, b, over_a, over_b):
    return lax.dot_general(a, b, (((over_a,), (over_b,)), ((), ())), preferred_element_type=f32)


def after(x, *waits):
    return lax.optimization_barrier((x, waits))[0] if waits else x


def swap(x, axis, bit, done=()):
    return after(lax.ppermute(x, axis, [(i, i ^ bit) for i in range(lax.axis_size(axis))]), *done)


def gather(x, axis, stride=1, done=()):
    return jnp.stack([x] + [swap(x, axis, i, done) for i in range(stride, lax.axis_size(axis), stride)])


def scatter(x, axis, stride=1, done=()):
    terms = [x[0]] + [swap(x[i], axis, i * stride, done) for i in range(1, x.shape[0])]
    return sum(term.astype(f32) for term in terms)


class Gather:
    def __init__(self, x, bits):
        self.x, self.held, self.left = x, [], list(bits)

    def step(self, count=1, done=()):
        for bit in self.left[:count]:
            place = sum(other > bit for other in self.held)
            self.x = jnp.stack([self.x, swap(self.x, "dp", 1 << bit, done)], axis=place)
            self.held.append(bit)
        self.left = self.left[count:]
        return self

    def finish(self, done=()):
        self.step(len(self.left), done)
        return self.x.reshape((-1,) + self.x.shape[len(self.held) :])


def narrow_sum(*terms):
    return sum(term.astype(f32) for term in terms).astype(bf16)


class Reduction:
    def __init__(self, x, bits):
        self.x = x.reshape((2,) * len(bits) + x.shape[1:])
        self.held, self.left = sorted(bits, reverse=True), list(bits)

    def step(self, count=1, done=()):
        for bit in self.left[:count]:
            place = self.held.index(bit)
            self.held.remove(bit)
            keep, send = (lax.index_in_dim(self.x, side, place, keepdims=False) for side in (0, 1))
            self.x = narrow_sum(keep, swap(send, "dp", 1 << bit, done))
        self.left = self.left[count:]
        return self

    def finish(self, done=()):
        return self.step(len(self.left), done).x


def sum_all(x):
    for axis in ("dp", "mp"):
        bit = 1
        while bit < lax.axis_size(axis):
            x = x + swap(x, axis, bit)
            bit *= 2
    return x


def parts_of(x, axis, stride=1):
    return [x] + [swap(x, axis, i) for i in range(stride, lax.axis_size(axis), stride)]


def parts_for(x, axis):
    return [x[0]] + [swap(x[i], axis, i) for i in range(1, x.shape[0])]


def turn(x):
    return lax.all_to_all(x, "mp", 0, 0)


def exchange(x, done=()):
    return jnp.stack([x[0]] + [swap(x[i], "mp", i, done) for i in range(1, x.shape[0])])


def spread(x, *orders):
    x = x.astype(bf16)
    if orders:
        half = x.shape[0] // 16 * 8
        x = [Gather(part, bits).finish() for part, bits in zip((x[:half], x[half:]), orders)]
        x = jnp.concatenate(x, axis=1)
    else:
        x = gather(x, "dp", 2)
    return jnp.concatenate([x, swap(x, "dp", 1)])


class Spread:
    def __init__(self, x, *orders):
        half = x.shape[0] // 16 * 8
        self.parts = [Gather(part, bits) for part, bits in zip((x[:half], x[half:]), orders)]

    @property
    def x(self):
        return [part.x for part in self.parts]

    def step(self, done=()):
        for part in self.parts:
            part.step(done=done)

    def finish(self, done=()):
        x = jnp.concatenate([part.finish(done=done) for part in self.parts], axis=1)
        return jnp.concatenate([x, swap(x, "dp", 1)])


class Doubling:
    def __init__(self, x):
        self.x = x
        self.left = [
            (axis, 1 << bit) for axis in ("dp", "mp") for bit in range(lax.axis_size(axis).bit_length() - 1)
        ]

    def step(self):
        if self.left:
            self.x = self.x + swap(self.x, *self.left.pop(0))

    def finish(self):
        while self.left:
            self.step()


def absolute(x, start, rows):
    here = lax.axis_index("dp")
    count = x.shape[0]
    picks = []
    for index in range(count):
        relative = here ^ index
        at = (relative & 1) * (count // 2) + (relative >> 1)
        picks.append(lax.dynamic_slice(x, (at, start, 0), (1, rows, x.shape[2]))[0])
    return jnp.concatenate(picks).astype(f32)


def plain_body(
    tables,
    tokens,
    gain_first,
    input_weight,
    kernel,
    pad_len,
    output_weight,
    gain_second,
    up_weight,
    down_weight,
    cotangent,
):
    ways, rows_mp = lax.axis_size("dp"), lax.axis_size("mp")
    here_dp, here_mp = lax.axis_index("dp"), lax.axis_index("mp")
    chips = list(range(1, ways.bit_length() - 1))
    first_bits, second_bits = chips, chips[::-1]
    here = here_mp.astype(jnp.int32)[None]
    spots, width = tokens.shape[1:]
    length = spots * rows_mp
    own_channels = kernel.shape[0]
    slice_channels = own_channels // ways
    slice_hidden = up_weight.shape[1] // ways
    channels = own_channels * rows_mp

    own_in = lax.dynamic_slice_in_dim(input_weight, here_dp * slice_channels, slice_channels, 2)
    own_out = lax.dynamic_slice_in_dim(output_weight, here_dp * slice_channels, slice_channels, 0)
    mixer_rows = gather(jnp.concatenate([own_in.transpose(1, 2, 0), own_out[None]]), "mp")
    start_rows = tokens[0].astype(f32)
    unit_one, inverse_one = norm(start_rows)
    normed_low = (unit_one * gain_first).astype(bf16)
    own_up = lax.dynamic_slice_in_dim(up_weight, here_dp * slice_hidden, slice_hidden, 1).T
    own_down = lax.dynamic_slice_in_dim(down_weight, here_dp * slice_hidden, slice_hidden, 0)
    own_feed = jnp.stack([own_up, own_down])

    picks = []
    for core in range(2):
        for chip in range(ways // 2):
            at = (here_dp ^ (2 * chip + core)) * slice_channels
            picks.append(at)
    kernel_rel = jnp.concatenate([lax.dynamic_slice_in_dim(kernel, at, slice_channels, 0) for at in picks])
    pad_rel = jnp.concatenate([lax.dynamic_slice_in_dim(pad_len, at, slice_channels, 0) for at in picks])
    filt = shrink_pool(kernel_rel, pad_rel)
    fspec = filter_spectrum(jnp.pad(filt, ((0, 0), (0, length - filt.shape[1])))[None], tables)

    feed_rows = gather(after(own_feed, mixer_rows), "mp")
    mixer_rows = gather(after(mixer_rows, fspec, normed_low, own_feed), "dp", 2)
    feeds = [
        Gather(after(feed_rows[:, side], mixer_rows), bits).step()
        for side, bits in ((0, first_bits), (1, second_bits))
    ]
    mixer_rows = jnp.stack([mixer_rows, swap(mixer_rows, "dp", 1)])
    mixer_weights = mixer_rows.transpose(3, 2, 0, 1, 4, 5)
    weight_in = mixer_weights[:3].reshape(3 * channels, width)
    weight_out = mixer_weights[3].reshape(channels, width)

    proj = dot(weight_in, normed_low, 1, 1).reshape(3, channels, spots)
    value, gate_one, gate_two = proj[0], proj[1], proj[2]
    mixed_in = (value * gate_one).astype(bf16).reshape(rows_mp, own_channels, spots)
    for feed in feeds:
        feed.x = after(feed.x, mixed_in)
        feed.finish()
    *conv_out, uspec = conv_forward(here, list(exchange(mixed_in)), fspec, tables)
    conv_out = jnp.stack(conv_out)
    feeds = [after(feed.x, conv_out).reshape(-1, width) for feed in feeds]
    conv = exchange(conv_out).reshape(channels, spots).astype(f32)
    mixer_low = (gate_two * conv).astype(bf16)
    residual_one = start_rows + dot(mixer_low, weight_out, 0, 0)

    unit_two, inverse_two = norm(residual_one)
    second_low = (unit_two * gain_second).astype(bf16)
    grad_rows = cotangent[0]
    feeds = [[feed, swap(feed, "dp", 1)] for feed in feeds]
    block_out, grad_norm_two = residual_one, 0.0
    up_grads, down_grads = [], []
    for up, down in zip(*feeds):
        act, slope = gelu_both(dot(second_low, up, 1, 1))
        act_low = act.astype(bf16)
        grad_pre = (dot(grad_rows, down, 1, 1) * slope).astype(bf16)
        block_out = block_out + dot(act_low, down, 1, 0)
        grad_norm_two = grad_norm_two + dot(grad_pre, up, 1, 0)
        up_grads.append(dot(grad_pre, second_low, 0, 0).astype(bf16))
        down_grads.append(dot(act_low, grad_rows, 0, 0).astype(bf16))
    grad_mid_norm, gain_second_grad = norm_back(unit_two, inverse_two, gain_second, grad_norm_two)
    grad_mid = grad_rows.astype(f32) + grad_mid_norm
    mid_low = grad_mid.astype(bf16)

    chips_count = ways // 2

    def hidden_sum(parts, bits):
        kept = narrow_sum(parts[0], swap(parts[1], "dp", 1))
        return Reduction(kept.reshape(chips_count, rows_mp, slice_hidden, width), bits)

    down_sum = hidden_sum(down_grads, second_bits)
    up_sum = hidden_sum(up_grads, first_bits)

    def by_slice(parts):
        parts = [part.astype(bf16).reshape(rows_mp, 2, chips_count, slice_channels, width) for part in parts]
        return jnp.concatenate(parts, axis=3).transpose(1, 2, 0, 3, 4)

    grad_mixer = dot(weight_out, mid_low, 1, 1)
    grad_conv = (grad_mixer * gate_two).astype(bf16).reshape(rows_mp, own_channels, spots)
    grad_conv = exchange(grad_conv)
    grad_gate_two = (grad_mixer * conv).astype(bf16)
    out_grad = dot(mixer_low, mid_low, 1, 0)
    late = by_slice([dot(grad_gate_two, normed_low, 1, 0), out_grad])
    late = narrow_sum(late[0], swap(late[1], "dp", 1))
    grad_conv = after(grad_conv, down_sum.x, up_sum.x, late)
    *mixed_out, gspec = conv_mixed(here, list(grad_conv), fspec, tables)
    filt_grad = conv_filt(gspec, uspec, tables, length, length, length)
    mixed_out = jnp.stack(mixed_out)
    down_sum.step()
    up_sum.step()
    late = scatter(late, "dp", 2).astype(bf16)
    grad_mixed = exchange(mixed_out).reshape(channels, spots).astype(f32)
    grad_mixed = after(grad_mixed, down_sum.x, up_sum.x, late)
    grad_value = (grad_mixed * gate_one).astype(bf16)
    grad_gate_one = (grad_mixed * value).astype(bf16)
    rest = by_slice([dot(grad, normed_low, 1, 0) for grad in (grad_value, grad_gate_one)])
    grad_norm_one = dot(jnp.concatenate([grad_value, grad_gate_one, grad_gate_two]), weight_in, 0, 0)
    grad_start, gain_first_grad = norm_back(unit_one, inverse_one, gain_first, grad_norm_one)
    grad_tokens = grad_mid + grad_start

    taps = kernel.shape[1]
    filt_grad = filt_grad[0, :, :taps].astype(bf16).reshape(2, chips_count, -1, width)
    rest = jnp.concatenate([rest.reshape(2, chips_count, -1, width), filt_grad], axis=2)
    rest = scatter(narrow_sum(rest[0], swap(rest[1], "dp", 1)), "dp", 2)
    split = rest.shape[0] - filt_grad.shape[2]
    own_kernel = lax.dynamic_slice_in_dim(kernel, here_dp * slice_channels, slice_channels, 0)
    own_pad = lax.dynamic_slice_in_dim(pad_len, here_dp * slice_channels, slice_channels, 0)
    _, filter_back = jax.vjp(partial(shrink_pool, pad_len=own_pad), own_kernel)
    (own_filt,) = filter_back(rest[split:].reshape(slice_channels, taps))
    rest = scatter(rest[:split].astype(bf16).reshape(rows_mp, 2 * slice_channels, width), "mp")
    rest = spread(jnp.concatenate([rest, own_filt.reshape(-1, width)]))
    bulk = jnp.concatenate([up_sum.finish(), down_sum.finish(), late], axis=1)
    bulk = spread(scatter(bulk, "mp"))

    up_grad = absolute(bulk, 0, slice_hidden).T
    down_grad = absolute(bulk, slice_hidden, slice_hidden)
    in_grad = [
        absolute(rest, 0, slice_channels),
        absolute(rest, slice_channels, slice_channels),
        absolute(bulk, 2 * slice_hidden, slice_channels),
    ]
    in_full = jnp.stack(in_grad).transpose(2, 0, 1)
    out_full = absolute(bulk, 2 * slice_hidden + slice_channels, slice_channels)
    kernel_grad = absolute(rest, 2 * slice_channels, filt_grad.shape[2]).reshape(own_channels, taps)

    gains = sum_all(jnp.stack([gain_first_grad, gain_second_grad]))
    return (
        block_out.astype(bf16)[None],
        grad_tokens[None],
        gains[0],
        in_full,
        kernel_grad,
        out_full,
        gains[1],
        up_grad,
        down_grad,
    )


def whole_call(kernel, outs, scratch=(), name=None, smem=0, count=0, room=6):
    return pl.pallas_call(
        kernel,
        out_shape=tuple(out if isinstance(out, pl.MemoryRef) else jax.ShapeDtypeStruct(*out) for out in outs),
        in_specs=[SM] * smem + [VM] * count,
        out_specs=tuple(VM for _ in outs),
        scratch_shapes=[pltpu.VMEM(shape, dtype) for shape, dtype in scratch],
        compiler_params=pltpu.CompilerParams(vmem_limit_bytes=room << 20),
        name=name,
    )


def relative_index(here, place, count):
    chip, core = place % (count // 2), place // (count // 2)
    return here ^ (2 * chip + core)


def filter_slices_kernel(
    here_ref, kernel_ref, pad_ref, high_ref, low_ref, twiddle_ref, spec_ref, filt, zh, zl, *, radix, channels, ways
):
    here = here_ref[0]
    rows = channels // ways
    taps = kernel_ref.shape[1]
    filt[...] = jnp.zeros_like(filt)
    spot = lax.broadcasted_iota(jnp.int32, (8, taps), 1)
    for place in range(ways):
        start = relative_index(here, place, ways) * rows
        for tile in range(rows // 8):
            at = pl.ds(pl.multiple_of(start + tile * 8, 8), 8)
            raw = kernel_ref[at, :]
            shrunk = jnp.maximum(raw - thresh, 0.0) - jnp.maximum(-raw - thresh, 0.0)
            before = jnp.where(spot == 0, 0.0, pltpu.roll(shrunk, 1, 1))
            behind = jnp.where(spot == taps - 1, 0.0, pltpu.roll(shrunk, taps - 1, 1))
            pooled = (before + shrunk + behind) / 3.0
            kept = jnp.where(spot < taps - pad_ref[at, :], pooled, 0.0)
            put_rows = place * rows + tile * 8
            filt[0, put_rows : put_rows + 8, :taps] = kept
    filter_kernel(filt, high_ref, low_ref, twiddle_ref, spec_ref, zh, zl, radix=radix, channels=channels)


def filter_slices(here, kernel, pad_len, tables, length, ways):
    high, low, twiddle = tables
    channels = kernel.shape[0]
    radix = length // BASE
    rows = radix * channels
    return whole_call(
        partial(filter_slices_kernel, radix=radix, channels=channels, ways=ways),
        [((rows, 2 * BASE), f32)],
        [((1, channels, length), f32), ((rows, 2 * BASE), bf16), ((rows, 2 * BASE), bf16)],
        name="filter_spectrum",
        smem=1,
        count=5,
        room=14,
    )(here, kernel, pad_len[:, None], high, low, twiddle)[0]


def nt(a, b):
    return dot(a, b, 1, 1)


def tn(a, b):
    return dot(a, b, 0, 0)


def project_kernel(level_ref, x_ref, gain_ref, *refs, rows, mesh_rows):
    pieces, sends = refs[:8], refs[8 : 8 + mesh_rows]
    v_ref, one_ref, two_ref, out_ref, low_ref, weights, low, proj, sems = refs[8 + mesh_rows :]
    step = pl.program_id(0)
    copies = [pltpu.make_async_copy(piece, weights.at[k], sems.at[k]) for k, piece in enumerate(pieces)]

    @pl.when(step == 0)
    def _():
        for copy in copies:
            copy.start()
        unit, _ = norm(x_ref[...].astype(f32))
        low[...] = (unit * gain_ref[...]).astype(bf16)
        low_ref[...] = low[...]

    for core in range(2):
        slot = core * 4 + step
        pltpu.make_async_copy(pieces[0], weights.at[slot], sems.at[slot]).wait()
        proj[...] = nt(weights[slot], low[...])
        for i, send_ref in enumerate(sends):
            to = i ^ level_ref[0]
            at = pl.multiple_of(to * (4 * rows), 8)
            value, one, two = (proj[pl.ds(at + k * rows, rows), :] for k in range(3))
            send_ref[core, 0] = (value * one).astype(bf16)
            v_ref[to, core, 0] = value
            one_ref[to, core, 0] = one
            two_ref[to, core, 0] = two
            at = (4 * i + 3) * rows
            out_ref[i, core, 0] = weights[slot, at : at + rows, :]


def project(level, x, gain, pieces, mesh_rows):
    spots, width = x.shape
    size = pieces[0].shape[0]
    rows = size // (4 * mesh_rows)
    block = lambda last: pl.BlockSpec((mesh_rows, 2, 1, rows, last), lambda j: (0, 0, j, 0, 0))
    shape = lambda last, dtype: pltpu.HBM((mesh_rows, 2, 4, rows, last), dtype)
    full = pl.BlockSpec((spots, width), lambda j: (0, 0))
    return pl.pallas_call(
        partial(project_kernel, rows=rows, mesh_rows=mesh_rows),
        grid=(4,),
        in_specs=[SM, full, pl.BlockSpec((1, width), lambda j: (0, 0))] + [pl.BlockSpec(memory_space=pl.ANY)] * 8,
        out_specs=[pl.BlockSpec((2, 1, rows, spots), lambda j: (0, j, 0, 0))] * mesh_rows
        + [block(spots)] * 3
        + [block(width), full],
        out_shape=[pltpu.HBM((2, 4, rows, spots), bf16)] * mesh_rows
        + [
            shape(spots, f32),
            shape(spots, f32),
            shape(spots, f32),
            shape(width, bf16),
            pltpu.HBM((spots, width), bf16),
        ],
        scratch_shapes=[
            pltpu.VMEM((8, size, width), bf16),
            pltpu.VMEM((spots, width), bf16),
            pltpu.VMEM((size, spots), f32),
            pltpu.SemaphoreType.DMA((8,)),
        ],
        compiler_params=pltpu.CompilerParams(vmem_limit_bytes=18 << 20),
        name="project",
    )(level, x, gain[None], *pieces)


def stack_kernel(*refs):
    for index, out_ref in enumerate(refs[len(refs) // 3 * 2 :]):
        out_ref[0] = refs[2 * index][...]
        out_ref[1] = refs[2 * index + 1][...]


def feed_kernel(*refs, mesh_rows):
    here_ref, x_ref, two_ref, out_weight_ref, gain_ref, grad_ref = refs[:6]
    sent, refs = refs[6 : 6 + mesh_rows], refs[6 + mesh_rows :]
    ups, downs, up_firsts, down_firsts = refs[:2], refs[2:4], refs[4:8], refs[8:12]
    mixer_ref, block_ref, mid_ref, mid_low_ref, gain_grad_ref, grad_two_ref = refs[12:18]
    sends, refs = refs[18 : 18 + mesh_rows], refs[18 + mesh_rows :]
    up_near, up_far, down_near, down_far = refs[:4]
    residual, second, out_acc, norm_acc, conv, turned, weights, grads, sems, grad_sems = refs[4:]
    step = pl.program_id(0)
    size = weights.shape[2]
    copies = []
    for side, (firsts, pairs) in enumerate(((up_firsts, ups), (down_firsts, downs))):
        for k in range(8):
            core, chip = divmod(k, 4)
            first = (0, 1) if side == 0 else (0, 2)
            if chip in first:
                source = firsts[2 * core + first.index(chip)]
            else:
                source = pairs[core].at[0 if chip == (2 if side == 0 else 1) else 1]
            copies.append(pltpu.make_async_copy(source, weights.at[side, k], sems.at[side, k]))

    @pl.when(step == 0)
    def _():
        for copy in copies:
            copy.start()
        for i, ref in enumerate(sent):
            conv[i ^ here_ref[0]] = ref[...]
        mixer_ref[...] = (two_ref[...] * conv[...].reshape(two_ref.shape).astype(f32)).astype(bf16)
        residual[...] = x_ref[...].astype(f32) + tn(mixer_ref[...], out_weight_ref[...])
        unit, _ = norm(residual[...])
        second[...] = (unit * gain_ref[...]).astype(bf16)
        out_acc[...] = residual[...]
        norm_acc[...] = jnp.zeros_like(norm_acc)

    for side in range(2):
        pltpu.make_async_copy(up_firsts[0], weights.at[side, step], sems.at[side, step]).wait()
    slot = step % 2

    @pl.when(step >= 2)
    def _():
        for side in range(2):
            pltpu.make_async_copy(
                grads.at[side, slot], up_near.at[pl.ds(0, size), :], grad_sems.at[side, slot]
            ).wait()

    up, down = weights[0, step], weights[1, step]
    act, slope = gelu_both(nt(second[...], up))
    act_low = act.astype(bf16)
    grad_pre = (nt(grad_ref[...], down) * slope).astype(bf16)
    out_acc[...] += dot(act_low, down, 1, 0)
    norm_acc[...] += dot(grad_pre, up, 1, 0)
    grads[0, slot] = tn(grad_pre, second[...]).astype(bf16)
    grads[1, slot] = tn(act_low, grad_ref[...]).astype(bf16)
    at = pl.ds(pl.multiple_of((step % 4) * size, size), size)
    for core, outs in enumerate(((up_near, down_near), (up_far, down_far))):

        @pl.when(step // 4 == core)
        def _():
            for side in range(2):
                pltpu.make_async_copy(
                    grads.at[side, slot], outs[side].at[at, :], grad_sems.at[side, slot]
                ).start()

    @pl.when(step == pl.num_programs(0) - 1)
    def _():
        unit, inverse = norm(residual[...])
        grad, gain_grad = norm_back(unit, inverse, gain_ref[...], norm_acc[...])
        gain_grad_ref[...] = gain_grad[None]
        mid = grad_ref[...].astype(f32) + grad
        mid_ref[...] = mid
        mid_low_ref[...] = mid.astype(bf16)
        block_ref[...] = out_acc[...].astype(bf16)
        grad_mixer = nt(out_weight_ref[...], mid_low_ref[...])
        flat = conv[...].reshape(two_ref.shape)
        grad_two_ref[...] = (grad_mixer * flat.astype(f32)).astype(bf16)
        turned[...] = (grad_mixer * two_ref[...]).astype(bf16).reshape(turned.shape)
        for i, ref in enumerate(sends):
            ref[...] = turned[i ^ here_ref[0]]
        for side in range(2):
            for last in range(2):
                pltpu.make_async_copy(
                    grads.at[side, last], up_near.at[pl.ds(0, size), :], grad_sems.at[side, last]
                ).wait()


def feed_forward(here, wholes, conv, ups, downs, channels):
    mesh_rows = len(conv)
    size, width = ups[2].shape
    spots = wholes[0].shape[0]
    shape = jax.ShapeDtypeStruct
    tall = shape((channels, spots), bf16)
    piece = shape((channels // mesh_rows, spots), bf16)
    anywhere = pl.BlockSpec(memory_space=pl.ANY)
    return pl.pallas_call(
        partial(feed_kernel, mesh_rows=mesh_rows),
        grid=(8,),
        in_specs=[SM] + [VM] * (len(wholes) + mesh_rows) + [anywhere] * 12,
        out_specs=[VM] * (6 + mesh_rows) + [anywhere] * 4,
        out_shape=[
            tall,
            pltpu.HBM((spots, width), bf16),
            pltpu.HBM((spots, width), f32),
            shape((spots, width), bf16),
            shape((1, width), f32),
            pltpu.HBM((channels, spots), bf16),
        ]
        + [piece] * mesh_rows
        + [shape((4 * size, width), bf16)] * 4,
        scratch_shapes=[
            pltpu.VMEM((spots, width), f32),
            pltpu.VMEM((spots, width), bf16),
            pltpu.VMEM((spots, width), f32),
            pltpu.VMEM((spots, width), f32),
            pltpu.VMEM((mesh_rows, channels // mesh_rows, spots), bf16),
            pltpu.VMEM((mesh_rows, channels // mesh_rows, spots), bf16),
            pltpu.VMEM((2, 8, size, width), bf16),
            pltpu.VMEM((2, 2, size, width), bf16),
            pltpu.SemaphoreType.DMA((2, 8)),
            pltpu.SemaphoreType.DMA((2, 2)),
        ],
        compiler_params=pltpu.CompilerParams(vmem_limit_bytes=42 << 20),
        name="feed_forward",
    )(here, *wholes, *conv, *ups[:2], *downs[:2], *ups[2:], *downs[2:])


def put_slices(out_refs, rows_at, product, mesh_rows, rows):
    for i in range(mesh_rows):
        for core in range(2):
            for chip in range(4):
                start = ((i * 2 + core) * 4 + chip) * rows
                at = rows_at(i)
                out_refs[core][chip, at : at + rows, :] = product[start : start + rows, :].astype(bf16)


def late_kernel(grad_two_ref, low_ref, mixer_ref, mid_low_ref, near_ref, far_ref, product, *, mesh_rows, rows):
    for kind, pair in enumerate(((mixer_ref, mid_low_ref), (grad_two_ref, low_ref))):
        product[...] = dot(pair[0][...], pair[1][...], 1, 0)
        put_slices((near_ref, far_ref), lambda i: (2 * i + kind) * rows, product, mesh_rows, rows)


def rest_kernel(*refs, mesh_rows, rows):
    here_ref, sent = refs[0], refs[1 : 1 + mesh_rows]
    value_ref, one_ref, low_ref, filt_ref, near_ref, far_ref, grad_value_ref, grad_one_ref, product = refs[1 + mesh_rows :]
    size = sent[0].shape[0]
    for i, ref in enumerate(sent):
        at = pl.ds(pl.multiple_of((i ^ here_ref[0]) * size, size), size)
        mixed = ref[...].astype(f32)
        grad_value_ref[at, :] = (mixed * one_ref[at, :]).astype(bf16)
        grad_one_ref[at, :] = (mixed * value_ref[at, :]).astype(bf16)
    for kind, grad_ref in enumerate((grad_value_ref, grad_one_ref)):
        product[...] = dot(grad_ref[...], low_ref[...], 1, 0)
        put_slices((near_ref, far_ref), lambda i: (2 * i + kind) * rows, product, mesh_rows, rows)
    base = 2 * mesh_rows * rows
    for part in range(filt_ref.shape[0]):
        for core, ref in enumerate((near_ref, far_ref)):
            for chip in range(4):
                start = (core * 4 + chip) * rows
                at = base + part * rows
                ref[chip, at : at + rows, :] = filt_ref[part, start : start + rows, :].astype(bf16)


def first_norm_kernel(*refs, mesh_rows, rows):
    grads, pieces = refs[:3], refs[3:11]
    x_ref, gain_ref, mid_ref, tokens_ref, gain_grad_ref, gathered, acc = refs[11:]
    for slot, ref in enumerate(pieces):
        for i in range(mesh_rows):
            start = (i * 8 + slot) * rows
            for k, grad_ref in enumerate(grads):
                at = (i * 4 + k) * rows
                gathered[at : at + rows, :] = grad_ref[start : start + rows, :]
            at = (i * 4 + 3) * rows
            gathered[at : at + rows, :] = jnp.zeros((rows, gathered.shape[1]), bf16)
        term = tn(gathered[...], ref[...])
        acc[...] = term if slot == 0 else acc[...] + term
    unit, inverse = norm(x_ref[...].astype(f32))
    grad, gain_grad = norm_back(unit, inverse, gain_ref[...], acc[...])
    tokens_ref[...] = mid_ref[...] + grad
    gain_grad_ref[...] = gain_grad[None]


def add_low(*terms):
    return sum(term.astype(f32) for term in terms).astype(bf16)


def kept_kernel(
    up_ref, up_in, down_ref, down_in, late_ref, late_in, up_keep, up_send, down_keep, down_send, *, mesh_rows, hidden, rows
):
    for chip in range(4):
        for i in range(mesh_rows):
            at = slice((chip * mesh_rows + i) * hidden, (chip * mesh_rows + i + 1) * hidden)
            late = [slice((2 * i + kind) * rows, (2 * i + kind + 1) * rows) for kind in range(2)]
            out_ref, side = (up_send if chip & 1 else up_keep), chip >> 1
            out_ref[side, i, :hidden] = add_low(up_ref[at, :], up_in[at, :])
            out_ref[side, i, hidden:] = add_low(late_ref[chip, late[0], :], late_in[chip, late[0], :])
            out_ref, side = (down_send if chip >> 1 else down_keep), chip & 1
            out_ref[side, i, :hidden] = add_low(down_ref[at, :], down_in[at, :])
            out_ref[side, i, hidden:] = add_low(late_ref[chip, late[1], :], late_in[chip, late[1], :])


def pair_kernel(up_ref, up_in, down_ref, down_in, up_keep, up_send, down_keep, down_send):
    up_keep[...] = add_low(up_ref[0], up_in[0])
    up_send[...] = add_low(up_ref[1], up_in[1])
    down_keep[...] = add_low(down_ref[0], down_in[0])
    down_send[...] = add_low(down_ref[1], down_in[1])


def bulk_kernel(up_ref, up_in, down_ref, down_in, bulk_ref):
    mesh_rows, size = up_ref.shape[:2]
    for i in range(mesh_rows):
        bulk_ref[i, :size] = add_low(up_ref[i], up_in[i])
        bulk_ref[i, size:] = add_low(down_ref[i], down_in[i])


def split_kernel(near_ref, far_ref, *outs):
    for chip, out_ref in enumerate(outs):
        out_ref[...] = add_low(near_ref[chip], far_ref[chip])


def split_gain(gain):
    high = gain.astype(bf16)
    return high, (gain - high.astype(f32)).astype(bf16)


def rest_sum_kernel(
    here_ref, level_ref, p0, p1, p2, p3, kernel_ref, pad_ref, gain_one_ref, gain_two_ref, filt_ref, *sends, rows
):
    mesh_rows = len(sends)
    size, width = sends[0].shape
    size = size - 8
    pairs = [split_gain(ref[...]) for ref in (gain_one_ref, gain_two_ref)]
    gains = jnp.concatenate([pair[part].astype(f32) for part in range(2) for pair in pairs], axis=0)
    gains = jnp.concatenate([gains, jnp.zeros_like(gains)], axis=0).astype(bf16)
    for i, ref in enumerate(sends):
        at = pl.ds(pl.multiple_of((i ^ level_ref[0]) * size, 16), size)
        ref[:size] = add_low(*(part[at, :] for part in (p0, p1, p2, p3)))
        ref[size:] = gains
    taps = kernel_ref.shape[1]
    base = mesh_rows * size
    parts = filt_ref.shape[0] // rows
    grad = [
        sum(ref[base + part * rows : base + (part + 1) * rows, :].astype(f32) for ref in (p0, p1, p2, p3))
        for part in range(parts)
    ]
    grad = jnp.concatenate(grad, axis=1)[:, :taps]
    at = pl.ds(pl.multiple_of(here_ref[0] * rows, rows), rows)
    spot = lax.broadcasted_iota(jnp.int32, (rows, taps), 1)
    grad = jnp.where(spot < taps - pad_ref[at, :], grad, 0.0)
    before = jnp.where(spot == 0, 0.0, pltpu.roll(grad, 1, 1))
    behind = jnp.where(spot == taps - 1, 0.0, pltpu.roll(grad, taps - 1, 1))
    grad = jnp.where(jnp.abs(kernel_ref[at, :]) > thresh, (before + grad + behind) / 3.0, 0.0)
    for part in range(parts):
        size = min(width, taps - part * width)
        piece = grad[:, part * width : part * width + size].astype(bf16)
        filt_ref[part * rows : (part + 1) * rows, :size] = piece
        if size < width:
            filt_ref[part * rows : (part + 1) * rows, size:] = jnp.zeros((rows, width - size), bf16)


def mesh_sum_kernel(x_ref, out_ref):
    out_ref[...] = add_low(*(x_ref[i] for i in range(x_ref.shape[0])))


def tree_sum(terms):
    while len(terms) > 1:
        terms = [a + b for a, b in zip(terms[0::2], terms[1::2])]
    return terms[0]


def rest_mesh_sum_kernel(filt_ref, *refs):
    sent, out_ref = refs[:-1], refs[-1]
    size = sent[0].shape[0] - 8
    filt = filt_ref.shape[0]
    out_ref[:size] = add_low(*(ref[:size] for ref in sent))
    out_ref[size : size + filt] = filt_ref[...]
    gains = [ref[size:].astype(f32) for ref in sent]
    gains = tree_sum([gain[:2] + gain[2:4] for gain in gains])
    high, low = split_gain(gains)
    zeros = jnp.zeros((4, gains.shape[1]), f32)
    out_ref[size + filt :] = jnp.concatenate([high.astype(f32), low.astype(f32), zeros], axis=0).astype(bf16)


def slice_at(here, slot, rows):
    start = (here ^ (2 * (slot % 4) + slot // 4)) * rows
    return pl.ds(pl.multiple_of(start, 8), rows)


def unpack_bulk_kernel(here_ref, *refs, hidden, rows):
    pieces, (up_ref, down_ref, two_ref, out_ref, turned) = refs[:8], refs[8:]
    here = here_ref[0]
    size = hidden + rows
    for slot, ref in enumerate(pieces):
        at = slice_at(here, slot, hidden)
        turned[at, :] = ref[:hidden].astype(f32)
        down_ref[at, :] = ref[size : size + hidden].astype(f32)
        at = slice_at(here, slot, rows)
        out_ref[at, :] = ref[hidden:size].astype(f32)
        two_ref[at, :] = ref[size + hidden :].astype(f32)
    up_ref[...] = turned[...].T


def unpack_rest_kernel(here_ref, *refs, rows):
    pieces, (two_ref, in_ref, kernel_ref, gains_ref, gains) = refs[:8], refs[8:]
    width = in_ref.shape[2]
    taps = kernel_ref.shape[1]
    in_ref[2] = two_ref[...]
    for slot, ref in enumerate(pieces):
        at = slice_at(here_ref[0], slot, rows)
        in_ref[0, at, :] = ref[:rows].astype(f32)
        in_ref[1, at, :] = ref[rows : 2 * rows].astype(f32)
        parts = -(-taps // width)
        for part in range(parts):
            size = min(width, taps - part * width)
            block = ref[(2 + part) * rows : (3 + part) * rows].astype(f32)
            kernel_ref[at, part * width : part * width + size] = block[:, :size]
        gain = ref[(2 + parts) * rows :].astype(f32)
        gains[relative_index(here_ref[0], slot, 8)] = gain[:2] + gain[2:4]
    gains_ref[...] = sum(gains[slot] for slot in range(8))


def chips_of(x, done=()):
    return [x] + [swap(x, "dp", 2 * chip, done) for chip in range(1, 4)]


def far(x):
    return pltpu.with_memory_space_constraint(x, pltpu.HBM)


def levels_of(pieces):
    return [pieces[0]] + [swap(pieces[i], "mp", i) for i in range(1, len(pieces))]


def pair_of(pieces, done=()):
    return pieces + [swap(piece, "dp", 1, done) for piece in pieces]


def fast_body(
    tables,
    tokens,
    gain_first,
    input_weight,
    kernel,
    pad_len,
    output_weight,
    gain_second,
    up_weight,
    down_weight,
    cotangent,
):
    ways, mesh_rows = lax.axis_size("dp"), lax.axis_size("mp")
    here = lax.axis_index("dp")
    place = here.astype(jnp.int32)[None]
    level = lax.axis_index("mp").astype(jnp.int32)[None]
    x, grad_rows = tokens[0], cotangent[0]
    spots, width = x.shape
    length = spots * mesh_rows
    own_channels, taps = kernel.shape
    rows = own_channels // ways
    hidden = up_weight.shape[1] // ways
    channels = own_channels * mesh_rows
    sizes = dict(mesh_rows=mesh_rows, rows=rows)
    filt_parts = -(-taps // width)

    own_in = lax.dynamic_slice_in_dim(input_weight.transpose(1, 2, 0), here * rows, rows, 1)
    own_out = lax.dynamic_slice_in_dim(output_weight, here * rows, rows, 0)
    own_mixer = jnp.concatenate([own_in, own_out[None]])
    mixer_rows = turn(jnp.broadcast_to(own_mixer, (mesh_rows,) + own_mixer.shape))
    own_up = lax.dynamic_slice_in_dim(up_weight, here * hidden, hidden, 1).T
    own_down = lax.dynamic_slice_in_dim(down_weight, here * hidden, hidden, 0)
    own_feed = jnp.stack([own_up, own_down])
    own_feed = jnp.broadcast_to(own_feed, (mesh_rows,) + own_feed.shape)
    fspec = filter_slices(place, kernel, pad_len, tables, length, ways)
    feed_rows = turn(after(own_feed, mixer_rows))
    mixer = chips_of(after(mixer_rows, own_feed).reshape(-1, width), done=(fspec,))
    feed_rows = after(feed_rows, *mixer[1:])
    up, down = (feed_rows[:, side].reshape(-1, width) for side in range(2))
    up_x, down_y = swap(up, "dp", 2), swap(down, "dp", 4)
    mixer = [far(piece) for piece in pair_of(mixer)]

    outs = project(level, x, gain_first, mixer, mesh_rows)
    mixed_in, (value, gate_one, gate_two, weight_out, normed_low) = outs[:mesh_rows], outs[mesh_rows:]
    value, gate_one, gate_two = (part.reshape(channels, spots) for part in (value, gate_one, gate_two))
    weight_out = weight_out.reshape(channels, width)
    received = levels_of([part.reshape(own_channels, spots) for part in mixed_in])
    up_x, down_y = after(up_x, *received[1:]), after(down_y, *received[1:])
    quarter = ((2, mesh_rows * hidden, width), bf16)
    up_pair, down_pair = whole_call(stack_kernel, [quarter] * 2, name="feed_pairs", count=4, room=8)(
        up, up_x, down, down_y
    )
    up_pair, down_pair = swap(up_pair, "dp", 4), swap(down_pair, "dp", 2)
    *conv_out, uspec = conv_forward(level, received, fspec, tables)
    conv = levels_of(conv_out)
    ups = [after(up_pair, *conv[1:]), up, up_x]
    downs = [after(down_pair, *conv[1:]), down, down_y]
    ups, downs = (
        [pair, swap(pair, "dp", 1), one, two, swap(one, "dp", 1), swap(two, "dp", 1)]
        for pair, one, two in (ups, downs)
    )

    wide, tall = ((spots, width), f32), ((channels, spots), bf16)
    outs = feed_forward(
        level,
        (far(x), far(gate_two), far(weight_out), gain_second[None], far(grad_rows)),
        conv,
        ups,
        downs,
        channels,
    )
    mixer_low, block_out, grad_mid, mid_low, gain_second_grad, grad_two = outs[:6]
    grad_conv, (up_near, up_far, down_near, down_far) = outs[6 : 6 + mesh_rows], outs[6 + mesh_rows :]
    received = levels_of(grad_conv)
    late_shape = ((4, 2 * mesh_rows * rows, width), bf16)
    late_near, late_far = whole_call(
        partial(late_kernel, **sizes), [late_shape] * 2, [((channels, width), f32)], name="late_grads", count=4
    )(grad_two, normed_low, mixer_low, mid_low)
    half = ((2, mesh_rows, hidden + rows, width), bf16)
    up_keep, up_send, down_keep, down_send = whole_call(
        partial(kept_kernel, hidden=hidden, **sizes), [half] * 4, name="kept", count=6, room=20
    )(
        up_near,
        swap(up_far, "dp", 1, received[1:]),
        down_near,
        swap(down_far, "dp", 1, received[1:]),
        late_near,
        swap(late_far, "dp", 1, received[1:]),
    )
    up_in, down_in = swap(up_send, "dp", 2), swap(down_send, "dp", 4)

    outs = conv_mixed(level, received, fspec, tables)
    mixed_out, gspec = outs[:mesh_rows], outs[mesh_rows]
    mixed = levels_of(mixed_out)
    filt_grad = conv_filt(gspec, uspec, tables, taps, width, length)
    quarter = (half[0][1:], bf16)
    up_keep, up_send, down_keep, down_send = whole_call(
        pair_kernel, [quarter] * 4, name="kept_again", count=4, room=12
    )(up_keep, after(up_in, *mixed[1:]), down_keep, after(down_in, *mixed[1:]))
    up_in, down_in = swap(up_send, "dp", 4), swap(down_send, "dp", 2)
    rest_rows = (2 * mesh_rows + filt_parts) * rows
    rest_near, rest_far, grad_value, grad_one = whole_call(
        partial(rest_kernel, **sizes),
        [((4, rest_rows, width), bf16)] * 2 + [pltpu.HBM(*tall)] * 2,
        [((channels, width), f32)],
        name="rest_grads",
        smem=1,
        count=mesh_rows + 4,
        room=12,
    )(level, *mixed, value, gate_one, normed_low, filt_grad)
    rest = whole_call(split_kernel, [((rest_rows, width), bf16)] * 4, name="rest_kept", count=2)(
        rest_near, swap(rest_far, "dp", 1)
    )
    (bulk,) = whole_call(
        bulk_kernel, [pltpu.HBM((mesh_rows, 2 * (hidden + rows), width), bf16)], name="bulk_sum", count=4
    )(up_keep, after(up_in, rest_near), down_keep, after(down_in, rest_near))
    bulk = turn(bulk)
    rest = [rest[0]] + [swap(rest[chip], "dp", 2 * chip) for chip in range(1, 4)]
    grad_tokens, gain_first_grad = whole_call(
        partial(first_norm_kernel, **sizes),
        [wide, ((1, width), f32)],
        [((4 * mesh_rows * rows, spots), bf16), wide],
        name="first_norm_back",
        count=14,
        room=20,
    )(far(grad_value), far(grad_one), far(grad_two), *mixer, far(x), gain_first[None], far(grad_mid))
    rest = [rest[0]] + [after(piece, grad_tokens) for piece in rest[1:]]
    own_filt, *rest = whole_call(
        partial(rest_sum_kernel, rows=rows),
        [((filt_parts * rows, width), bf16)] + [((2 * rows + 8, width), bf16)] * mesh_rows,
        name="rest_sum",
        smem=2,
        count=8,
    )(place, level, *rest, kernel, pad_len[:, None], gain_first_grad, gain_second_grad)
    rest = levels_of(rest)
    (bulk,) = whole_call(mesh_sum_kernel, [(bulk.shape[1:], bf16)], name="bulk_mesh_sum", count=1)(
        after(bulk, *rest[1:])
    )
    bulk = chips_of(bulk)
    (rest,) = whole_call(
        rest_mesh_sum_kernel, [(((2 + filt_parts) * rows + 8, width), bf16)], name="rest_mesh_sum", count=1 + mesh_rows
    )(own_filt, *rest)
    rest = chips_of(rest)
    bulk = pair_of(bulk)
    rest = pair_of(rest)
    channel_rows = ((own_channels, width), f32)
    up_grad, down_grad, two_grad, out_grad = whole_call(
        partial(unpack_bulk_kernel, hidden=hidden, rows=rows),
        [(up_weight.shape, f32), (down_weight.shape, f32), channel_rows, channel_rows],
        [(down_weight.shape, f32)],
        name="unpack_bulk",
        smem=1,
        count=8,
        room=14,
    )(place, *bulk)
    in_grad, kernel_grad, gains = whole_call(
        partial(unpack_rest_kernel, rows=rows),
        [((3, own_channels, width), f32), (kernel.shape, f32), ((2, width), f32)],
        [((8, 2, width), f32)],
        name="unpack_rest",
        smem=1,
        count=9,
        room=8,
    )(place, *rest, two_grad)
    return (
        block_out[None],
        grad_tokens[None],
        gains[0],
        in_grad.transpose(2, 0, 1),
        kernel_grad,
        out_grad,
        gains[1],
        up_grad,
        down_grad,
    )


def body(tables, *arrays):
    ways = lax.axis_size("dp")
    whole_tiles = arrays[3].shape[0] % (8 * ways) == 0 and arrays[7].shape[1] % (32 * ways) == 0
    assert arrays[0].shape[0] == 1
    return (fast_body if ways == 8 and whole_tiles else plain_body)(tables, *arrays)


def solution(mesh):
    in_specs = (
        P("dp", "mp", None),
        P(),
        P(None, None, "mp"),
        P("mp", None),
        P("mp"),
        P("mp", None),
        P(),
        P(None, "mp"),
        P("mp", None),
        P("dp", "mp", None),
    )
    out_specs = (
        P("dp", "mp", None),
        P("dp", "mp", None),
        P(),
        P(None, None, "mp"),
        P("mp", None),
        P("mp", None),
        P(),
        P(None, "mp"),
        P("mp", None),
    )

    def program(tokens, *rest):
        tables = dft_tables(tokens.shape[1])
        inner = jax.shard_map(
            body, mesh=mesh, in_specs=((P(), P(), P()),) + in_specs, out_specs=out_specs, check_vma=False
        )
        return inner(tables, tokens, *rest)

    return program
```

profile of v0, /device:TPU:0, one launch (start us, length us, event | category | flops | bytes accessed | tf_op | source)
XLA Modules:
  0.0 324.4 jit_solution(17355791946893232747)
XLA Ops:
  3.3 6.3 %all-to-all-start = ((bf16[4,4,24,768]{3,2,1,0:T(8,128)(2,1)}), bf16[4,4,24,768]{3,2,1,0:T(8,128)(2,1)}, u32[]{:S(2)}, u32[]{:S(2)}) async-start(bf16[4,4,24,768]{3,2,1,0:T(8,128)(2,1)} %broadcast_in_dim.39), calls=%async_computation | async-start | bytes 1179648 | tf_op jit(solution)/shard_map/all_to_all | solution.py:435
  10.9 14.8 %all-to-all-done = bf16[4,4,24,768]{3,2,1,0:T(8,128)(2,1)} async-done(((bf16[4,4,24,768]{3,2,1,0:T(8,128)(2,1)}), bf16[4,4,24,768]{3,2,1,0:T(8,128)(2,1)}, u32[]{:S(2)}, u32[]{:S(2)}) %all-to-all-start) | async-done | bytes 589856 | tf_op jit(solution)/shard_map/all_to_all | solution.py:435
  26.7 4.4 %all-to-all-start.1 = ((bf16[4,2,96,768]{3,2,1,0:T(8,128)(2,1)}), bf16[4,2,96,768]{3,2,1,0:T(8,128)(2,1)}, u32[]{:S(2)}, u32[]{:S(2)}) async-start(bf16[4,2,96,768]{3,2,1,0:T(8,128)(2,1)} %broadcast_in_dim.40), calls=%async_computation.1 | async-start | bytes 2359296 | tf_op jit(solution)/shard_map/all_to_all | solution.py:435
  37.3 5.0 %filter_spectrum.1.refs_4_ = f32[1536,512]{1,0:T(8,128)S(1)} custom-call(s32[1]{0:T(128)} %bitcast.8.here_ref, f32[192,2048]{1,0:T(8,128)S(1)} %copy-done.5, s32[192,1]{1,0:T(8,128)S(1)} %copy.27.pad_ref, bf16[512,512]{1,0:T(8,128)(2,1)S(1)} %fusion.high_ref.refs_5_, bf16[512,512]{1,0:T(8,128)(2,1)S(1)} %subtract_convert_fusion.low_ref, ...), custom_call_target="tpu_custom_call" | custom-call | tf_op jit(solution)/shard_map/filter_spectrum/pallas_call | solution.py:705
  42.3 6.4 %collective-permute-done.2.refs_3_.refs_6_ = bf16[384,768]{1,0:T(8,128)(2,1)} collective-permute-done((bf16[384,768]{1,0:T(8,128)(2,1)}, bf16[384,768]{1,0:T(8,128)(2,1)}, u32[]{:S(2)}, u32[]{:S(2)}) %collective-permute-start.2) | collective-permute-done | bytes 589856 | tf_op jit(solution)/shard_map/ppermute | solution.py:366
  48.7 10.6 %collective-permute-done.1.refs_2_.refs_5_ = bf16[384,768]{1,0:T(8,128)(2,1)} collective-permute-done((bf16[384,768]{1,0:T(8,128)(2,1)}, bf16[384,768]{1,0:T(8,128)(2,1)}, u32[]{:S(2)}, u32[]{:S(2)}) %collective-permute-start.1) | collective-permute-done | bytes 589856 | tf_op jit(solution)/shard_map/ppermute | solution.py:366
  65.8 7.6 %project.1 = (bf16[2,4,24,512]{3,2,1,0:T(8,128)(2,1)}, bf16[2,4,24,512]{3,2,1,0:T(8,128)(2,1)}, bf16[2,4,24,512]{3,2,1,0:T(8,128)(2,1)}, bf16[2,4,24,512]{3,2,1,...) custom-call(s32[1]{0:T(128)} %bitcast.level_ref.here_ref.refs_0_, ...), custom_call_target="tpu_custom_call" | custom-call | tf_op jit(solution)/shard_map/project/pallas_call | solution.py:761
  77.8 6.0 %collective-permute-done.7.refs_1_ = bf16[192,512]{1,0:T(8,128)(2,1)S(1)} collective-permute-done((bf16[192,512]{1,0:T(8,128)(2,1)}, bf16[192,512]{1,0:T(8,128)(2,1)S(1)}, u32[]{:S(2)}, u32[]{:S(2)}) %collective-permute-start.7) | collective-permute-done | bytes 196640 | tf_op jit(solution)/shard_map/ppermute | solution.py:366
  83.8 8.6 %collective-permute-done.8.refs_2_ = bf16[192,512]{1,0:T(8,128)(2,1)S(1)} collective-permute-done((bf16[192,512]{1,0:T(8,128)(2,1)}, bf16[192,512]{1,0:T(8,128)(2,1)S(1)}, u32[]{:S(2)}, u32[]{:S(2)}) %collective-permute-start.8) | collective-permute-done | bytes 196640 | tf_op jit(solution)/shard_map/ppermute | solution.py:366
  96.0 6.3 %conv_forward.1 = (bf16[192,512]{1,0:T(8,128)(2,1)S(1)}, bf16[192,512]{1,0:T(8,128)(2,1)S(1)}, bf16[192,512]{1,0:T(8,128)(2,1)S(1)}, bf16[192,512]{1,0:T(8,128)(2,1)S(1)}, bf16[1536,512]{1,0:T(8,128)(2,1)}) custom-call(s32[1]{0:T(128)} %bitcast.level_ref.here_ref.refs_0_, bf16[192,512]{1,0:T(8,128)(2,1)S(1)} %bitcast.33, ...), custom_call_target="tpu_custom_call" | custom-call | tf_op jit(solution)/shard_map/conv_forward/pallas_call | solution.py:274
  102.3 3.5 %collective-permute-start.10 = (bf16[192,512]{1,0:T(8,128)(2,1)S(1)}, bf16[192,512]{1,0:T(8,128)(2,1)S(1)}, u32[]{:S(2)}, u32[]{:S(2)}) collective-permute-start(bf16[192,512]{1,0:T(8,128)(2,1)S(1)} %get-tuple-element.108), channel_id=1, source_target_pairs={{0,1},{1,0},{2,3},{3,2},{4,5},{5,4},{6,7},{7,6},{8,9},{9,8},{10,11... | collective-permute-start | bytes 589832 | tf_op jit(solution)/shard_map/ppermute | solution.py:366
  108.2 3.7 %collective-permute-done.10.refs_7_ = bf16[192,512]{1,0:T(8,128)(2,1)S(1)} collective-permute-done((bf16[192,512]{1,0:T(8,128)(2,1)S(1)}, bf16[192,512]{1,0:T(8,128)(2,1)S(1)}, u32[]{:S(2)}, u32[]{:S(2)}) %collective-permute-start.10) | collective-permute-done | bytes 196640 | tf_op jit(solution)/shard_map/ppermute | solution.py:366
  111.9 10.2 %collective-permute-done.11.refs_8_ = bf16[192,512]{1,0:T(8,128)(2,1)S(1)} collective-permute-done((bf16[192,512]{1,0:T(8,128)(2,1)S(1)}, bf16[192,512]{1,0:T(8,128)(2,1)S(1)}, u32[]{:S(2)}, u32[]{:S(2)}) %collective-permute-start.11) | collective-permute-done | bytes 196640 | tf_op jit(solution)/shard_map/ppermute | solution.py:366
  123.2 3.6 %collective-permute-done.21.refs_20_ = bf16[384,768]{1,0:T(8,128)(2,1)S(1)} collective-permute-done((bf16[384,768]{1,0:T(8,128)(2,1)}, bf16[384,768]{1,0:T(8,128)(2,1)S(1)}, u32[]{:S(2)}, u32[]{:S(2)}) %collective-permute-start.21) | collective-permute-done | bytes 589856 | tf_op jit(solution)/shard_map/ppermute | solution.py:366
  130.4 28.5 %feed_forward.1 = (bf16[768,512]{1,0:T(8,128)(2,1)S(1)}, bf16[512,768]{1,0:T(8,128)(2,1)}, f32[512,768]{1,0:T(8,128)}, bf16[512,768]{1,0:T(8,128)(2,1)S(1)}, f32...) custom-call(s32[1]{0:T(128)} %bitcast.level_ref.here_ref.refs_0_, ...), custom_call_target="tpu_custom_call" | custom-call | tf_op jit(solution)/shard_map/feed_forward/pallas_call | solution.py:886
  165.7 8.5 %collective-permute-done.23.refs_1_ = bf16[192,512]{1,0:T(8,128)(2,1)S(1)} collective-permute-done((bf16[192,512]{1,0:T(8,128)(2,1)S(1)}, bf16[192,512]{1,0:T(8,128)(2,1)S(1)}, u32[]{:S(2)}, u32[]{:S(2)}) %collective-permute-start.23) | collective-permute-done | bytes 196640 | tf_op jit(solution)/shard_map/ppermute | solution.py:366
  177.1 5.7 %collective-permute-done.25.refs_3_ = bf16[192,512]{1,0:T(8,128)(2,1)S(1)} collective-permute-done((bf16[192,512]{1,0:T(8,128)(2,1)S(1)}, bf16[192,512]{1,0:T(8,128)(2,1)S(1)}, u32[]{:S(2)}, u32[]{:S(2)}) %collective-permute-start.25) | collective-permute-done | bytes 196640 | tf_op jit(solution)/shard_map/ppermute | solution.py:366
  188.1 5.1 %conv_mixed.1 = (bf16[192,512]{1,0:T(8,128)(2,1)S(1)}, bf16[192,512]{1,0:T(8,128)(2,1)S(1)}, bf16[192,512]{1,0:T(8,128)(2,1)S(1)}, bf16[192,512]{1,0:T(8,128)(2,1)S(1)}, f32[1536,512]{1,0:T(8,128)S(1)}) custom-call(s32[1]{0:T(128)} %bitcast.level_ref.here_ref.refs_0_, bf16[192,512]{1,0:T(8,128)(2,1)S(1)} %get-tuple-element.120.refs_0_, ...), custom_call_target="tpu_custom_call" | custom-call | tf_op jit(solution)/shard_map/conv_mixed/pallas_call | solution.py:293
  198.8 4.6 %collective-permute-done.26.refs_2_ = bf16[192,512]{1,0:T(8,128)(2,1)S(1)} collective-permute-done((bf16[192,512]{1,0:T(8,128)(2,1)S(1)}, bf16[192,512]{1,0:T(8,128)(2,1)S(1)}, u32[]{:S(2)}, u32[]{:S(2)}) %collective-permute-start.26) | collective-permute-done | bytes 196640 | tf_op jit(solution)/shard_map/ppermute | solution.py:366
  203.5 9.6 %collective-permute-done.27.refs_3_ = bf16[192,512]{1,0:T(8,128)(2,1)S(1)} collective-permute-done((bf16[192,512]{1,0:T(8,128)(2,1)S(1)}, bf16[192,512]{1,0:T(8,128)(2,1)S(1)}, u32[]{:S(2)}, u32[]{:S(2)}) %collective-permute-start.27) | collective-permute-done | bytes 196640 | tf_op jit(solution)/shard_map/ppermute | solution.py:366
  213.1 5.9 %collective-permute-done.46.up_in = bf16[2,4,120,768]{3,2,1,0:T(8,128)(2,1)S(1)} collective-permute-done((bf16[2,4,120,768]{3,2,1,0:T(8,128)(2,1)S(1)}, bf16[2,4,120,768]{3,2,1,0:T(8,128)(2,1)S(1)}, u32[]{:S(2)}, u32[]{:S(2)}) %collective-permute-start.46) | collective-permute-done | bytes 1474592 | tf_op jit(solution)/shard_map/ppermute | solution.py:366
  227.9 9.1 %collective-permute-done.48.up_in = bf16[4,120,768]{2,1,0:T(8,128)(2,1)S(1)} collective-permute-done((bf16[4,120,768]{2,1,0:T(8,128)(2,1)S(1)}, bf16[4,120,768]{2,1,0:T(8,128)(2,1)S(1)}, u32[]{:S(2)}, u32[]{:S(2)}) %collective-permute-start.48) | collective-permute-done | bytes 737312 | tf_op jit(solution)/shard_map/ppermute | solution.py:366
  238.9 6.5 %all-to-all-start.2 = ((bf16[4,240,768]{2,1,0:T(8,128)(2,1)}), bf16[4,240,768]{2,1,0:T(8,128)(2,1)S(1)}, u32[]{:S(2)}, u32[]{:S(2)}) async-start(bf16[4,240,768]{2,1,0:T(8,128)(2,1)} %bulk_sum.1), calls=%async_computation.2 | async-start | bytes 2949120 | tf_op jit(solution)/shard_map/all_to_all | solution.py:435
  245.5 3.7 %collective-permute-done.29.far_ref = bf16[4,264,768]{2,1,0:T(8,128)(2,1)S(1)} collective-permute-done((bf16[4,264,768]{2,1,0:T(8,128)(2,1)}, bf16[4,264,768]{2,1,0:T(8,128)(2,1)S(1)}, u32[]{:S(2)}, u32[]{:S(2)}) %collective-permute-start.29) | collective-permute-done | bytes 1622048 | tf_op jit(solution)/shard_map/ppermute | solution.py:366
  253.1 9.1 %first_norm_back.1 = (f32[512,768]{1,0:T(8,128)}, f32[1,768]{1,0:T(1,128)S(1)}) custom-call(bf16[768,512]{1,0:T(8,128)(2,1)} %get-tuple-element.133.refs_0_, bf16[768,512]{1,0:T(8,128)(2,1)} %get-tuple-element.134.refs_1_, bf16[768,512]{1,0:T(8,128)(2,1)} %get-tuple-element.135.refs_2_.grad_two_ref, bf16[384,768]{1,0:T(8,128)(2,1)} %bitcast.7.refs_0_.refs_3_, ...), custom_call_target="tpu_custom_call" | custom-call | tf_op jit(solution)/shard_map/first_norm_back/pallas_call | solution.py:1247
  262.2 8.3 %collective-permute-done.31.p2 = bf16[264,768]{1,0:T(8,128)(2,1)S(1)} collective-permute-done((bf16[264,768]{1,0:T(8,128)(2,1)S(1)}, bf16[264,768]{1,0:T(8,128)(2,1)S(1)}, u32[]{:S(2)}, u32[]{:S(2)}) %collective-permute-start.31) | collective-permute-done | bytes 405536 | tf_op jit(solution)/shard_map/ppermute | solution.py:366
  275.8 3.4 %collective-permute-done.33.refs_1_ = bf16[56,768]{1,0:T(8,128)(2,1)S(1)} collective-permute-done((bf16[56,768]{1,0:T(8,128)(2,1)S(1)}, bf16[56,768]{1,0:T(8,128)(2,1)S(1)}, u32[]{:S(2)}, u32[]{:S(2)}) %collective-permute-start.33) | collective-permute-done | bytes 86048 | tf_op jit(solution)/shard_map/ppermute | solution.py:366
  279.2 5.4 %collective-permute-done.34.refs_2_ = bf16[56,768]{1,0:T(8,128)(2,1)S(1)} collective-permute-done((bf16[56,768]{1,0:T(8,128)(2,1)S(1)}, bf16[56,768]{1,0:T(8,128)(2,1)S(1)}, u32[]{:S(2)}, u32[]{:S(2)}) %collective-permute-start.34) | collective-permute-done | bytes 86048 | tf_op jit(solution)/shard_map/ppermute | solution.py:366
  291.0 10.4 %collective-permute-done.38.refs_3_ = bf16[128,768]{1,0:T(8,128)(2,1)S(1)} collective-permute-done((bf16[128,768]{1,0:T(8,128)(2,1)S(1)}, bf16[128,768]{1,0:T(8,128)(2,1)S(1)}, u32[]{:S(2)}, u32[]{:S(2)}) %collective-permute-start.38) | collective-permute-done | bytes 196640 | tf_op jit(solution)/shard_map/ppermute | solution.py:366
  302.0 4.6 %collective-permute-done.51.refs_2_ = bf16[240,768]{1,0:T(8,128)(2,1)S(1)} collective-permute-done((bf16[240,768]{1,0:T(8,128)(2,1)S(1)}, bf16[240,768]{1,0:T(8,128)(2,1)S(1)}, u32[]{:S(2)}, u32[]{:S(2)}) %collective-permute-start.51) | collective-permute-done | bytes 368672 | tf_op jit(solution)/shard_map/ppermute | solution.py:366
  306.5 4.1 %collective-permute-done.37.refs_2_ = bf16[128,768]{1,0:T(8,128)(2,1)S(1)} collective-permute-done((bf16[128,768]{1,0:T(8,128)(2,1)S(1)}, bf16[128,768]{1,0:T(8,128)(2,1)S(1)}, u32[]{:S(2)}, u32[]{:S(2)}) %collective-permute-start.37) | collective-permute-done | bytes 196640 | tf_op jit(solution)/shard_map/ppermute | solution.py:366
  311.8 5.7 %collective-permute-done.36.refs_1_ = bf16[128,768]{1,0:T(8,128)(2,1)S(1)} collective-permute-done((bf16[128,768]{1,0:T(8,128)(2,1)S(1)}, bf16[128,768]{1,0:T(8,128)(2,1)S(1)}, u32[]{:S(2)}, u32[]{:S(2)}) %collective-permute-start.36) | collective-permute-done | bytes 196640 | tf_op jit(solution)/shard_map/ppermute | solution.py:366
  (167 shorter events, 88.3 us)
Async XLA Ops:
  3.3 22.3 %all-to-all-start = ((bf16[4,4,24,768]{3,2,1,0:T(8,128)(2,1)}), bf16[4,4,24,768]{3,2,1,0:T(8,128)(2,1)}, u32[]{:S(2)}, u32[]{:S(2)}) async-start(bf16[4,4,24,768]{3,2,1,0:T(8,128)(2,1)} %broadcast_in_dim.39), calls=%async_computation | async-start | bytes 1179648 | tf_op jit(solution)/shard_map/all_to_all | solution.py:435
  26.7 33.2 %all-to-all-start.1 = ((bf16[4,2,96,768]{3,2,1,0:T(8,128)(2,1)}), bf16[4,2,96,768]{3,2,1,0:T(8,128)(2,1)}, u32[]{:S(2)}, u32[]{:S(2)}) async-start(bf16[4,2,96,768]{3,2,1,0:T(8,128)(2,1)} %broadcast_in_dim.40), calls=%async_computation.1 | async-start | bytes 2359296 | tf_op jit(solution)/shard_map/all_to_all | solution.py:435
  31.1 17.6 %collective-permute-start.2 = (bf16[384,768]{1,0:T(8,128)(2,1)}, bf16[384,768]{1,0:T(8,128)(2,1)}, u32[]{:S(2)}, u32[]{:S(2)}) collective-permute-start(bf16[384,768]{1,0:T(8,128)(2,1)} %bitcast.7.refs_0_.refs_3_), channel_id=1, source_target_pairs={{0,24},{4,28},{8,16},{12,20},{16,8},{20,12},{24,0},{28,4},{1,25},{... | collective-permute-start | bytes 1769480 | tf_op jit(solution)/shard_map/ppermute | solution.py:366
  33.6 25.7 %collective-permute-start.1 = (bf16[384,768]{1,0:T(8,128)(2,1)}, bf16[384,768]{1,0:T(8,128)(2,1)}, u32[]{:S(2)}, u32[]{:S(2)}) collective-permute-start(bf16[384,768]{1,0:T(8,128)(2,1)} %bitcast.7.refs_0_.refs_3_), channel_id=1, source_target_pairs={{0,16},{4,20},{8,24},{12,28},{16,0},{20,4},{24,8},{28,12},{1,17},{... | collective-permute-start | bytes 1769480 | tf_op jit(solution)/shard_map/ppermute | solution.py:366
  34.2 25.3 %collective-permute-start = (bf16[384,768]{1,0:T(8,128)(2,1)}, bf16[384,768]{1,0:T(8,128)(2,1)}, u32[]{:S(2)}, u32[]{:S(2)}) collective-permute-start(bf16[384,768]{1,0:T(8,128)(2,1)} %bitcast.7.refs_0_.refs_3_), channel_id=1, source_target_pairs={{0,8},{4,12},{8,0},{12,4},{16,24},{20,28},{24,16},{28,20},{1,9},{5... | collective-permute-start | bytes 1769480 | tf_op jit(solution)/shard_map/ppermute | solution.py:366
  35.9 27.9 %collective-permute-start.3 = (bf16[384,768]{1,0:T(8,128)(2,1)}, bf16[384,768]{1,0:T(8,128)(2,1)}, u32[]{:S(2)}, u32[]{:S(2)}) collective-permute-start(bf16[384,768]{1,0:T(8,128)(2,1)} %bitcast.7.refs_0_.refs_3_), channel_id=1, source_target_pairs={{0,4},{4,0},{8,12},{12,8},{16,20},{20,16},{24,28},{28,24},{1,5},{5... | collective-permute-start | bytes 1769480 | tf_op jit(solution)/shard_map/ppermute | solution.py:366
  62.3 30.0 %collective-permute-start.14 = (bf16[384,768]{1,0:T(8,128)(2,1)}, bf16[384,768]{1,0:T(8,128)(2,1)}, u32[]{:S(2)}, u32[]{:S(2)}) collective-permute-start(bf16[384,768]{1,0:T(8,128)(2,1)} %bitcast.18.refs_2_.refs_18_), channel_id=1, source_target_pairs={{0,16},{4,20},{8,24},{12,28},{16,0},{20,4},{24,8},{28,12},{1,17},{... | collective-permute-start | bytes 1769480 | tf_op jit(solution)/shard_map/ppermute | solution.py:366
  63.8 28.6 %collective-permute-start.13 = (bf16[384,768]{1,0:T(8,128)(2,1)}, bf16[384,768]{1,0:T(8,128)(2,1)}, u32[]{:S(2)}, u32[]{:S(2)}) collective-permute-start(bf16[384,768]{1,0:T(8,128)(2,1)} %bitcast.17.refs_0_.refs_14_), channel_id=1, source_target_pairs={{0,8},{4,12},{8,0},{12,4},{16,24},{20,28},{24,16},{28,20},{1,9},{5... | collective-permute-start | bytes 1769480 | tf_op jit(solution)/shard_map/ppermute | solution.py:366
  75.0 17.3 %collective-permute-start.8 = (bf16[192,512]{1,0:T(8,128)(2,1)}, bf16[192,512]{1,0:T(8,128)(2,1)S(1)}, u32[]{:S(2)}, u32[]{:S(2)}) collective-permute-start(bf16[192,512]{1,0:T(8,128)(2,1)} %bitcast.43), channel_id=1, source_target_pairs={{0,2},{1,3},{2,0},{3,1},{4,6},{5,7},{6,4},{7,5},{8,10},{9,11},{10,... | collective-permute-start | bytes 589832 | tf_op jit(solution)/shard_map/ppermute | solution.py:366
  77.4 15.0 %collective-permute-start.9 = (bf16[192,512]{1,0:T(8,128)(2,1)}, bf16[192,512]{1,0:T(8,128)(2,1)S(1)}, u32[]{:S(2)}, u32[]{:S(2)}) collective-permute-start(bf16[192,512]{1,0:T(8,128)(2,1)} %bitcast.42), channel_id=1, source_target_pairs={{0,3},{1,2},{2,1},{3,0},{4,7},{5,6},{6,5},{7,4},{8,11},{9,10},{10,... | collective-permute-start | bytes 589832 | tf_op jit(solution)/shard_map/ppermute | solution.py:366
  94.1 27.9 %collective-permute-start.15 = (bf16[2,384,768]{2,1,0:T(8,128)(2,1)S(1)}, bf16[2,384,768]{2,1,0:T(8,128)(2,1)S(1)}, u32[]{:S(2)}, u32[]{:S(2)}) collective-permute-start(bf16[2,384,768]{2,1,0:T(8,128)(2,1)S(1)} %get-tuple-element.115), channel_id=1, source_target_pairs={{0,16},{4,20},{8,24},{12,28},{16,0},{20,4},{24,8},{28,12},{1,17},{... | collective-permute-start | bytes 3538952 | tf_op jit(solution)/shard_map/ppermute | solution.py:366
  95.5 26.6 %collective-permute-start.17 = (bf16[2,384,768]{2,1,0:T(8,128)(2,1)S(1)}, bf16[2,384,768]{2,1,0:T(8,128)(2,1)S(1)}, u32[]{:S(2)}, u32[]{:S(2)}) collective-permute-start(bf16[2,384,768]{2,1,0:T(8,128)(2,1)S(1)} %get-tuple-element.117), channel_id=1, source_target_pairs={{0,8},{4,12},{8,0},{12,4},{16,24},{20,28},{24,16},{28,20},{1,9},{5... | collective-permute-start | bytes 3538952 | tf_op jit(solution)/shard_map/ppermute | solution.py:366
  105.8 16.2 %collective-permute-start.11 = (bf16[192,512]{1,0:T(8,128)(2,1)S(1)}, bf16[192,512]{1,0:T(8,128)(2,1)S(1)}, u32[]{:S(2)}, u32[]{:S(2)}) collective-permute-start(bf16[192,512]{1,0:T(8,128)(2,1)S(1)} %get-tuple-element.109), channel_id=1, source_target_pairs={{0,2},{1,3},{2,0},{3,1},{4,6},{5,7},{6,4},{7,5},{8,10},{9,11},{10,... | collective-permute-start | bytes 589832 | tf_op jit(solution)/shard_map/ppermute | solution.py:366
  106.7 15.3 %collective-permute-start.12 = (bf16[192,512]{1,0:T(8,128)(2,1)S(1)}, bf16[192,512]{1,0:T(8,128)(2,1)S(1)}, u32[]{:S(2)}, u32[]{:S(2)}) collective-permute-start(bf16[192,512]{1,0:T(8,128)(2,1)S(1)} %get-tuple-element.110), channel_id=1, source_target_pairs={{0,3},{1,2},{2,1},{3,0},{4,7},{5,6},{6,5},{7,4},{8,11},{9,10},{10,... | collective-permute-start | bytes 589832 | tf_op jit(solution)/shard_map/ppermute | solution.py:366
  158.9 23.9 %collective-permute-start.43 = (bf16[1536,768]{1,0:T(8,128)(2,1)}, bf16[1536,768]{1,0:T(8,128)(2,1)S(1)}, u32[]{:S(2)}, u32[]{:S(2)}) collective-permute-start(bf16[1536,768]{1,0:T(8,128)(2,1)} %get-tuple-element.155), channel_id=1, source_target_pairs={{0,4},{4,0},{8,12},{12,8},{16,20},{20,16},{24,28},{28,24},{1,5},{5... | collective-permute-start | bytes 7077896 | tf_op jit(solution)/shard_map/ppermute | solution.py:366
  159.1 23.7 %collective-permute-start.44 = (bf16[1536,768]{1,0:T(8,128)(2,1)}, bf16[1536,768]{1,0:T(8,128)(2,1)S(1)}, u32[]{:S(2)}, u32[]{:S(2)}) collective-permute-start(bf16[1536,768]{1,0:T(8,128)(2,1)} %get-tuple-element.158), channel_id=1, source_target_pairs={{0,4},{4,0},{8,12},{12,8},{16,20},{20,16},{24,28},{28,24},{1,5},{5... | collective-permute-start | bytes 7077896 | tf_op jit(solution)/shard_map/ppermute | solution.py:366
  162.0 20.8 %collective-permute-start.45 = (bf16[4,192,768]{2,1,0:T(8,128)(2,1)S(1)}, bf16[4,192,768]{2,1,0:T(8,128)(2,1)S(1)}, u32[]{:S(2)}, u32[]{:S(2)}) collective-permute-start(bf16[4,192,768]{2,1,0:T(8,128)(2,1)S(1)} %get-tuple-element.163), channel_id=1, source_target_pairs={{0,4},{4,0},{8,12},{12,8},{16,20},{20,16},{24,28},{28,24},{1,5},{5... | collective-permute-start | bytes 3538952 | tf_op jit(solution)/shard_map/ppermute | solution.py:366
  185.8 33.1 %collective-permute-start.46 = (bf16[2,4,120,768]{3,2,1,0:T(8,128)(2,1)S(1)}, bf16[2,4,120,768]{3,2,1,0:T(8,128)(2,1)S(1)}, u32[]{:S(2)}, u32[]{:S(2)}) collective-permute-start(bf16[2,4,120,768]{3,2,1,0:T(8,128)(2,1)S(1)} %get-tuple-element.166), channel_id=1, source_target_pairs={{0,8},{4,12},{8,0},{12,4},{16,24},{20,28},{24,16},{28,20},{1,9},{5... | collective-permute-start | bytes 4423688 | tf_op jit(solution)/shard_map/ppermute | solution.py:366
  187.3 32.8 %collective-permute-start.47 = (bf16[2,4,120,768]{3,2,1,0:T(8,128)(2,1)S(1)}, bf16[2,4,120,768]{3,2,1,0:T(8,128)(2,1)S(1)}, u32[]{:S(2)}, u32[]{:S(2)}) collective-permute-start(bf16[2,4,120,768]{3,2,1,0:T(8,128)(2,1)S(1)} %get-tuple-element.169), channel_id=1, source_target_pairs={{0,16},{4,20},{8,24},{12,28},{16,0},{20,4},{24,8},{28,12},{1,17},{... | collective-permute-start | bytes 4423688 | tf_op jit(solution)/shard_map/ppermute | solution.py:366
  196.4 16.7 %collective-permute-start.27 = (bf16[192,512]{1,0:T(8,128)(2,1)S(1)}, bf16[192,512]{1,0:T(8,128)(2,1)S(1)}, u32[]{:S(2)}, u32[]{:S(2)}) collective-permute-start(bf16[192,512]{1,0:T(8,128)(2,1)S(1)} %get-tuple-element.126), channel_id=1, source_target_pairs={{0,2},{1,3},{2,0},{3,1},{4,6},{5,7},{6,4},{7,5},{8,10},{9,11},{10,... | collective-permute-start | bytes 589832 | tf_op jit(solution)/shard_map/ppermute | solution.py:366
  197.4 15.7 %collective-permute-start.28 = (bf16[192,512]{1,0:T(8,128)(2,1)S(1)}, bf16[192,512]{1,0:T(8,128)(2,1)S(1)}, u32[]{:S(2)}, u32[]{:S(2)}) collective-permute-start(bf16[192,512]{1,0:T(8,128)(2,1)S(1)} %get-tuple-element.127), channel_id=1, source_target_pairs={{0,3},{1,2},{2,1},{3,0},{4,7},{5,6},{6,5},{7,4},{8,11},{9,10},{10,... | collective-permute-start | bytes 589832 | tf_op jit(solution)/shard_map/ppermute | solution.py:366
  220.9 16.1 %collective-permute-start.48 = (bf16[4,120,768]{2,1,0:T(8,128)(2,1)S(1)}, bf16[4,120,768]{2,1,0:T(8,128)(2,1)S(1)}, u32[]{:S(2)}, u32[]{:S(2)}) collective-permute-start(bf16[4,120,768]{2,1,0:T(8,128)(2,1)S(1)} %get-tuple-element.172), channel_id=1, source_target_pairs={{0,16},{4,20},{8,24},{12,28},{16,0},{20,4},{24,8},{28,12},{1,17},{... | collective-permute-start | bytes 2211848 | tf_op jit(solution)/shard_map/ppermute | solution.py:366
  221.7 15.8 %collective-permute-start.49 = (bf16[4,120,768]{2,1,0:T(8,128)(2,1)S(1)}, bf16[4,120,768]{2,1,0:T(8,128)(2,1)S(1)}, u32[]{:S(2)}, u32[]{:S(2)}) collective-permute-start(bf16[4,120,768]{2,1,0:T(8,128)(2,1)S(1)} %get-tuple-element.175), channel_id=1, source_target_pairs={{0,8},{4,12},{8,0},{12,4},{16,24},{20,28},{24,16},{28,20},{1,9},{5... | collective-permute-start | bytes 2211848 | tf_op jit(solution)/shard_map/ppermute | solution.py:366
  238.9 45.6 %all-to-all-start.2 = ((bf16[4,240,768]{2,1,0:T(8,128)(2,1)}), bf16[4,240,768]{2,1,0:T(8,128)(2,1)S(1)}, u32[]{:S(2)}, u32[]{:S(2)}) async-start(bf16[4,240,768]{2,1,0:T(8,128)(2,1)} %bulk_sum.1), calls=%async_computation.2 | async-start | bytes 2949120 | tf_op jit(solution)/shard_map/all_to_all | solution.py:435
  250.7 19.8 %collective-permute-start.31 = (bf16[264,768]{1,0:T(8,128)(2,1)S(1)}, bf16[264,768]{1,0:T(8,128)(2,1)S(1)}, u32[]{:S(2)}, u32[]{:S(2)}) collective-permute-start(bf16[264,768]{1,0:T(8,128)(2,1)S(1)} %get-tuple-element.143), channel_id=1, source_target_pairs={{0,16},{4,20},{8,24},{12,28},{16,0},{20,4},{24,8},{28,12},{1,17},{... | collective-permute-start | bytes 1216520 | tf_op jit(solution)/shard_map/ppermute | solution.py:366
  251.5 19.1 %collective-permute-start.32 = (bf16[264,768]{1,0:T(8,128)(2,1)S(1)}, bf16[264,768]{1,0:T(8,128)(2,1)S(1)}, u32[]{:S(2)}, u32[]{:S(2)}) collective-permute-start(bf16[264,768]{1,0:T(8,128)(2,1)S(1)} %get-tuple-element.145), channel_id=1, source_target_pairs={{0,24},{4,28},{8,16},{12,20},{16,8},{20,12},{24,0},{28,4},{1,25},{... | collective-permute-start | bytes 1216520 | tf_op jit(solution)/shard_map/ppermute | solution.py:366
  284.7 16.7 %collective-permute-start.52 = (bf16[240,768]{1,0:T(8,128)(2,1)S(1)}, bf16[240,768]{1,0:T(8,128)(2,1)S(1)}, u32[]{:S(2)}, u32[]{:S(2)}) collective-permute-start(bf16[240,768]{1,0:T(8,128)(2,1)S(1)} %bulk_mesh_sum.1.refs_0_), channel_id=1, source_target_pairs={{0,24},{4,28},{8,16},{12,20},{16,8},{20,12},{24,0},{28,4},{1,25},{... | collective-permute-start | bytes 1105928 | tf_op jit(solution)/shard_map/ppermute | solution.py:366
  286.2 20.3 %collective-permute-start.51 = (bf16[240,768]{1,0:T(8,128)(2,1)S(1)}, bf16[240,768]{1,0:T(8,128)(2,1)S(1)}, u32[]{:S(2)}, u32[]{:S(2)}) collective-permute-start(bf16[240,768]{1,0:T(8,128)(2,1)S(1)} %bulk_mesh_sum.1.refs_0_), channel_id=1, source_target_pairs={{0,16},{4,20},{8,24},{12,28},{16,0},{20,4},{24,8},{28,12},{1,17},{... | collective-permute-start | bytes 1105928 | tf_op jit(solution)/shard_map/ppermute | solution.py:366
  289.1 22.7 %collective-permute-start.50 = (bf16[240,768]{1,0:T(8,128)(2,1)S(1)}, bf16[240,768]{1,0:T(8,128)(2,1)S(1)}, u32[]{:S(2)}, u32[]{:S(2)}) collective-permute-start(bf16[240,768]{1,0:T(8,128)(2,1)S(1)} %bulk_mesh_sum.1.refs_0_), channel_id=1, source_target_pairs={{0,8},{4,12},{8,0},{12,4},{16,24},{20,28},{24,16},{28,20},{1,9},{5... | collective-permute-start | bytes 1105928 | tf_op jit(solution)/shard_map/ppermute | solution.py:366
  289.8 20.8 %collective-permute-start.37 = (bf16[128,768]{1,0:T(8,128)(2,1)S(1)}, bf16[128,768]{1,0:T(8,128)(2,1)S(1)}, u32[]{:S(2)}, u32[]{:S(2)}) collective-permute-start(bf16[128,768]{1,0:T(8,128)(2,1)S(1)} %rest_mesh_sum.1.refs_0_), channel_id=1, source_target_pairs={{0,16},{4,20},{8,24},{12,28},{16,0},{20,4},{24,8},{28,12},{1,17},{... | collective-permute-start | bytes 589832 | tf_op jit(solution)/shard_map/ppermute | solution.py:366
  301.5 16.0 %collective-permute-start.53 = (bf16[240,768]{1,0:T(8,128)(2,1)S(1)}, bf16[240,768]{1,0:T(8,128)(2,1)S(1)}, u32[]{:S(2)}, u32[]{:S(2)}) collective-permute-start(bf16[240,768]{1,0:T(8,128)(2,1)S(1)} %bulk_mesh_sum.1.refs_0_), channel_id=1, source_target_pairs={{0,4},{4,0},{8,12},{12,8},{16,20},{20,16},{24,28},{28,24},{1,5},{5... | collective-permute-start | bytes 1105928 | tf_op jit(solution)/shard_map/ppermute | solution.py:366
  301.5 16.5 %collective-permute-start.56 = (bf16[240,768]{1,0:T(8,128)(2,1)S(1)}, bf16[240,768]{1,0:T(8,128)(2,1)S(1)}, u32[]{:S(2)}, u32[]{:S(2)}) collective-permute-start(bf16[240,768]{1,0:T(8,128)(2,1)S(1)} %collective-permute-done.52.refs_3_), channel_id=1, source_target_pairs={{0,4},{4,0},{8,12},{12,8},{16,20},{20,16},{24,28},{28,24},{1,5},{5... | collective-permute-start | bytes 1105928 | tf_op jit(solution)/shard_map/ppermute | solution.py:366
  (49 other events, 438.6 us)
where the time goes:
time: 325 us; the launch traced here: 324 us
  waiting for transfers between devices  158 us (49%)
  Pallas kernels  79.5 us (24%)
  starting transfers between devices  70 us (22%)
  local copies, waits for them, and re-layouts  13.2 us (4%)
    ppermute x57, waiting for transfers between devices, swap(): lax.ppermute(x, axis, [(i, i ^ bit) for i in range(lax.axis_size(axis))])  144 us
    ppermute x57, starting transfers between devices, swap(): lax.ppermute(x, axis, [(i, i ^ bit) for i in range(lax.axis_size(axis))])  52.7 us
    pallas_call x1, Pallas kernels, feed_forward(): pl.pallas_call(partial(feed_kernel, mesh_rows=mesh_rows), grid=(8,), in_s...  28.5 us
    all_to_all x3, starting transfers between devices, turn(): return lax.all_to_all(x, 'mp', 0, 0)  17.3 us
    all_to_all x3, waiting for transfers between devices, turn(): return lax.all_to_all(x, 'mp', 0, 0)  14.8 us
    pallas_call x1, Pallas kernels, fast_body(): whole_call(partial(first_norm_kernel, **sizes), [wide, ((1, width), f32)]...  9.12 us
    pallas_call x1, Pallas kernels, project(): pl.pallas_call(partial(project_kernel, rows=rows, mesh_rows=mesh_rows), g...  7.57 us
  transfers between devices with their start and end apart: 60, of which 28 were waited for; matrix products, arithmetic and copies ran while one was open for 2% of the time, Pallas kernels for 13%

commit v1 on v0

--- a/solution.py
+++ b/solution.py
@@ -218,17 +218,16 @@
 
 def conv_mixed_kernel(here_ref, *refs, parts, radix, channels, length):
     sent, (fspec_ref, high_ref, twiddle_ref) = refs[:parts], refs[parts : parts + 3]
-    mixed, (spec_ref, z, y, big, turned) = refs[parts + 3 : 2 * parts + 3], refs[2 * parts + 3 :]
+    mixed_ref, spec_ref, z, y, big, turned = refs[parts + 3 :]
     here = here_ref[0]
     for i, ref in enumerate(sent):
         turned[i ^ here] = ref[...]
     split_in(partial(cut, turned, 0), twiddle_ref, into_scratch(z, channels), radix, channels)
-    spec_ref[...] = forward_dot(z[...], high_ref[...])
-    product_loop(tile_load(spec_ref), tile_load(fspec_ref), tile_store(y), radix * channels, True)
+    big[...] = forward_dot(z[...], high_ref[...])
+    spec_ref[...] = big[...].astype(bf16)
+    product_loop(tile_load(big), tile_load(fspec_ref), tile_store(y), radix * channels, True)
     big[...] = inverse_dot(y[...], high_ref[...])
-    split_out(from_scratch(big, channels), twiddle_ref, partial(put, turned, 0), radix, channels, length)
-    for i, ref in enumerate(mixed):
-        ref[...] = turned[i ^ here]
+    split_out(from_scratch(big, channels), twiddle_ref, partial(put, mixed_ref, 0), radix, channels, length)
 
 
 def conv_filt_kernel(
@@ -292,10 +291,12 @@
     rows = radix * channels
     return pl.pallas_call(
         partial(conv_mixed_kernel, parts=parts, radix=radix, channels=channels, length=length),
-        out_shape=[jax.ShapeDtypeStruct((channels, width), bf16)] * parts
-        + [jax.ShapeDtypeStruct((rows, 2 * BASE), f32)],
+        out_shape=(
+            pltpu.HBM((parts, channels, width), bf16),
+            pltpu.HBM((rows, 2 * BASE), bf16),
+        ),
         in_specs=[SM] + [VM] * (parts + 3),
-        out_specs=[VM] * (parts + 1),
+        out_specs=(VM, VM),
         scratch_shapes=[pltpu.VMEM((rows, 2 * BASE), bf16)] * 2
         + [pltpu.VMEM((rows, 2 * BASE), f32), pltpu.VMEM((parts, channels, width), bf16)],
         compiler_params=pltpu.CompilerParams(vmem_limit_bytes=16 << 20),
@@ -603,9 +604,9 @@
     late = by_slice([dot(grad_gate_two, normed_low, 1, 0), out_grad])
     late = narrow_sum(late[0], swap(late[1], "dp", 1))
     grad_conv = after(grad_conv, down_sum.x, up_sum.x, late)
-    *mixed_out, gspec = conv_mixed(here, list(grad_conv), fspec, tables)
+    mixed_out, gspec = conv_mixed(here, list(grad_conv), fspec, tables)
     filt_grad = conv_filt(gspec, uspec, tables, length, length, length)
-    mixed_out = jnp.stack(mixed_out)
+    mixed_out = jnp.take(mixed_out, lax.iota(jnp.int32, rows_mp) ^ here_mp, axis=0)
     down_sum.step()
     up_sum.step()
     late = scatter(late, "dp", 2).astype(bf16)
@@ -710,7 +711,7 @@
         smem=1,
         count=5,
         room=14,
-    )(here, kernel, pad_len[:, None], high, low, twiddle)[0]
+    )(here, far(kernel), pad_len[:, None], far(high), far(low), far(twiddle))[0]
 
 
 def nt(a, b):
@@ -721,67 +722,64 @@
     return dot(a, b, 0, 0)
 
 
-def project_kernel(level_ref, x_ref, gain_ref, *refs, rows, mesh_rows):
-    pieces, sends = refs[:8], refs[8 : 8 + mesh_rows]
-    v_ref, one_ref, two_ref, out_ref, low_ref, weights, low, proj, sems = refs[8 + mesh_rows :]
+def first_norm_forward_kernel(x_ref, gain_ref, low_ref):
+    unit, _ = norm(x_ref[...].astype(f32))
+    low_ref[...] = (unit * gain_ref[...]).astype(bf16)
+
+
+def project_kernel(level_ref, low_ref, *refs, rows, mesh_rows):
+    groups, sends = (refs[:8], refs[8:16]), refs[16 : 16 + mesh_rows]
+    v_ref, one_ref, two_ref, out_ref, weights, sems = refs[16 + mesh_rows :]
     step = pl.program_id(0)
-    copies = [pltpu.make_async_copy(piece, weights.at[k], sems.at[k]) for k, piece in enumerate(pieces)]
+
+    def weight_copy(group, source, slot):
+        size = source.shape[0]
+        start = group * groups[0][0].shape[0]
+        return pltpu.make_async_copy(source, weights.at[slot, pl.ds(start, size), :], sems.at[group, slot])
 
     @pl.when(step == 0)
     def _():
-        for copy in copies:
-            copy.start()
-        unit, _ = norm(x_ref[...].astype(f32))
-        low[...] = (unit * gain_ref[...]).astype(bf16)
-        low_ref[...] = low[...]
+        for chip in range(4):
+            for core in range(2):
+                for group, pieces in enumerate(groups):
+                    weight_copy(group, pieces[core * 4 + chip], core * 4 + chip).start()
 
     for core in range(2):
         slot = core * 4 + step
-        pltpu.make_async_copy(pieces[0], weights.at[slot], sems.at[slot]).wait()
-        proj[...] = nt(weights[slot], low[...])
+        for group, pieces in enumerate(groups):
+            weight_copy(group, pieces[0], slot).wait()
+        proj = nt(weights[slot], low_ref[...])
         for i, send_ref in enumerate(sends):
             to = i ^ level_ref[0]
-            at = pl.multiple_of(to * (4 * rows), 8)
-            value, one, two = (proj[pl.ds(at + k * rows, rows), :] for k in range(3))
+            at = 4 * i * rows
+            value, one, two = (proj[at + k * rows : at + (k + 1) * rows] for k in range(3))
             send_ref[core, 0] = (value * one).astype(bf16)
             v_ref[to, core, 0] = value
             one_ref[to, core, 0] = one
             two_ref[to, core, 0] = two
-            at = (4 * i + 3) * rows
-            out_ref[i, core, 0] = weights[slot, at : at + rows, :]
-
-
-def project(level, x, gain, pieces, mesh_rows):
-    spots, width = x.shape
-    size = pieces[0].shape[0]
+            out_ref[to, core, 0] = weights[slot, at + 3 * rows : at + 4 * rows, :]
+
+
+def project(level, low, groups, mesh_rows):
+    spots, width = low.shape
+    size = sum(group[0].shape[0] for group in groups)
     rows = size // (4 * mesh_rows)
     block = lambda last: pl.BlockSpec((mesh_rows, 2, 1, rows, last), lambda j: (0, 0, j, 0, 0))
     shape = lambda last, dtype: pltpu.HBM((mesh_rows, 2, 4, rows, last), dtype)
-    full = pl.BlockSpec((spots, width), lambda j: (0, 0))
     return pl.pallas_call(
         partial(project_kernel, rows=rows, mesh_rows=mesh_rows),
         grid=(4,),
-        in_specs=[SM, full, pl.BlockSpec((1, width), lambda j: (0, 0))] + [pl.BlockSpec(memory_space=pl.ANY)] * 8,
+        in_specs=[SM, VM] + [pl.BlockSpec(memory_space=pl.ANY)] * 16,
         out_specs=[pl.BlockSpec((2, 1, rows, spots), lambda j: (0, j, 0, 0))] * mesh_rows
         + [block(spots)] * 3
-        + [block(width), full],
+        + [block(width)],
         out_shape=[pltpu.HBM((2, 4, rows, spots), bf16)] * mesh_rows
-        + [
-            shape(spots, f32),
-            shape(spots, f32),
-            shape(spots, f32),
-            shape(width, bf16),
-            pltpu.HBM((spots, width), bf16),
-        ],
-        scratch_shapes=[
-            pltpu.VMEM((8, size, width), bf16),
-            pltpu.VMEM((spots, width), bf16),
-            pltpu.VMEM((size, spots), f32),
-            pltpu.SemaphoreType.DMA((8,)),
-        ],
+        + [shape(spots, f32)] * 3
+        + [shape(width, bf16)],
+        scratch_shapes=[pltpu.VMEM((8, size, width), bf16), pltpu.SemaphoreType.DMA((2, 8))],
         compiler_params=pltpu.CompilerParams(vmem_limit_bytes=18 << 20),
         name="project",
-    )(level, x, gain[None], *pieces)
+    )(level, low, *groups[0], *groups[1])
 
 
 def stack_kernel(*refs):
@@ -796,8 +794,8 @@
     ups, downs, up_firsts, down_firsts = refs[:2], refs[2:4], refs[4:8], refs[8:12]
     mixer_ref, block_ref, mid_ref, mid_low_ref, gain_grad_ref, grad_two_ref = refs[12:18]
     sends, refs = refs[18 : 18 + mesh_rows], refs[18 + mesh_rows :]
-    up_near, up_far, down_near, down_far = refs[:4]
-    residual, second, out_acc, norm_acc, conv, turned, weights, grads, sems, grad_sems = refs[4:]
+    up_near, down_near, far_grads = refs[:3]
+    residual, second, out_acc, norm_acc, conv, turned, weights, grads, sems, grad_sems = refs[3:]
     step = pl.program_id(0)
     size = weights.shape[2]
     copies = []
@@ -844,7 +842,7 @@
     grads[0, slot] = tn(grad_pre, second[...]).astype(bf16)
     grads[1, slot] = tn(act_low, grad_ref[...]).astype(bf16)
     at = pl.ds(pl.multiple_of((step % 4) * size, size), size)
-    for core, outs in enumerate(((up_near, down_near), (up_far, down_far))):
+    for core, outs in enumerate(((up_near, down_near), (far_grads.at[0], far_grads.at[1]))):
 
         @pl.when(step // 4 == core)
         def _():
@@ -887,7 +885,7 @@
         partial(feed_kernel, mesh_rows=mesh_rows),
         grid=(8,),
         in_specs=[SM] + [VM] * (len(wholes) + mesh_rows) + [anywhere] * 12,
-        out_specs=[VM] * (6 + mesh_rows) + [anywhere] * 4,
+        out_specs=[VM] * (6 + mesh_rows) + [anywhere] * 3,
         out_shape=[
             tall,
             pltpu.HBM((spots, width), bf16),
@@ -897,7 +895,8 @@
             pltpu.HBM((channels, spots), bf16),
         ]
         + [piece] * mesh_rows
-        + [shape((4 * size, width), bf16)] * 4,
+        + [shape((4 * size, width), bf16)] * 2
+        + [shape((2, 4 * size, width), bf16)],
         scratch_shapes=[
             pltpu.VMEM((spots, width), f32),
             pltpu.VMEM((spots, width), bf16),
@@ -930,15 +929,13 @@
         put_slices((near_ref, far_ref), lambda i: (2 * i + kind) * rows, product, mesh_rows, rows)
 
 
-def rest_kernel(*refs, mesh_rows, rows):
-    here_ref, sent = refs[0], refs[1 : 1 + mesh_rows]
-    value_ref, one_ref, low_ref, filt_ref, near_ref, far_ref, grad_value_ref, grad_one_ref, product = refs[1 + mesh_rows :]
-    size = sent[0].shape[0]
-    for i, ref in enumerate(sent):
-        at = pl.ds(pl.multiple_of((i ^ here_ref[0]) * size, size), size)
-        mixed = ref[...].astype(f32)
-        grad_value_ref[at, :] = (mixed * one_ref[at, :]).astype(bf16)
-        grad_one_ref[at, :] = (mixed * value_ref[at, :]).astype(bf16)
+def rest_kernel(
+    mixed_ref, value_ref, one_ref, low_ref, filt_ref, near_ref, far_ref, grad_value_ref, grad_one_ref, product,
+    *, mesh_rows, rows,
+):
+    mixed = mixed_ref[...].astype(f32)
+    grad_value_ref[...] = (mixed * one_ref[...]).astype(bf16)
+    grad_one_ref[...] = (mixed * value_ref[...]).astype(bf16)
     for kind, grad_ref in enumerate((grad_value_ref, grad_one_ref)):
         product[...] = dot(grad_ref[...], low_ref[...], 1, 0)
         put_slices((near_ref, far_ref), lambda i: (2 * i + kind) * rows, product, mesh_rows, rows)
@@ -951,18 +948,19 @@
                 ref[chip, at : at + rows, :] = filt_ref[part, start : start + rows, :].astype(bf16)
 
 
-def first_norm_kernel(*refs, mesh_rows, rows):
-    grads, pieces = refs[:3], refs[3:11]
-    x_ref, gain_ref, mid_ref, tokens_ref, gain_grad_ref, gathered, acc = refs[11:]
-    for slot, ref in enumerate(pieces):
+def first_norm_kernel(level_ref, *refs, mesh_rows, rows):
+    grads, groups = refs[:3], (refs[3:11], refs[11:19])
+    x_ref, gain_ref, mid_ref, tokens_ref, gain_grad_ref, gathered, acc = refs[19:]
+    split = groups[0][0].shape[0]
+    for slot in range(8):
         for i in range(mesh_rows):
-            start = (i * 8 + slot) * rows
+            start = slot * rows
             for k, grad_ref in enumerate(grads):
                 at = (i * 4 + k) * rows
-                gathered[at : at + rows, :] = grad_ref[start : start + rows, :]
+                gathered[at : at + rows, :] = grad_ref[i ^ level_ref[0], start : start + rows, :]
             at = (i * 4 + 3) * rows
             gathered[at : at + rows, :] = jnp.zeros((rows, gathered.shape[1]), bf16)
-        term = tn(gathered[...], ref[...])
+        term = tn(gathered[:split], groups[0][slot][...]) + tn(gathered[split:], groups[1][slot][...])
         acc[...] = term if slot == 0 else acc[...] + term
     unit, inverse = norm(x_ref[...].astype(f32))
     grad, gain_grad = norm_back(unit, inverse, gain_ref[...], acc[...])
@@ -975,17 +973,17 @@
 
 
 def kept_kernel(
-    up_ref, up_in, down_ref, down_in, late_ref, late_in, up_keep, up_send, down_keep, down_send, *, mesh_rows, hidden, rows
+    up_ref, down_ref, far_in, late_ref, late_in, up_keep, up_send, down_keep, down_send, *, mesh_rows, hidden, rows
 ):
     for chip in range(4):
         for i in range(mesh_rows):
             at = slice((chip * mesh_rows + i) * hidden, (chip * mesh_rows + i + 1) * hidden)
             late = [slice((2 * i + kind) * rows, (2 * i + kind + 1) * rows) for kind in range(2)]
             out_ref, side = (up_send if chip & 1 else up_keep), chip >> 1
-            out_ref[side, i, :hidden] = add_low(up_ref[at, :], up_in[at, :])
+            out_ref[side, i, :hidden] = add_low(up_ref[at, :], far_in[0, at, :])
             out_ref[side, i, hidden:] = add_low(late_ref[chip, late[0], :], late_in[chip, late[0], :])
             out_ref, side = (down_send if chip >> 1 else down_keep), chip & 1
-            out_ref[side, i, :hidden] = add_low(down_ref[at, :], down_in[at, :])
+            out_ref[side, i, :hidden] = add_low(down_ref[at, :], far_in[1, at, :])
             out_ref[side, i, hidden:] = add_low(late_ref[chip, late[1], :], late_in[chip, late[1], :])
 
 
@@ -1058,17 +1056,21 @@
     return terms[0]
 
 
-def rest_mesh_sum_kernel(filt_ref, *refs):
+def rest_mesh_sum_kernel(bulk_ref, filt_ref, *refs):
     sent, out_ref = refs[:-1], refs[-1]
+    base = bulk_ref.shape[1]
     size = sent[0].shape[0] - 8
     filt = filt_ref.shape[0]
-    out_ref[:size] = add_low(*(ref[:size] for ref in sent))
-    out_ref[size : size + filt] = filt_ref[...]
+    mesh_sum_kernel(bulk_ref, out_ref.at[:base])
+    out_ref[base : base + size] = add_low(*(ref[:size] for ref in sent))
+    out_ref[base + size : base + size + filt] = filt_ref[...]
     gains = [ref[size:].astype(f32) for ref in sent]
     gains = tree_sum([gain[:2] + gain[2:4] for gain in gains])
     high, low = split_gain(gains)
     zeros = jnp.zeros((4, gains.shape[1]), f32)
-    out_ref[size + filt :] = jnp.concatenate([high.astype(f32), low.astype(f32), zeros], axis=0).astype(bf16)
+    out_ref[base + size + filt :] = jnp.concatenate(
+        [high.astype(f32), low.astype(f32), zeros], axis=0
+    ).astype(bf16)
 
 
 def slice_at(here, slot, rows):
@@ -1076,37 +1078,30 @@
     return pl.ds(pl.multiple_of(start, 8), rows)
 
 
-def unpack_bulk_kernel(here_ref, *refs, hidden, rows):
-    pieces, (up_ref, down_ref, two_ref, out_ref, turned) = refs[:8], refs[8:]
+def unpack_kernel(here_ref, *refs, hidden, rows):
+    pieces, (up_ref, down_ref, out_ref, in_ref, kernel_ref, gains_ref, turned, gains) = refs[:8], refs[8:]
     here = here_ref[0]
-    size = hidden + rows
+    width = in_ref.shape[2]
+    taps = kernel_ref.shape[1]
+    parts = -(-taps // width)
     for slot, ref in enumerate(pieces):
         at = slice_at(here, slot, hidden)
         turned[at, :] = ref[:hidden].astype(f32)
-        down_ref[at, :] = ref[size : size + hidden].astype(f32)
+        start = hidden + rows
+        down_ref[at, :] = ref[start : start + hidden].astype(f32)
         at = slice_at(here, slot, rows)
-        out_ref[at, :] = ref[hidden:size].astype(f32)
-        two_ref[at, :] = ref[size + hidden :].astype(f32)
-    up_ref[...] = turned[...].T
-
-
-def unpack_rest_kernel(here_ref, *refs, rows):
-    pieces, (two_ref, in_ref, kernel_ref, gains_ref, gains) = refs[:8], refs[8:]
-    width = in_ref.shape[2]
-    taps = kernel_ref.shape[1]
-    in_ref[2] = two_ref[...]
-    for slot, ref in enumerate(pieces):
-        at = slice_at(here_ref[0], slot, rows)
-        in_ref[0, at, :] = ref[:rows].astype(f32)
-        in_ref[1, at, :] = ref[rows : 2 * rows].astype(f32)
-        parts = -(-taps // width)
+        out_ref[at, :] = ref[hidden : hidden + rows].astype(f32)
+        start = 2 * hidden + rows
+        for place, gate in enumerate((2, 0, 1)):
+            in_ref[gate, at, :] = ref[start + place * rows : start + (place + 1) * rows].astype(f32)
         for part in range(parts):
             size = min(width, taps - part * width)
-            block = ref[(2 + part) * rows : (3 + part) * rows].astype(f32)
+            block = ref[start + (3 + part) * rows : start + (4 + part) * rows].astype(f32)
             kernel_ref[at, part * width : part * width + size] = block[:, :size]
-        gain = ref[(2 + parts) * rows :].astype(f32)
-        gains[relative_index(here_ref[0], slot, 8)] = gain[:2] + gain[2:4]
+        gain = ref[start + (3 + parts) * rows :].astype(f32)
+        gains[relative_index(here, slot, 8)] = gain[:2] + gain[2:4]
     gains_ref[...] = sum(gains[slot] for slot in range(8))
+    up_ref[...] = turned[...].T
 
 
 def chips_of(x, done=()):
@@ -1119,6 +1114,12 @@
 
 def levels_of(pieces):
     return [pieces[0]] + [swap(pieces[i], "mp", i) for i in range(1, len(pieces))]
+
+
+def stacked(*parts):
+    shape = (len(parts),) + parts[0].shape
+    (out,) = whole_call(stack_kernel, [(shape, bf16)], name="mixer_group", count=len(parts))(*parts)
+    return out.reshape(-1, shape[-1])
 
 
 def pair_of(pieces, done=()):
@@ -1154,25 +1155,31 @@
 
     own_in = lax.dynamic_slice_in_dim(input_weight.transpose(1, 2, 0), here * rows, rows, 1)
     own_out = lax.dynamic_slice_in_dim(output_weight, here * rows, rows, 0)
-    own_mixer = jnp.concatenate([own_in, own_out[None]])
-    mixer_rows = turn(jnp.broadcast_to(own_mixer, (mesh_rows,) + own_mixer.shape))
+    own_mixer = jnp.concatenate([own_in, own_out[None]]).reshape(-1, width)
+    next_mixer = swap(own_mixer, "mp", 1)
     own_up = lax.dynamic_slice_in_dim(up_weight, here * hidden, hidden, 1).T
     own_down = lax.dynamic_slice_in_dim(down_weight, here * hidden, hidden, 0)
     own_feed = jnp.stack([own_up, own_down])
     own_feed = jnp.broadcast_to(own_feed, (mesh_rows,) + own_feed.shape)
+    other_mixers = [swap(after(own_mixer, next_mixer), "mp", i) for i in range(2, mesh_rows)]
     fspec = filter_slices(place, kernel, pad_len, tables, length, ways)
-    feed_rows = turn(after(own_feed, mixer_rows))
-    mixer = chips_of(after(mixer_rows, own_feed).reshape(-1, width), done=(fspec,))
-    feed_rows = after(feed_rows, *mixer[1:])
-    up, down = (feed_rows[:, side].reshape(-1, width) for side in range(2))
-    up_x, down_y = swap(up, "dp", 2), swap(down, "dp", 4)
-    mixer = [far(piece) for piece in pair_of(mixer)]
-
-    outs = project(level, x, gain_first, mixer, mesh_rows)
-    mixed_in, (value, gate_one, gate_two, weight_out, normed_low) = outs[:mesh_rows], outs[mesh_rows:]
+    (normed_low,) = whole_call(
+        first_norm_forward_kernel, [((spots, width), bf16)], name="first_norm", count=2, room=10
+    )(x, gain_first[None])
+    first_group = chips_of(stacked(own_mixer, next_mixer))
+    other_mixers = [after(part, *first_group[1:], fspec, normed_low) for part in other_mixers]
+    second_group = chips_of(stacked(*other_mixers))
+    feed_rows = turn(after(own_feed, *other_mixers))
+    mixer = [[far(piece) for piece in pair_of(group)] for group in (first_group, second_group)]
+
+    outs = project(level, normed_low, mixer, mesh_rows)
+    mixed_in, (value, gate_one, gate_two, weight_out) = outs[:mesh_rows], outs[mesh_rows:]
     value, gate_one, gate_two = (part.reshape(channels, spots) for part in (value, gate_one, gate_two))
     weight_out = weight_out.reshape(channels, width)
     received = levels_of([part.reshape(own_channels, spots) for part in mixed_in])
+    feed_rows = after(feed_rows, value)
+    up, down = (feed_rows[:, side].reshape(-1, width) for side in range(2))
+    up_x, down_y = swap(up, "dp", 2), swap(down, "dp", 4)
     up_x, down_y = after(up_x, *received[1:]), after(down_y, *received[1:])
     quarter = ((2, mesh_rows * hidden, width), bf16)
     up_pair, down_pair = whole_call(stack_kernel, [quarter] * 2, name="feed_pairs", count=4, room=8)(
@@ -1198,44 +1205,36 @@
         channels,
     )
     mixer_low, block_out, grad_mid, mid_low, gain_second_grad, grad_two = outs[:6]
-    grad_conv, (up_near, up_far, down_near, down_far) = outs[6 : 6 + mesh_rows], outs[6 + mesh_rows :]
+    grad_conv, (up_near, down_near, far_grads) = outs[6 : 6 + mesh_rows], outs[6 + mesh_rows :]
     received = levels_of(grad_conv)
     late_shape = ((4, 2 * mesh_rows * rows, width), bf16)
     late_near, late_far = whole_call(
         partial(late_kernel, **sizes), [late_shape] * 2, [((channels, width), f32)], name="late_grads", count=4
-    )(grad_two, normed_low, mixer_low, mid_low)
+    )(far(grad_two), far(normed_low), mixer_low, mid_low)
     half = ((2, mesh_rows, hidden + rows, width), bf16)
     up_keep, up_send, down_keep, down_send = whole_call(
-        partial(kept_kernel, hidden=hidden, **sizes), [half] * 4, name="kept", count=6, room=20
-    )(
-        up_near,
-        swap(up_far, "dp", 1, received[1:]),
-        down_near,
-        swap(down_far, "dp", 1, received[1:]),
-        late_near,
-        swap(late_far, "dp", 1, received[1:]),
-    )
+        partial(kept_kernel, hidden=hidden, **sizes), [pltpu.HBM(*half), half] * 2, name="kept", count=5, room=20
+    )(up_near, down_near, swap(far_grads, "dp", 1), late_near, swap(late_far, "dp", 1))
     up_in, down_in = swap(up_send, "dp", 2), swap(down_send, "dp", 4)
 
-    outs = conv_mixed(level, received, fspec, tables)
-    mixed_out, gspec = outs[:mesh_rows], outs[mesh_rows]
-    mixed = levels_of(mixed_out)
+    received = [received[0]] + [after(piece, up_keep) for piece in received[1:]]
+    mixed_out, gspec = conv_mixed(level, received, fspec, tables)
+    mixed = turn(mixed_out).reshape(channels, spots)
     filt_grad = conv_filt(gspec, uspec, tables, taps, width, length)
     quarter = (half[0][1:], bf16)
     up_keep, up_send, down_keep, down_send = whole_call(
-        pair_kernel, [quarter] * 4, name="kept_again", count=4, room=12
-    )(up_keep, after(up_in, *mixed[1:]), down_keep, after(down_in, *mixed[1:]))
+        pair_kernel, [pltpu.HBM(*quarter), quarter] * 2, name="kept_again", count=4, room=12
+    )(up_keep, after(up_in, mixed_out), down_keep, after(down_in, mixed_out))
     up_in, down_in = swap(up_send, "dp", 4), swap(down_send, "dp", 2)
     rest_rows = (2 * mesh_rows + filt_parts) * rows
     rest_near, rest_far, grad_value, grad_one = whole_call(
         partial(rest_kernel, **sizes),
-        [((4, rest_rows, width), bf16)] * 2 + [pltpu.HBM(*tall)] * 2,
+        [pltpu.HBM((4, rest_rows, width), bf16), ((4, rest_rows, width), bf16)] + [pltpu.HBM(*tall)] * 2,
         [((channels, width), f32)],
         name="rest_grads",
-        smem=1,
-        count=mesh_rows + 4,
+        count=5,
         room=12,
-    )(level, *mixed, value, gate_one, normed_low, filt_grad)
+    )(mixed, far(value), far(gate_one), far(normed_low), filt_grad)
     rest = whole_call(split_kernel, [((rest_rows, width), bf16)] * 4, name="rest_kept", count=2)(
         rest_near, swap(rest_far, "dp", 1)
     )
@@ -1249,9 +1248,18 @@
         [wide, ((1, width), f32)],
         [((4 * mesh_rows * rows, spots), bf16), wide],
         name="first_norm_back",
-        count=14,
+        smem=1,
+        count=22,
         room=20,
-    )(far(grad_value), far(grad_one), far(grad_two), *mixer, far(x), gain_first[None], far(grad_mid))
+    )(
+        level,
+        *(far(part.reshape(mesh_rows, own_channels, spots)) for part in (grad_value, grad_one, grad_two)),
+        *mixer[0],
+        *mixer[1],
+        far(x),
+        gain_first[None],
+        far(grad_mid),
+    )
     rest = [rest[0]] + [after(piece, grad_tokens) for piece in rest[1:]]
     own_filt, *rest = whole_call(
         partial(rest_sum_kernel, rows=rows),
@@ -1261,35 +1269,29 @@
         count=8,
     )(place, level, *rest, kernel, pad_len[:, None], gain_first_grad, gain_second_grad)
     rest = levels_of(rest)
-    (bulk,) = whole_call(mesh_sum_kernel, [(bulk.shape[1:], bf16)], name="bulk_mesh_sum", count=1)(
-        after(bulk, *rest[1:])
-    )
-    bulk = chips_of(bulk)
-    (rest,) = whole_call(
-        rest_mesh_sum_kernel, [(((2 + filt_parts) * rows + 8, width), bf16)], name="rest_mesh_sum", count=1 + mesh_rows
-    )(own_filt, *rest)
-    rest = chips_of(rest)
-    bulk = pair_of(bulk)
-    rest = pair_of(rest)
-    channel_rows = ((own_channels, width), f32)
-    up_grad, down_grad, two_grad, out_grad = whole_call(
-        partial(unpack_bulk_kernel, hidden=hidden, rows=rows),
-        [(up_weight.shape, f32), (down_weight.shape, f32), channel_rows, channel_rows],
-        [(down_weight.shape, f32)],
-        name="unpack_bulk",
+    (mine,) = whole_call(
+        rest_mesh_sum_kernel,
+        [((bulk.shape[1] + (2 + filt_parts) * rows + 8, width), bf16)],
+        name="mesh_sum",
+        count=2 + mesh_rows,
+        room=8,
+    )(after(bulk, *rest[1:]), own_filt, *rest)
+    up_grad, down_grad, out_grad, in_grad, kernel_grad, gains = whole_call(
+        partial(unpack_kernel, hidden=hidden, rows=rows),
+        [
+            (up_weight.shape, f32),
+            (down_weight.shape, f32),
+            ((own_channels, width), f32),
+            ((3, own_channels, width), f32),
+            (kernel.shape, f32),
+            ((2, width), f32),
+        ],
+        [(down_weight.shape, f32), ((8, 2, width), f32)],
+        name="unpack",
         smem=1,
         count=8,
-        room=14,
-    )(place, *bulk)
-    in_grad, kernel_grad, gains = whole_call(
-        partial(unpack_rest_kernel, rows=rows),
-        [((3, own_channels, width), f32), (kernel.shape, f32), ((2, width), f32)],
-        [((8, 2, width), f32)],
-        name="unpack_rest",
-        smem=1,
-        count=9,
-        room=8,
-    )(place, *rest, two_grad)
+        room=24,
+    )(place, *pair_of(chips_of(mine)))
     return (
         block_out[None],
         grad_tokens[None],

time: 325 us -> 308 us (0.948)
  waiting for transfers between devices: 158 us -> 126 us
  Pallas kernels: 79.5 us -> 94 us
  starting transfers between devices: 70 us -> 64.9 us
  local copies, waits for them, and re-layouts: 13.2 us -> 17 us
    ppermute x57 -> x56, waiting for transfers between devices: 144 us -> 118 us  [swap(): lax.ppermute(x, axis, [(i, i ^ bit) for i in range(lax.axis_size(axis))])]
    pallas_call x7 -> x8, Pallas kernels: 9.46 us -> 20.1 us  [the longest x1 4.77 us: fast_body(): whole_call(partial(rest_kernel, **sizes), [pltpu.HBM((4, rest_rows, width...]
    all_to_all x3, waiting for transfers between devices: 14.8 us -> 7.56 us  [turn(): return lax.all_to_all(x, 'mp', 0, 0)]
    unnamed x43 -> x65, local copies, waits for them, and re-layouts: 5.37 us -> 10.3 us
    all_to_all x3, starting transfers between devices: 17.3 us -> 12.6 us  [turn(): return lax.all_to_all(x, 'mp', 0, 0)]
    ppermute x57 -> x56, starting transfers between devices: 52.7 us -> 52.3 us  [swap(): lax.ppermute(x, axis, [(i, i ^ bit) for i in range(lax.axis_size(axis))])]
  transfers between devices with their start and end apart: 60 -> 59, of which waited for: 28 -> 27; matrix products, arithmetic and copies ran while one was open for 2% -> 2% of each run, Pallas kernels for 13% -> 17%
where the time goes in v1:
time: 308 us; the launch traced here: 307 us
  waiting for transfers between devices  126 us (41%)
  Pallas kernels  94 us (31%)
  starting transfers between devices  64.9 us (21%)
  local copies, waits for them, and re-layouts  17 us (6%)
  other arithmetic  4.41 us (1%)
    ppermute x56, waiting for transfers between devices, swap(): lax.ppermute(x, axis, [(i, i ^ bit) for i in range(lax.axis_size(axis))])  118 us
    ppermute x56, starting transfers between devices, swap(): lax.ppermute(x, axis, [(i, i ^ bit) for i in range(lax.axis_size(axis))])  52.3 us
    pallas_call x1, Pallas kernels, feed_forward(): pl.pallas_call(partial(feed_kernel, mesh_rows=mesh_rows), grid=(8,), in_s...  28.9 us
    all_to_all x3, starting transfers between devices, turn(): return lax.all_to_all(x, 'mp', 0, 0)  12.6 us
    unnamed x65, local copies, waits for them, and re-layouts  10.3 us
    pallas_call x1, Pallas kernels, fast_body(): whole_call(partial(first_norm_kernel, **sizes), [wide, ((1, width), f32)]...  9.11 us
    all_to_all x3, waiting for transfers between devices, turn(): return lax.all_to_all(x, 'mp', 0, 0)  7.56 us
    pallas_call x1, Pallas kernels, filter_slices(): whole_call(partial(filter_slices_kernel, radix=radix, channels=channels,...  6.76 us
  transfers between devices with their start and end apart: 59, of which 27 were waited for; matrix products, arithmetic and copies ran while one was open for 2% of the time, Pallas kernels for 17%

profile of v1, /device:TPU:0, one launch (start us, length us, event | category | flops | bytes accessed | tf_op | source)
XLA Modules:
  0.0 307.4 jit_solution(9636633153846762418)
XLA Ops:
  14.8 3.8 %collective-permute-start.9 = (bf16[96,768]{1,0:T(8,128)(2,1)}, bf16[96,768]{1,0:T(8,128)(2,1)}, u32[]{:S(2)}, u32[]{:S(2)}) collective-permute-start(bf16[96,768]{1,0:T(8,128)(2,1)} %bitcast.4.refs_0_), channel_id=1, source_target_pairs={{0,3},{1,2},{2,1},{3,0},{4,7},{5,6},{6,5},{7,4},{8,11},{9,10},{10,... | collective-permute-start | bytes 442376 | tf_op jit(solution)/shard_map/ppermute | solution.py:367
  22.6 6.8 %filter_spectrum.1.refs_4_ = f32[1536,512]{1,0:T(8,128)S(1)} custom-call(s32[1]{0:T(128)} %bitcast.6.here_ref, f32[192,2048]{1,0:T(8,128)} %kernel_ref.3, s32[192,1]{1,0:T(8,128)S(1)} %copy.26.pad_ref, bf16[512,512]{1,0:T(8,128)(2,1)} %fusion.high_ref.refs_5_, bf16[512,512]{1,0:T(8,128)(2,1)} %subtract_convert_fusion.low_ref, ...), custom_call_target="tpu_custom_call" | custom-call | tf_op jit(solution)/shard_map/filter_spectrum/pallas_call | solution.py:706
  30.8 4.5 %all-to-all-start = ((bf16[4,2,96,768]{3,2,1,0:T(8,128)(2,1)}), bf16[4,2,96,768]{3,2,1,0:T(8,128)(2,1)}, u32[]{:S(2)}, u32[]{:S(2)}) async-start(bf16[4,2,96,768]{3,2,1,0:T(8,128)(2,1)} %broadcast_in_dim.39), calls=%async_computation | async-start | bytes 2359296 | tf_op jit(solution)/shard_map/all_to_all | solution.py:436
  42.4 6.3 %collective-permute-done.12.refs_11_.refs_14_ = bf16[192,768]{1,0:T(8,128)(2,1)} collective-permute-done((bf16[192,768]{1,0:T(8,128)(2,1)}, bf16[192,768]{1,0:T(8,128)(2,1)}, u32[]{:S(2)}, u32[]{:S(2)}) %collective-permute-start.12) | collective-permute-done | bytes 294944 | tf_op jit(solution)/shard_map/ppermute | solution.py:367
  48.8 5.8 %collective-permute-done.11.refs_10_.refs_13_ = bf16[192,768]{1,0:T(8,128)(2,1)} collective-permute-done((bf16[192,768]{1,0:T(8,128)(2,1)}, bf16[192,768]{1,0:T(8,128)(2,1)}, u32[]{:S(2)}, u32[]{:S(2)}) %collective-permute-start.11) | collective-permute-done | bytes 294944 | tf_op jit(solution)/shard_map/ppermute | solution.py:367
  57.8 6.7 %project.1 = (bf16[2,4,24,512]{3,2,1,0:T(8,128)(2,1)}, bf16[2,4,24,512]{3,2,1,0:T(8,128)(2,1)}, bf16[2,4,24,512]{3,2,1,0:T(8,128)(2,1)}, bf16[2,4,24,512]{3,2,1,...) custom-call(s32[1]{0:T(128)} %bitcast.level_ref.here_ref.refs_0_, ...), custom_call_target="tpu_custom_call" | custom-call | tf_op jit(solution)/shard_map/project/pallas_call | solution.py:769
  72.7 5.1 %collective-permute-done.17.refs_1_ = bf16[192,512]{1,0:T(8,128)(2,1)S(1)} collective-permute-done((bf16[192,512]{1,0:T(8,128)(2,1)S(1)}, bf16[192,512]{1,0:T(8,128)(2,1)S(1)}, u32[]{:S(2)}, u32[]{:S(2)}) %collective-permute-start.17) | collective-permute-done | bytes 196640 | tf_op jit(solution)/shard_map/ppermute | solution.py:367
  77.9 9.4 %collective-permute-done.18.refs_2_ = bf16[192,512]{1,0:T(8,128)(2,1)S(1)} collective-permute-done((bf16[192,512]{1,0:T(8,128)(2,1)S(1)}, bf16[192,512]{1,0:T(8,128)(2,1)S(1)}, u32[]{:S(2)}, u32[]{:S(2)}) %collective-permute-start.18) | collective-permute-done | bytes 196640 | tf_op jit(solution)/shard_map/ppermute | solution.py:367
  89.2 6.3 %conv_forward.1 = (bf16[192,512]{1,0:T(8,128)(2,1)S(1)}, bf16[192,512]{1,0:T(8,128)(2,1)S(1)}, bf16[192,512]{1,0:T(8,128)(2,1)S(1)}, bf16[192,512]{1,0:T(8,128)(2,1)S(1)}, bf16[1536,512]{1,0:T(8,128)(2,1)}) custom-call(s32[1]{0:T(128)} %bitcast.level_ref.here_ref.refs_0_, bf16[192,512]{1,0:T(8,128)(2,1)S(1)} %bitcast.52, ...), custom_call_target="tpu_custom_call" | custom-call | tf_op jit(solution)/shard_map/conv_forward/pallas_call | solution.py:273
  95.5 3.1 %collective-permute-start.20 = (bf16[192,512]{1,0:T(8,128)(2,1)S(1)}, bf16[192,512]{1,0:T(8,128)(2,1)S(1)}, u32[]{:S(2)}, u32[]{:S(2)}) collective-permute-start(bf16[192,512]{1,0:T(8,128)(2,1)S(1)} %get-tuple-element.100), channel_id=1, source_target_pairs={{0,1},{1,0},{2,3},{3,2},{4,5},{5,4},{6,7},{7,6},{8,9},{9,8},{10,11... | collective-permute-start | bytes 589832 | tf_op jit(solution)/shard_map/ppermute | solution.py:367
  101.0 3.1 %collective-permute-done.20.refs_7_ = bf16[192,512]{1,0:T(8,128)(2,1)S(1)} collective-permute-done((bf16[192,512]{1,0:T(8,128)(2,1)S(1)}, bf16[192,512]{1,0:T(8,128)(2,1)S(1)}, u32[]{:S(2)}, u32[]{:S(2)}) %collective-permute-start.20) | collective-permute-done | bytes 196640 | tf_op jit(solution)/shard_map/ppermute | solution.py:367
  104.1 10.3 %collective-permute-done.21.refs_8_ = bf16[192,512]{1,0:T(8,128)(2,1)S(1)} collective-permute-done((bf16[192,512]{1,0:T(8,128)(2,1)S(1)}, bf16[192,512]{1,0:T(8,128)(2,1)S(1)}, u32[]{:S(2)}, u32[]{:S(2)}) %collective-permute-start.21) | collective-permute-done | bytes 196640 | tf_op jit(solution)/shard_map/ppermute | solution.py:367
  115.6 4.3 %collective-permute-done.31.refs_20_ = bf16[384,768]{1,0:T(8,128)(2,1)S(1)} collective-permute-done((bf16[384,768]{1,0:T(8,128)(2,1)S(1)}, bf16[384,768]{1,0:T(8,128)(2,1)S(1)}, u32[]{:S(2)}, u32[]{:S(2)}) %collective-permute-start.31) | collective-permute-done | bytes 589856 | tf_op jit(solution)/shard_map/ppermute | solution.py:367
  122.6 28.9 %feed_forward.1 = (bf16[768,512]{1,0:T(8,128)(2,1)S(1)}, bf16[512,768]{1,0:T(8,128)(2,1)}, f32[512,768]{1,0:T(8,128)}, bf16[512,768]{1,0:T(8,128)(2,1)S(1)}, f32...) custom-call(s32[1]{0:T(128)} %bitcast.level_ref.here_ref.refs_0_, ...), custom_call_target="tpu_custom_call" | custom-call | tf_op jit(solution)/shard_map/feed_forward/pallas_call | solution.py:884
  155.0 6.1 %collective-permute-done.35.late_in = bf16[4,192,768]{2,1,0:T(8,128)(2,1)S(1)} collective-permute-done((bf16[4,192,768]{2,1,0:T(8,128)(2,1)S(1)}, bf16[4,192,768]{2,1,0:T(8,128)(2,1)S(1)}, u32[]{:S(2)}, u32[]{:S(2)}) %collective-permute-start.35) | collective-permute-done | bytes 1179680 | tf_op jit(solution)/shard_map/ppermute | solution.py:367
  162.8 3.9 %kept.1 = (bf16[2,4,120,768]{3,2,1,0:T(8,128)(2,1)}, bf16[2,4,120,768]{3,2,1,0:T(8,128)(2,1)}, bf16[2,4,120,768]{3,2,1,0:T(8,128)(2,1)}, bf16[2,4,120,768]{3,2,1,0:T(8,128)(2,1)}) custom-call(bf16[1536,768]{1,0:T(8,128)(2,1)S(1)} %copy-done.9, bf16[1536,768]{1,0:T(8,128)(2,1)S(1)} %copy-done.10, bf16[2,1536,768]{2,1,0:T(8,128)(2,1)S(1)} %collective-permute-done.34.far_in, ...), custom_call_target="tpu_custom_call" | custom-call | tf_op jit(solution)/shard_map/kept/pallas_call | solution.py:1215
  173.4 5.3 %collective-permute-done.37.refs_3_ = bf16[192,512]{1,0:T(8,128)(2,1)S(1)} collective-permute-done((bf16[192,512]{1,0:T(8,128)(2,1)S(1)}, bf16[192,512]{1,0:T(8,128)(2,1)S(1)}, u32[]{:S(2)}, u32[]{:S(2)}) %collective-permute-start.37) | collective-permute-done | bytes 196640 | tf_op jit(solution)/shard_map/ppermute | solution.py:367
  178.7 11.1 %collective-permute-done.36.refs_2_ = bf16[192,512]{1,0:T(8,128)(2,1)S(1)} collective-permute-done((bf16[192,512]{1,0:T(8,128)(2,1)S(1)}, bf16[192,512]{1,0:T(8,128)(2,1)S(1)}, u32[]{:S(2)}, u32[]{:S(2)}) %collective-permute-start.36) | collective-permute-done | bytes 196640 | tf_op jit(solution)/shard_map/ppermute | solution.py:367
  189.8 6.4 %conv_mixed.1 = (bf16[4,192,512]{2,1,0:T(8,128)(2,1)}, bf16[1536,512]{1,0:T(8,128)(2,1)}) custom-call(s32[1]{0:T(128)} %bitcast.level_ref.here_ref.refs_0_, bf16[192,512]{1,0:T(8,128)(2,1)S(1)} %get-tuple-element.113.refs_0_, bf16[192,512]{1,0:T(8,128)(2,1)S(1)} %collective-permute-done.33.refs_1_, bf16[192,512]{1,0:T(8,128)(2,1)S(1)} %collective-permute-done.36.refs_2_, ...), custom_call_target="tpu_custom_call" | custom-call | tf_op jit(solution)/shard_map/conv_mixed/pallas_call | solution.py:292
  196.2 3.6 %all-to-all-start.1 = ((bf16[4,192,512]{2,1,0:T(8,128)(2,1)}), bf16[4,192,512]{2,1,0:T(8,128)(2,1)S(1)}, u32[]{:S(2)}, u32[]{:S(2)}) async-start(bf16[4,192,512]{2,1,0:T(8,128)(2,1)} %get-tuple-element.129), calls=%async_computation.1 | async-start | bytes 1572864 | tf_op jit(solution)/shard_map/all_to_all | solution.py:436
  203.9 3.8 %kept_again.1 = (bf16[4,120,768]{2,1,0:T(8,128)(2,1)}, bf16[4,120,768]{2,1,0:T(8,128)(2,1)}, bf16[4,120,768]{2,1,0:T(8,128)(2,1)}, bf16[4,120,768]{2,1,0:T(8,128)(2,1)}) custom-call(bf16[2,4,120,768]{3,2,1,0:T(8,128)(2,1)S(1)} %copy-done.14, bf16[2,4,120,768]{3,2,1,0:T(8,128)(2,1)} %collective-permute-done.38.up_in, bf16[2,4,120,768]{3,2,1,0:T(8,128)(2,1)S(1)} %copy-done.15, ...), custom_call_target="tpu_custom_call" | custom-call | tf_op jit(solution)/shard_map/kept_again/pallas_call | solution.py:1225
  212.8 7.6 %all-to-all-done.1 = bf16[4,192,512]{2,1,0:T(8,128)(2,1)S(1)} async-done(((bf16[4,192,512]{2,1,0:T(8,128)(2,1)}), bf16[4,192,512]{2,1,0:T(8,128)(2,1)S(1)}, u32[]{:S(2)}, u32[]{:S(2)}) %all-to-all-start.1) | async-done | bytes 786464 | tf_op jit(solution)/shard_map/all_to_all | solution.py:436
  220.4 4.8 %rest_grads.1 = (bf16[4,264,768]{2,1,0:T(8,128)(2,1)}, bf16[4,264,768]{2,1,0:T(8,128)(2,1)S(1)}, bf16[768,512]{1,0:T(8,128)(2,1)}, bf16[768,512]{1,0:T(8,128)(2,1)}) custom-call(bf16[768,512]{1,0:T(8,128)(2,1)S(1)} %bitcast.45, f32[768,512]{1,0:T(8,128)} %bitcast.55, f32[768,512]{1,0:T(8,128)} %bitcast.56, bf16[512,768]{1,0:T(8,128)(2,1)} %copy-done.4, ...), custom_call_target="tpu_custom_call" | custom-call | tf_op jit(solution)/shard_map/rest_grads/pallas_call | solution.py:1230
  229.1 4.6 %all-to-all-start.2 = ((bf16[4,240,768]{2,1,0:T(8,128)(2,1)}), bf16[4,240,768]{2,1,0:T(8,128)(2,1)S(1)}, u32[]{:S(2)}, u32[]{:S(2)}) async-start(bf16[4,240,768]{2,1,0:T(8,128)(2,1)} %bulk_sum.1), calls=%async_computation.2 | async-start | bytes 2949120 | tf_op jit(solution)/shard_map/all_to_all | solution.py:436
  233.7 3.7 %collective-permute-done.42.far_ref = bf16[4,264,768]{2,1,0:T(8,128)(2,1)S(1)} collective-permute-done((bf16[4,264,768]{2,1,0:T(8,128)(2,1)}, bf16[4,264,768]{2,1,0:T(8,128)(2,1)S(1)}, u32[]{:S(2)}, u32[]{:S(2)}) %collective-permute-start.42) | collective-permute-done | bytes 1622048 | tf_op jit(solution)/shard_map/ppermute | solution.py:367
  242.7 9.1 %first_norm_back.1 = (f32[512,768]{1,0:T(8,128)}, f32[1,768]{1,0:T(1,128)S(1)}) custom-call(s32[1]{0:T(128)} %bitcast.level_ref.here_ref.refs_0_, bf16[4,192,512]{2,1,0:T(8,128)(2,1)} %bitcast.59, bf16[4,192,512]{2,1,0:T(8,128)(2,1)} %bitcast.60, bf16[4,192,512]{2,1,0:T(8,128)(2,1)} %bitcast.53, bf16[192,768]{1,0:T(8,128)(2,1)} %bitcast.51, ...), custom_call_target="tpu_custom_call" | custom-call | tf_op jit(solution)/shard_map/first_norm_back/pallas_call | solution.py:1246
  251.9 8.4 %collective-permute-done.44.p2 = bf16[264,768]{1,0:T(8,128)(2,1)S(1)} collective-permute-done((bf16[264,768]{1,0:T(8,128)(2,1)S(1)}, bf16[264,768]{1,0:T(8,128)(2,1)S(1)}, u32[]{:S(2)}, u32[]{:S(2)}) %collective-permute-start.44) | collective-permute-done | bytes 405536 | tf_op jit(solution)/shard_map/ppermute | solution.py:367
  265.2 3.8 %collective-permute-done.46.refs_1_ = bf16[56,768]{1,0:T(8,128)(2,1)S(1)} collective-permute-done((bf16[56,768]{1,0:T(8,128)(2,1)S(1)}, bf16[56,768]{1,0:T(8,128)(2,1)S(1)}, u32[]{:S(2)}, u32[]{:S(2)}) %collective-permute-start.46) | collective-permute-done | bytes 86048 | tf_op jit(solution)/shard_map/ppermute | solution.py:367
  269.0 4.6 %collective-permute-done.47.refs_2_ = bf16[56,768]{1,0:T(8,128)(2,1)S(1)} collective-permute-done((bf16[56,768]{1,0:T(8,128)(2,1)S(1)}, bf16[56,768]{1,0:T(8,128)(2,1)S(1)}, u32[]{:S(2)}, u32[]{:S(2)}) %collective-permute-start.47) | collective-permute-done | bytes 86048 | tf_op jit(solution)/shard_map/ppermute | solution.py:367
  277.5 13.1 %collective-permute-done.51.refs_3_ = bf16[368,768]{1,0:T(8,128)(2,1)S(1)} collective-permute-done((bf16[368,768]{1,0:T(8,128)(2,1)S(1)}, bf16[368,768]{1,0:T(8,128)(2,1)S(1)}, u32[]{:S(2)}, u32[]{:S(2)}) %collective-permute-start.51) | collective-permute-done | bytes 565280 | tf_op jit(solution)/shard_map/ppermute | solution.py:367
  290.6 9.0 %collective-permute-done.50.refs_2_ = bf16[368,768]{1,0:T(8,128)(2,1)S(1)} collective-permute-done((bf16[368,768]{1,0:T(8,128)(2,1)S(1)}, bf16[368,768]{1,0:T(8,128)(2,1)S(1)}, u32[]{:S(2)}, u32[]{:S(2)}) %collective-permute-start.50) | collective-permute-done | bytes 565280 | tf_op jit(solution)/shard_map/ppermute | solution.py:367
  302.4 4.4 %unpack.1 = (f32[768,768]{1,0:T(8,128)}, f32[768,768]{1,0:T(8,128)}, f32[192,768]{1,0:T(8,128)}, f32[3,192,768]{2,1,0:T(8,128)}, f32[192,2048]{1,0:T(8,128)}, /*index=5*/f32[2,768]{1,0:T(2,128)S(1)}) custom-call(s32[1]{0:T(128)} %bitcast.6.here_ref, bf16[368,768]{1,0:T(8,128)(2,1)S(1)} %mesh_sum.1.refs_0_, ...), custom_call_target="tpu_custom_call" | custom-call | tf_op jit(solution)/shard_map/unpack/pallas_call | solution.py:1279
  (187 shorter events, 88.7 us)
Async XLA Ops:
  11.1 18.3 %collective-permute-start.3 = (bf16[192,768]{1,0:T(8,128)(2,1)S(1)}, bf16[192,768]{1,0:T(8,128)(2,1)}, u32[]{:S(2)}, u32[]{:S(2)}) collective-permute-start(bf16[192,768]{1,0:T(8,128)(2,1)S(1)} %bitcast.46), channel_id=1, source_target_pairs={{0,24},{4,28},{8,16},{12,20},{16,8},{20,12},{24,0},{28,4},{1,25},{... | collective-permute-start | bytes 884744 | tf_op jit(solution)/shard_map/ppermute | solution.py:367
  13.8 15.6 %collective-permute-start.2 = (bf16[192,768]{1,0:T(8,128)(2,1)S(1)}, bf16[192,768]{1,0:T(8,128)(2,1)}, u32[]{:S(2)}, u32[]{:S(2)}) collective-permute-start(bf16[192,768]{1,0:T(8,128)(2,1)S(1)} %bitcast.47), channel_id=1, source_target_pairs={{0,16},{4,20},{8,24},{12,28},{16,0},{20,4},{24,8},{28,12},{1,17},{... | collective-permute-start | bytes 884744 | tf_op jit(solution)/shard_map/ppermute | solution.py:367
  14.3 15.1 %collective-permute-start.1 = (bf16[192,768]{1,0:T(8,128)(2,1)S(1)}, bf16[192,768]{1,0:T(8,128)(2,1)}, u32[]{:S(2)}, u32[]{:S(2)}) collective-permute-start(bf16[192,768]{1,0:T(8,128)(2,1)S(1)} %bitcast.48), channel_id=1, source_target_pairs={{0,8},{4,12},{8,0},{12,4},{16,24},{20,28},{24,16},{28,20},{1,9},{5... | collective-permute-start | bytes 884744 | tf_op jit(solution)/shard_map/ppermute | solution.py:367
  14.8 14.6 %collective-permute-start.9 = (bf16[96,768]{1,0:T(8,128)(2,1)}, bf16[96,768]{1,0:T(8,128)(2,1)}, u32[]{:S(2)}, u32[]{:S(2)}) collective-permute-start(bf16[96,768]{1,0:T(8,128)(2,1)} %bitcast.4.refs_0_), channel_id=1, source_target_pairs={{0,3},{1,2},{2,1},{3,0},{4,7},{5,6},{6,5},{7,4},{8,11},{9,10},{10,... | collective-permute-start | bytes 442376 | tf_op jit(solution)/shard_map/ppermute | solution.py:367
  30.8 33.7 %all-to-all-start = ((bf16[4,2,96,768]{3,2,1,0:T(8,128)(2,1)}), bf16[4,2,96,768]{3,2,1,0:T(8,128)(2,1)}, u32[]{:S(2)}, u32[]{:S(2)}) async-start(bf16[4,2,96,768]{3,2,1,0:T(8,128)(2,1)} %broadcast_in_dim.39), calls=%async_computation | async-start | bytes 2359296 | tf_op jit(solution)/shard_map/all_to_all | solution.py:436
  40.1 14.4 %collective-permute-start.11 = (bf16[192,768]{1,0:T(8,128)(2,1)}, bf16[192,768]{1,0:T(8,128)(2,1)}, u32[]{:S(2)}, u32[]{:S(2)}) collective-permute-start(bf16[192,768]{1,0:T(8,128)(2,1)} %bitcast.8.refs_8_.refs_11_), channel_id=1, source_target_pairs={{0,16},{4,20},{8,24},{12,28},{16,0},{20,4},{24,8},{28,12},{1,17},{... | collective-permute-start | bytes 884744 | tf_op jit(solution)/shard_map/ppermute | solution.py:367
  41.4 13.2 %collective-permute-start.10 = (bf16[192,768]{1,0:T(8,128)(2,1)}, bf16[192,768]{1,0:T(8,128)(2,1)S(1)}, u32[]{:S(2)}, u32[]{:S(2)}) collective-permute-start(bf16[192,768]{1,0:T(8,128)(2,1)} %bitcast.8.refs_8_.refs_11_), channel_id=1, source_target_pairs={{0,8},{4,12},{8,0},{12,4},{16,24},{20,28},{24,16},{28,20},{1,9},{5... | collective-permute-start | bytes 884744 | tf_op jit(solution)/shard_map/ppermute | solution.py:367
  41.9 13.2 %collective-permute-start.13 = (bf16[192,768]{1,0:T(8,128)(2,1)}, bf16[192,768]{1,0:T(8,128)(2,1)}, u32[]{:S(2)}, u32[]{:S(2)}) collective-permute-start(bf16[192,768]{1,0:T(8,128)(2,1)} %bitcast.8.refs_8_.refs_11_), channel_id=1, source_target_pairs={{0,4},{4,0},{8,12},{12,8},{16,20},{20,16},{24,28},{28,24},{1,5},{5... | collective-permute-start | bytes 884744 | tf_op jit(solution)/shard_map/ppermute | solution.py:367
  41.9 13.2 %collective-permute-start.5 = (bf16[192,768]{1,0:T(8,128)(2,1)}, bf16[192,768]{1,0:T(8,128)(2,1)}, u32[]{:S(2)}, u32[]{:S(2)}) collective-permute-start(bf16[192,768]{1,0:T(8,128)(2,1)} %collective-permute-done.1.refs_1_.refs_4_), channel_id=1, source_target_pairs={{0,4},{4,0},{8,12},{12,8},{16,20},{20,16},{24,28},{28,24},{1,5},{5... | collective-permute-start | bytes 884744 | tf_op jit(solution)/shard_map/ppermute | solution.py:367
  66.0 21.3 %collective-permute-start.23 = (bf16[384,768]{1,0:T(8,128)(2,1)S(1)}, bf16[384,768]{1,0:T(8,128)(2,1)S(1)}, u32[]{:S(2)}, u32[]{:S(2)}) collective-permute-start(bf16[384,768]{1,0:T(8,128)(2,1)S(1)} %bitcast.41), channel_id=1, source_target_pairs={{0,8},{4,12},{8,0},{12,4},{16,24},{20,28},{24,16},{28,20},{1,9},{5... | collective-permute-start | bytes 1769480 | tf_op jit(solution)/shard_map/ppermute | solution.py:367
  67.5 19.7 %collective-permute-start.24 = (bf16[384,768]{1,0:T(8,128)(2,1)S(1)}, bf16[384,768]{1,0:T(8,128)(2,1)S(1)}, u32[]{:S(2)}, u32[]{:S(2)}) collective-permute-start(bf16[384,768]{1,0:T(8,128)(2,1)S(1)} %bitcast.37), channel_id=1, source_target_pairs={{0,16},{4,20},{8,24},{12,28},{16,0},{20,4},{24,8},{28,12},{1,17},{... | collective-permute-start | bytes 1769480 | tf_op jit(solution)/shard_map/ppermute | solution.py:367
  70.1 17.2 %collective-permute-start.18 = (bf16[192,512]{1,0:T(8,128)(2,1)S(1)}, bf16[192,512]{1,0:T(8,128)(2,1)S(1)}, u32[]{:S(2)}, u32[]{:S(2)}) collective-permute-start(bf16[192,512]{1,0:T(8,128)(2,1)S(1)} %bitcast.67), channel_id=1, source_target_pairs={{0,2},{1,3},{2,0},{3,1},{4,6},{5,7},{6,4},{7,5},{8,10},{9,11},{10,... | collective-permute-start | bytes 589832 | tf_op jit(solution)/shard_map/ppermute | solution.py:367
  72.4 14.8 %collective-permute-start.19 = (bf16[192,512]{1,0:T(8,128)(2,1)S(1)}, bf16[192,512]{1,0:T(8,128)(2,1)S(1)}, u32[]{:S(2)}, u32[]{:S(2)}) collective-permute-start(bf16[192,512]{1,0:T(8,128)(2,1)S(1)} %bitcast.66), channel_id=1, source_target_pairs={{0,3},{1,2},{2,1},{3,0},{4,7},{5,6},{6,5},{7,4},{8,11},{9,10},{10,... | collective-permute-start | bytes 589832 | tf_op jit(solution)/shard_map/ppermute | solution.py:367
  87.4 27.0 %collective-permute-start.25 = (bf16[2,384,768]{2,1,0:T(8,128)(2,1)S(1)}, bf16[2,384,768]{2,1,0:T(8,128)(2,1)S(1)}, u32[]{:S(2)}, u32[]{:S(2)}) collective-permute-start(bf16[2,384,768]{2,1,0:T(8,128)(2,1)S(1)} %get-tuple-element.108), channel_id=1, source_target_pairs={{0,16},{4,20},{8,24},{12,28},{16,0},{20,4},{24,8},{28,12},{1,17},{... | collective-permute-start | bytes 3538952 | tf_op jit(solution)/shard_map/ppermute | solution.py:367
  88.7 25.8 %collective-permute-start.27 = (bf16[2,384,768]{2,1,0:T(8,128)(2,1)S(1)}, bf16[2,384,768]{2,1,0:T(8,128)(2,1)S(1)}, u32[]{:S(2)}, u32[]{:S(2)}) collective-permute-start(bf16[2,384,768]{2,1,0:T(8,128)(2,1)S(1)} %get-tuple-element.110), channel_id=1, source_target_pairs={{0,8},{4,12},{8,0},{12,4},{16,24},{20,28},{24,16},{28,20},{1,9},{5... | collective-permute-start | bytes 3538952 | tf_op jit(solution)/shard_map/ppermute | solution.py:367
  98.6 15.8 %collective-permute-start.21 = (bf16[192,512]{1,0:T(8,128)(2,1)S(1)}, bf16[192,512]{1,0:T(8,128)(2,1)S(1)}, u32[]{:S(2)}, u32[]{:S(2)}) collective-permute-start(bf16[192,512]{1,0:T(8,128)(2,1)S(1)} %get-tuple-element.101), channel_id=1, source_target_pairs={{0,2},{1,3},{2,0},{3,1},{4,6},{5,7},{6,4},{7,5},{8,10},{9,11},{10,... | collective-permute-start | bytes 589832 | tf_op jit(solution)/shard_map/ppermute | solution.py:367
  99.6 14.9 %collective-permute-start.22 = (bf16[192,512]{1,0:T(8,128)(2,1)S(1)}, bf16[192,512]{1,0:T(8,128)(2,1)S(1)}, u32[]{:S(2)}, u32[]{:S(2)}) collective-permute-start(bf16[192,512]{1,0:T(8,128)(2,1)S(1)} %get-tuple-element.102), channel_id=1, source_target_pairs={{0,3},{1,2},{2,1},{3,0},{4,7},{5,6},{6,5},{7,4},{8,11},{9,10},{10,... | collective-permute-start | bytes 589832 | tf_op jit(solution)/shard_map/ppermute | solution.py:367
  166.7 34.7 %collective-permute-start.38 = (bf16[2,4,120,768]{3,2,1,0:T(8,128)(2,1)}, bf16[2,4,120,768]{3,2,1,0:T(8,128)(2,1)}, u32[]{:S(2)}, u32[]{:S(2)}) collective-permute-start(bf16[2,4,120,768]{3,2,1,0:T(8,128)(2,1)} %get-tuple-element.137), channel_id=1, source_target_pairs={{0,8},{4,12},{8,0},{12,4},{16,24},{20,28},{24,16},{28,20},{1,9},{5... | collective-permute-start | bytes 4423688 | tf_op jit(solution)/shard_map/ppermute | solution.py:367
  168.2 34.4 %collective-permute-start.39 = (bf16[2,4,120,768]{3,2,1,0:T(8,128)(2,1)}, bf16[2,4,120,768]{3,2,1,0:T(8,128)(2,1)}, u32[]{:S(2)}, u32[]{:S(2)}) collective-permute-start(bf16[2,4,120,768]{3,2,1,0:T(8,128)(2,1)} %get-tuple-element.140), channel_id=1, source_target_pairs={{0,16},{4,20},{8,24},{12,28},{16,0},{20,4},{24,8},{28,12},{1,17},{... | collective-permute-start | bytes 4423688 | tf_op jit(solution)/shard_map/ppermute | solution.py:367
  171.0 18.8 %collective-permute-start.36 = (bf16[192,512]{1,0:T(8,128)(2,1)S(1)}, bf16[192,512]{1,0:T(8,128)(2,1)S(1)}, u32[]{:S(2)}, u32[]{:S(2)}) collective-permute-start(bf16[192,512]{1,0:T(8,128)(2,1)S(1)} %get-tuple-element.125), channel_id=1, source_target_pairs={{0,2},{1,3},{2,0},{3,1},{4,6},{5,7},{6,4},{7,5},{8,10},{9,11},{10,... | collective-permute-start | bytes 589832 | tf_op jit(solution)/shard_map/ppermute | solution.py:367
  173.1 16.7 %collective-permute-start.33 = (bf16[192,512]{1,0:T(8,128)(2,1)S(1)}, bf16[192,512]{1,0:T(8,128)(2,1)S(1)}, u32[]{:S(2)}, u32[]{:S(2)}) collective-permute-start(bf16[192,512]{1,0:T(8,128)(2,1)S(1)} %get-tuple-element.114), channel_id=1, source_target_pairs={{0,1},{1,0},{2,3},{3,2},{4,5},{5,4},{6,7},{7,6},{8,9},{9,8},{10,11... | collective-permute-start | bytes 589832 | tf_op jit(solution)/shard_map/ppermute | solution.py:367
  196.2 24.2 %all-to-all-start.1 = ((bf16[4,192,512]{2,1,0:T(8,128)(2,1)}), bf16[4,192,512]{2,1,0:T(8,128)(2,1)S(1)}, u32[]{:S(2)}, u32[]{:S(2)}) async-start(bf16[4,192,512]{2,1,0:T(8,128)(2,1)} %get-tuple-element.129), calls=%async_computation.1 | async-start | bytes 1572864 | tf_op jit(solution)/shard_map/all_to_all | solution.py:436
  207.7 18.6 %collective-permute-start.40 = (bf16[4,120,768]{2,1,0:T(8,128)(2,1)}, bf16[4,120,768]{2,1,0:T(8,128)(2,1)}, u32[]{:S(2)}, u32[]{:S(2)}) collective-permute-start(bf16[4,120,768]{2,1,0:T(8,128)(2,1)} %get-tuple-element.143), channel_id=1, source_target_pairs={{0,16},{4,20},{8,24},{12,28},{16,0},{20,4},{24,8},{28,12},{1,17},{... | collective-permute-start | bytes 2211848 | tf_op jit(solution)/shard_map/ppermute | solution.py:367
  208.5 17.8 %collective-permute-start.41 = (bf16[4,120,768]{2,1,0:T(8,128)(2,1)}, bf16[4,120,768]{2,1,0:T(8,128)(2,1)}, u32[]{:S(2)}, u32[]{:S(2)}) collective-permute-start(bf16[4,120,768]{2,1,0:T(8,128)(2,1)} %get-tuple-element.147), channel_id=1, source_target_pairs={{0,8},{4,12},{8,0},{12,4},{16,24},{20,28},{24,16},{28,20},{1,9},{5... | collective-permute-start | bytes 2211848 | tf_op jit(solution)/shard_map/ppermute | solution.py:367
  229.1 44.5 %all-to-all-start.2 = ((bf16[4,240,768]{2,1,0:T(8,128)(2,1)}), bf16[4,240,768]{2,1,0:T(8,128)(2,1)S(1)}, u32[]{:S(2)}, u32[]{:S(2)}) async-start(bf16[4,240,768]{2,1,0:T(8,128)(2,1)} %bulk_sum.1), calls=%async_computation.2 | async-start | bytes 2949120 | tf_op jit(solution)/shard_map/all_to_all | solution.py:436
  239.2 12.7 %collective-permute-start.43 = (bf16[264,768]{1,0:T(8,128)(2,1)S(1)}, bf16[264,768]{1,0:T(8,128)(2,1)S(1)}, u32[]{:S(2)}, u32[]{:S(2)}) collective-permute-start(bf16[264,768]{1,0:T(8,128)(2,1)S(1)} %get-tuple-element.151), channel_id=1, source_target_pairs={{0,8},{4,12},{8,0},{12,4},{16,24},{20,28},{24,16},{28,20},{1,9},{5... | collective-permute-start | bytes 1216520 | tf_op jit(solution)/shard_map/ppermute | solution.py:367
  240.5 19.8 %collective-permute-start.44 = (bf16[264,768]{1,0:T(8,128)(2,1)S(1)}, bf16[264,768]{1,0:T(8,128)(2,1)S(1)}, u32[]{:S(2)}, u32[]{:S(2)}) collective-permute-start(bf16[264,768]{1,0:T(8,128)(2,1)S(1)} %get-tuple-element.153), channel_id=1, source_target_pairs={{0,16},{4,20},{8,24},{12,28},{16,0},{20,4},{24,8},{28,12},{1,17},{... | collective-permute-start | bytes 1216520 | tf_op jit(solution)/shard_map/ppermute | solution.py:367
  241.1 19.3 %collective-permute-start.45 = (bf16[264,768]{1,0:T(8,128)(2,1)S(1)}, bf16[264,768]{1,0:T(8,128)(2,1)S(1)}, u32[]{:S(2)}, u32[]{:S(2)}) collective-permute-start(bf16[264,768]{1,0:T(8,128)(2,1)S(1)} %get-tuple-element.155), channel_id=1, source_target_pairs={{0,24},{4,28},{8,16},{12,20},{16,8},{20,12},{24,0},{28,4},{1,25},{... | collective-permute-start | bytes 1216520 | tf_op jit(solution)/shard_map/ppermute | solution.py:367
  273.9 16.7 %collective-permute-start.51 = (bf16[368,768]{1,0:T(8,128)(2,1)S(1)}, bf16[368,768]{1,0:T(8,128)(2,1)S(1)}, u32[]{:S(2)}, u32[]{:S(2)}) collective-permute-start(bf16[368,768]{1,0:T(8,128)(2,1)S(1)} %mesh_sum.1.refs_0_), channel_id=1, source_target_pairs={{0,24},{4,28},{8,16},{12,20},{16,8},{20,12},{24,0},{28,4},{1,25},{... | collective-permute-start | bytes 1695752 | tf_op jit(solution)/shard_map/ppermute | solution.py:367
  275.1 24.5 %collective-permute-start.50 = (bf16[368,768]{1,0:T(8,128)(2,1)S(1)}, bf16[368,768]{1,0:T(8,128)(2,1)S(1)}, u32[]{:S(2)}, u32[]{:S(2)}) collective-permute-start(bf16[368,768]{1,0:T(8,128)(2,1)S(1)} %mesh_sum.1.refs_0_), channel_id=1, source_target_pairs={{0,16},{4,20},{8,24},{12,28},{16,0},{20,4},{24,8},{28,12},{1,17},{... | collective-permute-start | bytes 1695752 | tf_op jit(solution)/shard_map/ppermute | solution.py:367
  276.7 22.9 %collective-permute-start.49 = (bf16[368,768]{1,0:T(8,128)(2,1)S(1)}, bf16[368,768]{1,0:T(8,128)(2,1)S(1)}, u32[]{:S(2)}, u32[]{:S(2)}) collective-permute-start(bf16[368,768]{1,0:T(8,128)(2,1)S(1)} %mesh_sum.1.refs_0_), channel_id=1, source_target_pairs={{0,8},{4,12},{8,0},{12,4},{16,24},{20,28},{24,16},{28,20},{1,9},{5... | collective-permute-start | bytes 1695752 | tf_op jit(solution)/shard_map/ppermute | solution.py:367
  277.5 22.7 %collective-permute-start.52 = (bf16[368,768]{1,0:T(8,128)(2,1)S(1)}, bf16[368,768]{1,0:T(8,128)(2,1)S(1)}, u32[]{:S(2)}, u32[]{:S(2)}) collective-permute-start(bf16[368,768]{1,0:T(8,128)(2,1)S(1)} %mesh_sum.1.refs_0_), channel_id=1, source_target_pairs={{0,4},{4,0},{8,12},{12,8},{16,20},{20,16},{24,28},{28,24},{1,5},{5... | collective-permute-start | bytes 1695752 | tf_op jit(solution)/shard_map/ppermute | solution.py:367
  (59 other events, 495.2 us)

commit v2 on v1

--- a/solution.py
+++ b/solution.py
@@ -10,6 +10,7 @@
 from jax.sharding import PartitionSpec as P
 
 LANES = 128
+FEED_PACK = 2
 ROWS = 16
 BASE = 256
 f32 = jnp.float32
@@ -683,18 +684,20 @@
     taps = kernel_ref.shape[1]
     filt[...] = jnp.zeros_like(filt)
     spot = lax.broadcasted_iota(jnp.int32, (8, taps), 1)
-    for place in range(ways):
-        start = relative_index(here, place, ways) * rows
-        for tile in range(rows // 8):
-            at = pl.ds(pl.multiple_of(start + tile * 8, 8), 8)
-            raw = kernel_ref[at, :]
-            shrunk = jnp.maximum(raw - thresh, 0.0) - jnp.maximum(-raw - thresh, 0.0)
-            before = jnp.where(spot == 0, 0.0, pltpu.roll(shrunk, 1, 1))
-            behind = jnp.where(spot == taps - 1, 0.0, pltpu.roll(shrunk, taps - 1, 1))
-            pooled = (before + shrunk + behind) / 3.0
-            kept = jnp.where(spot < taps - pad_ref[at, :], pooled, 0.0)
-            put_rows = place * rows + tile * 8
-            filt[0, put_rows : put_rows + 8, :taps] = kept
+
+    def step(tile, carry):
+        place = tile // (rows // 8)
+        start = relative_index(here, place, ways) * rows + (tile % (rows // 8)) * 8
+        at = pl.ds(pl.multiple_of(start, 8), 8)
+        raw = kernel_ref[at, :]
+        shrunk = jnp.maximum(raw - thresh, 0.0) - jnp.maximum(-raw - thresh, 0.0)
+        before = jnp.where(spot == 0, 0.0, pltpu.roll(shrunk, 1, 1))
+        behind = jnp.where(spot == taps - 1, 0.0, pltpu.roll(shrunk, taps - 1, 1))
+        pooled = (before + shrunk + behind) / 3.0
+        filt[0, pl.ds(pl.multiple_of(tile * 8, 8), 8), :taps] = jnp.where(spot < taps - pad_ref[at, :], pooled, 0.0)
+        return carry
+
+    lax.fori_loop(0, channels // 8, step, 0)
     filter_kernel(filt, high_ref, low_ref, twiddle_ref, spec_ref, zh, zl, radix=radix, channels=channels)
 
 
@@ -742,22 +745,24 @@
         for chip in range(4):
             for core in range(2):
                 for group, pieces in enumerate(groups):
-                    weight_copy(group, pieces[core * 4 + chip], core * 4 + chip).start()
+                    weight_copy(group, pieces[core * 4 + chip], 2 * chip + core).start()
 
     for core in range(2):
-        slot = core * 4 + step
         for group, pieces in enumerate(groups):
-            weight_copy(group, pieces[0], slot).wait()
-        proj = nt(weights[slot], low_ref[...])
+            weight_copy(group, pieces[0], 2 * step + core).wait()
+    size = weights.shape[1]
+    proj = nt(weights[pl.ds(2 * step, 2)].reshape(2 * size, weights.shape[2]), low_ref[...])
+    for core in range(2):
         for i, send_ref in enumerate(sends):
             to = i ^ level_ref[0]
             at = 4 * i * rows
-            value, one, two = (proj[at + k * rows : at + (k + 1) * rows] for k in range(3))
+            start = core * size + at
+            value, one, two = (proj[start + k * rows : start + (k + 1) * rows] for k in range(3))
             send_ref[core, 0] = (value * one).astype(bf16)
             v_ref[to, core, 0] = value
             one_ref[to, core, 0] = one
             two_ref[to, core, 0] = two
-            out_ref[to, core, 0] = weights[slot, at + 3 * rows : at + 4 * rows, :]
+            out_ref[to, core, 0] = weights[2 * step + core, at + 3 * rows : at + 4 * rows, :]
 
 
 def project(level, low, groups, mesh_rows):
@@ -798,6 +803,7 @@
     residual, second, out_acc, norm_acc, conv, turned, weights, grads, sems, grad_sems = refs[3:]
     step = pl.program_id(0)
     size = weights.shape[2]
+    pack = grads.shape[2] // size
     copies = []
     for side, (firsts, pairs) in enumerate(((up_firsts, ups), (down_firsts, downs))):
         for k in range(8):
@@ -823,17 +829,20 @@
         norm_acc[...] = jnp.zeros_like(norm_acc)
 
     for side in range(2):
-        pltpu.make_async_copy(up_firsts[0], weights.at[side, step], sems.at[side, step]).wait()
+        for k in range(pack):
+            at = step * pack + k
+            pltpu.make_async_copy(up_firsts[0], weights.at[side, at], sems.at[side, at]).wait()
     slot = step % 2
 
     @pl.when(step >= 2)
     def _():
         for side in range(2):
             pltpu.make_async_copy(
-                grads.at[side, slot], up_near.at[pl.ds(0, size), :], grad_sems.at[side, slot]
+                grads.at[side, slot], up_near.at[pl.ds(0, pack * size), :], grad_sems.at[side, slot]
             ).wait()
 
-    up, down = weights[0, step], weights[1, step]
+    width = second.shape[1]
+    up, down = (weights[side, pl.ds(step * pack, pack)].reshape(pack * size, width) for side in range(2))
     act, slope = gelu_both(nt(second[...], up))
     act_low = act.astype(bf16)
     grad_pre = (nt(grad_ref[...], down) * slope).astype(bf16)
@@ -841,10 +850,11 @@
     norm_acc[...] += dot(grad_pre, up, 1, 0)
     grads[0, slot] = tn(grad_pre, second[...]).astype(bf16)
     grads[1, slot] = tn(act_low, grad_ref[...]).astype(bf16)
-    at = pl.ds(pl.multiple_of((step % 4) * size, size), size)
+    steps = 4 // pack
+    at = pl.ds(pl.multiple_of((step % steps) * pack * size, size), pack * size)
     for core, outs in enumerate(((up_near, down_near), (far_grads.at[0], far_grads.at[1]))):
 
-        @pl.when(step // 4 == core)
+        @pl.when(step // steps == core)
         def _():
             for side in range(2):
                 pltpu.make_async_copy(
@@ -869,7 +879,7 @@
         for side in range(2):
             for last in range(2):
                 pltpu.make_async_copy(
-                    grads.at[side, last], up_near.at[pl.ds(0, size), :], grad_sems.at[side, last]
+                    grads.at[side, last], up_near.at[pl.ds(0, pack * size), :], grad_sems.at[side, last]
                 ).wait()
 
 
@@ -883,7 +893,7 @@
     anywhere = pl.BlockSpec(memory_space=pl.ANY)
     return pl.pallas_call(
         partial(feed_kernel, mesh_rows=mesh_rows),
-        grid=(8,),
+        grid=(8 // FEED_PACK,),
         in_specs=[SM] + [VM] * (len(wholes) + mesh_rows) + [anywhere] * 12,
         out_specs=[VM] * (6 + mesh_rows) + [anywhere] * 3,
         out_shape=[
@@ -905,11 +915,11 @@
             pltpu.VMEM((mesh_rows, channels // mesh_rows, spots), bf16),
             pltpu.VMEM((mesh_rows, channels // mesh_rows, spots), bf16),
             pltpu.VMEM((2, 8, size, width), bf16),
-            pltpu.VMEM((2, 2, size, width), bf16),
+            pltpu.VMEM((2, 2, FEED_PACK * size, width), bf16),
             pltpu.SemaphoreType.DMA((2, 8)),
             pltpu.SemaphoreType.DMA((2, 2)),
         ],
-        compiler_params=pltpu.CompilerParams(vmem_limit_bytes=42 << 20),
+        compiler_params=pltpu.CompilerParams(vmem_limit_bytes=38 << 20),
         name="feed_forward",
     )(here, *wholes, *conv, *ups[:2], *downs[:2], *ups[2:], *downs[2:])
 
@@ -1079,29 +1089,42 @@
 
 
 def unpack_kernel(here_ref, *refs, hidden, rows):
-    pieces, (up_ref, down_ref, out_ref, in_ref, kernel_ref, gains_ref, turned, gains) = refs[:8], refs[8:]
+    pieces, outs, gains_ref = refs[:8], refs[8:13], refs[13]
+    held, (turned, gains, sems) = refs[14:19], refs[19:]
+    up, down, out, given, kernel = held
+    copies = [pltpu.make_async_copy(source, to, sems.at[k]) for k, (source, to) in enumerate(zip(held, outs))]
     here = here_ref[0]
-    width = in_ref.shape[2]
-    taps = kernel_ref.shape[1]
+    width = given.shape[2]
+    taps = kernel.shape[1]
     parts = -(-taps // width)
     for slot, ref in enumerate(pieces):
-        at = slice_at(here, slot, hidden)
-        turned[at, :] = ref[:hidden].astype(f32)
+        turned[slice_at(here, slot, hidden), :] = ref[:hidden].astype(f32)
+    up[...] = turned[...].T
+    copies[0].start()
+    for slot, ref in enumerate(pieces):
         start = hidden + rows
-        down_ref[at, :] = ref[start : start + hidden].astype(f32)
+        down[slice_at(here, slot, hidden), :] = ref[start : start + hidden].astype(f32)
+    copies[1].start()
+    start = 2 * hidden + rows
+    for slot, ref in enumerate(pieces):
         at = slice_at(here, slot, rows)
-        out_ref[at, :] = ref[hidden : hidden + rows].astype(f32)
-        start = 2 * hidden + rows
+        out[at, :] = ref[hidden : hidden + rows].astype(f32)
         for place, gate in enumerate((2, 0, 1)):
-            in_ref[gate, at, :] = ref[start + place * rows : start + (place + 1) * rows].astype(f32)
+            given[gate, at, :] = ref[start + place * rows : start + (place + 1) * rows].astype(f32)
+    copies[2].start()
+    copies[3].start()
+    for slot, ref in enumerate(pieces):
+        at = slice_at(here, slot, rows)
         for part in range(parts):
             size = min(width, taps - part * width)
             block = ref[start + (3 + part) * rows : start + (4 + part) * rows].astype(f32)
-            kernel_ref[at, part * width : part * width + size] = block[:, :size]
+            kernel[at, part * width : part * width + size] = block[:, :size]
         gain = ref[start + (3 + parts) * rows :].astype(f32)
         gains[relative_index(here, slot, 8)] = gain[:2] + gain[2:4]
+    copies[4].start()
     gains_ref[...] = sum(gains[slot] for slot in range(8))
-    up_ref[...] = turned[...].T
+    for copy in copies:
+        copy.wait()
 
 
 def chips_of(x, done=()):
@@ -1162,12 +1185,11 @@
     own_feed = jnp.stack([own_up, own_down])
     own_feed = jnp.broadcast_to(own_feed, (mesh_rows,) + own_feed.shape)
     other_mixers = [swap(after(own_mixer, next_mixer), "mp", i) for i in range(2, mesh_rows)]
-    fspec = filter_slices(place, kernel, pad_len, tables, length, ways)
     (normed_low,) = whole_call(
         first_norm_forward_kernel, [((spots, width), bf16)], name="first_norm", count=2, room=10
     )(x, gain_first[None])
     first_group = chips_of(stacked(own_mixer, next_mixer))
-    other_mixers = [after(part, *first_group[1:], fspec, normed_low) for part in other_mixers]
+    other_mixers = [after(part, *first_group[1:], normed_low, tables) for part in other_mixers]
     second_group = chips_of(stacked(*other_mixers))
     feed_rows = turn(after(own_feed, *other_mixers))
     mixer = [[far(piece) for piece in pair_of(group)] for group in (first_group, second_group)]
@@ -1180,12 +1202,14 @@
     feed_rows = after(feed_rows, value)
     up, down = (feed_rows[:, side].reshape(-1, width) for side in range(2))
     up_x, down_y = swap(up, "dp", 2), swap(down, "dp", 4)
-    up_x, down_y = after(up_x, *received[1:]), after(down_y, *received[1:])
+    fspec = filter_slices(place, after(kernel, gate_two), pad_len, tables, length, ways)
+    up_x, down_y = after(up_x, *received[1:], fspec), after(down_y, *received[1:], fspec)
     quarter = ((2, mesh_rows * hidden, width), bf16)
     up_pair, down_pair = whole_call(stack_kernel, [quarter] * 2, name="feed_pairs", count=4, room=8)(
         up, up_x, down, down_y
     )
     up_pair, down_pair = swap(up_pair, "dp", 4), swap(down_pair, "dp", 2)
+    received = [received[0]] + [after(piece, fspec) for piece in received[1:]]
     *conv_out, uspec = conv_forward(level, received, fspec, tables)
     conv = levels_of(conv_out)
     ups = [after(up_pair, *conv[1:]), up, up_x]
@@ -1224,23 +1248,23 @@
     quarter = (half[0][1:], bf16)
     up_keep, up_send, down_keep, down_send = whole_call(
         pair_kernel, [pltpu.HBM(*quarter), quarter] * 2, name="kept_again", count=4, room=12
-    )(up_keep, after(up_in, mixed_out), down_keep, after(down_in, mixed_out))
+    )(far(up_keep), after(up_in, mixed_out), far(down_keep), after(down_in, mixed_out))
     up_in, down_in = swap(up_send, "dp", 4), swap(down_send, "dp", 2)
     rest_rows = (2 * mesh_rows + filt_parts) * rows
     rest_near, rest_far, grad_value, grad_one = whole_call(
         partial(rest_kernel, **sizes),
-        [pltpu.HBM((4, rest_rows, width), bf16), ((4, rest_rows, width), bf16)] + [pltpu.HBM(*tall)] * 2,
+        [pltpu.HBM((4, rest_rows, width), bf16)] * 2 + [pltpu.HBM(*tall)] * 2,
         [((channels, width), f32)],
         name="rest_grads",
         count=5,
         room=12,
     )(mixed, far(value), far(gate_one), far(normed_low), filt_grad)
     rest = whole_call(split_kernel, [((rest_rows, width), bf16)] * 4, name="rest_kept", count=2)(
-        rest_near, swap(rest_far, "dp", 1)
+        far(rest_near), swap(rest_far, "dp", 1)
     )
     (bulk,) = whole_call(
         bulk_kernel, [pltpu.HBM((mesh_rows, 2 * (hidden + rows), width), bf16)], name="bulk_sum", count=4
-    )(up_keep, after(up_in, rest_near), down_keep, after(down_in, rest_near))
+    )(far(up_keep), after(up_in, rest_near), far(down_keep), after(down_in, rest_near))
     bulk = turn(bulk)
     rest = [rest[0]] + [swap(rest[chip], "dp", 2 * chip) for chip in range(1, 4)]
     grad_tokens, gain_first_grad = whole_call(
@@ -1276,21 +1300,16 @@
         count=2 + mesh_rows,
         room=8,
     )(after(bulk, *rest[1:]), own_filt, *rest)
-    up_grad, down_grad, out_grad, in_grad, kernel_grad, gains = whole_call(
+    shapes = [up_weight.shape, down_weight.shape, (own_channels, width), (3, own_channels, width), kernel.shape]
+    up_grad, down_grad, out_grad, in_grad, kernel_grad, gains = pl.pallas_call(
         partial(unpack_kernel, hidden=hidden, rows=rows),
-        [
-            (up_weight.shape, f32),
-            (down_weight.shape, f32),
-            ((own_channels, width), f32),
-            ((3, own_channels, width), f32),
-            (kernel.shape, f32),
-            ((2, width), f32),
-        ],
-        [(down_weight.shape, f32), ((8, 2, width), f32)],
+        out_shape=[jax.ShapeDtypeStruct(shape, f32) for shape in shapes + [(2, width)]],
+        in_specs=[SM] + [VM] * 8,
+        out_specs=[pl.BlockSpec(memory_space=pl.ANY)] * 5 + [VM],
+        scratch_shapes=[pltpu.VMEM(shape, f32) for shape in shapes + [down_weight.shape, (8, 2, width)]]
+        + [pltpu.SemaphoreType.DMA((5,))],
+        compiler_params=pltpu.CompilerParams(vmem_limit_bytes=24 << 20),
         name="unpack",
-        smem=1,
-        count=8,
-        room=24,
     )(place, *pair_of(chips_of(mine)))
     return (
         block_out[None],

time: 308 us -> 298 us (0.968)
  local copies, waits for them, and re-layouts: 17 us -> 6.91 us
    unnamed x65 -> x51, local copies, waits for them, and re-layouts: 10.3 us -> 0.26 us
  transfers between devices with their start and end apart: 59 -> 59, of which waited for: 27 -> 32; matrix products, arithmetic and copies ran while one was open for 2% -> 2% of each run, Pallas kernels for 17% -> 19%
where the time goes in v2:
time: 298 us
  waiting for transfers between devices  126 us (42%)
  Pallas kernels  94.8 us (32%)
  starting transfers between devices  65.3 us (22%)
  local copies, waits for them, and re-layouts  6.91 us (2%)
  other arithmetic  3.82 us (1%)
    ppermute x56, waiting for transfers between devices, swap(): lax.ppermute(x, axis, [(i, i ^ bit) for i in range(lax.axis_size(axis))])  116 us
    ppermute x56, starting transfers between devices, swap(): lax.ppermute(x, axis, [(i, i ^ bit) for i in range(lax.axis_size(axis))])  52.3 us
    pallas_call x1, Pallas kernels, feed_forward(): pl.pallas_call(partial(feed_kernel, mesh_rows=mesh_rows), grid=(8 // FEED...  26.2 us
    all_to_all x3, starting transfers between devices, turn(): return lax.all_to_all(x, 'mp', 0, 0)  12.9 us
    all_to_all x3, waiting for transfers between devices, turn(): return lax.all_to_all(x, 'mp', 0, 0)  10 us
    pallas_call x1, Pallas kernels, fast_body(): whole_call(partial(first_norm_kernel, **sizes), [wide, ((1, width), f32)]...  9.11 us
    pallas_call x1, Pallas kernels, filter_slices(): whole_call(partial(filter_slices_kernel, radix=radix, channels=channels,...  8.99 us
    pallas_call x1, Pallas kernels, conv_forward(): pl.pallas_call(partial(conv_kernel, parts=parts, radix=radix, channels=ch...  7.13 us
  transfers between devices with their start and end apart: 59, of which 32 were waited for; matrix products, arithmetic and copies ran while one was open for 2% of the time, Pallas kernels for 19%

profile of v2, /device:TPU:0, one launch (start us, length us, event | category | flops | bytes accessed | tf_op | source)
XLA Modules:
  0.0 297.7 jit_solution(10864268992729182276)
XLA Ops:
  14.1 3.8 %collective-permute-start.9 = (bf16[96,768]{1,0:T(8,128)(2,1)S(1)}, bf16[96,768]{1,0:T(8,128)(2,1)S(1)}, u32[]{:S(2)}, u32[]{:S(2)}) collective-permute-start(bf16[96,768]{1,0:T(8,128)(2,1)S(1)} %bitcast.60), channel_id=1, source_target_pairs={{0,3},{1,2},{2,1},{3,0},{4,7},{5,6},{6,5},{7,4},{8,11},{9,10},{10,... | collective-permute-start | bytes 442376 | tf_op jit(solution)/shard_map/ppermute | solution.py:368
  21.9 3.2 %collective-permute-done.2.refs_2_.refs_5_ = bf16[192,768]{1,0:T(8,128)(2,1)} collective-permute-done((bf16[192,768]{1,0:T(8,128)(2,1)S(1)}, bf16[192,768]{1,0:T(8,128)(2,1)}, u32[]{:S(2)}, u32[]{:S(2)}) %collective-permute-start.2) | collective-permute-done | bytes 294944 | tf_op jit(solution)/shard_map/ppermute | solution.py:368
  25.3 3.5 %collective-permute-done.8.refs_0_ = bf16[96,768]{1,0:T(8,128)(2,1)S(1)} collective-permute-done((bf16[96,768]{1,0:T(8,128)(2,1)S(1)}, bf16[96,768]{1,0:T(8,128)(2,1)S(1)}, u32[]{:S(2)}, u32[]{:S(2)}) %collective-permute-start.8) | collective-permute-done | bytes 147488 | tf_op jit(solution)/shard_map/ppermute | solution.py:368
  29.9 4.3 %all-to-all-start = ((bf16[4,2,96,768]{3,2,1,0:T(8,128)(2,1)}), bf16[4,2,96,768]{3,2,1,0:T(8,128)(2,1)}, u32[]{:S(2)}, u32[]{:S(2)}) async-start(bf16[4,2,96,768]{3,2,1,0:T(8,128)(2,1)} %broadcast_in_dim.39), calls=%async_computation | async-start | bytes 2359296 | tf_op jit(solution)/shard_map/all_to_all | solution.py:437
  39.0 6.7 %collective-permute-done.12.refs_11_.refs_14_ = bf16[192,768]{1,0:T(8,128)(2,1)S(1)} collective-permute-done((bf16[192,768]{1,0:T(8,128)(2,1)S(1)}, bf16[192,768]{1,0:T(8,128)(2,1)S(1)}, u32[]{:S(2)}, u32[]{:S(2)}) %collective-permute-start.12) | collective-permute-done | bytes 294944 | tf_op jit(solution)/shard_map/ppermute | solution.py:368
  45.7 5.8 %collective-permute-done.11.refs_10_.refs_13_ = bf16[192,768]{1,0:T(8,128)(2,1)S(1)} collective-permute-done((bf16[192,768]{1,0:T(8,128)(2,1)S(1)}, bf16[192,768]{1,0:T(8,128)(2,1)S(1)}, u32[]{:S(2)}, u32[]{:S(2)}) %collective-permute-start.11) | collective-permute-done | bytes 294944 | tf_op jit(solution)/shard_map/ppermute | solution.py:368
  53.7 6.3 %project.1 = (bf16[2,4,24,512]{3,2,1,0:T(8,128)(2,1)}, bf16[2,4,24,512]{3,2,1,0:T(8,128)(2,1)}, bf16[2,4,24,512]{3,2,1,0:T(8,128)(2,1)}, bf16[2,4,24,512]{3,2,1,...) custom-call(s32[1]{0:T(128)} %bitcast.level_ref.here_ref.refs_0_, ...), custom_call_target="tpu_custom_call" | custom-call | tf_op jit(solution)/shard_map/project/pallas_call | solution.py:774
  71.1 9.0 %filter_spectrum.1.refs_4_ = f32[1536,512]{1,0:T(8,128)S(1)} custom-call(s32[1]{0:T(128)} %bitcast.12.here_ref, f32[192,2048]{1,0:T(8,128)} %kernel_ref.2, s32[192,1]{1,0:T(8,128)S(1)} %copy.26.pad_ref, bf16[512,512]{1,0:T(8,128)(2,1)} %fusion.high_ref.refs_5_, bf16[512,512]{1,0:T(8,128)(2,1)} %subtract_convert_fusion.low_ref, ...), custom_call_target="tpu_custom_call" | custom-call | tf_op jit(solution)/shard_map/filter_spectrum/pallas_call | solution.py:709
  80.2 3.4 %collective-permute-done.18.refs_2_ = bf16[192,512]{1,0:T(8,128)(2,1)S(1)} collective-permute-done((bf16[192,512]{1,0:T(8,128)(2,1)}, bf16[192,512]{1,0:T(8,128)(2,1)S(1)}, u32[]{:S(2)}, u32[]{:S(2)}) %collective-permute-start.18) | collective-permute-done | bytes 196640 | tf_op jit(solution)/shard_map/ppermute | solution.py:368
  85.3 7.1 %conv_forward.1 = (bf16[192,512]{1,0:T(8,128)(2,1)S(1)}, bf16[192,512]{1,0:T(8,128)(2,1)S(1)}, bf16[192,512]{1,0:T(8,128)(2,1)S(1)}, bf16[192,512]{1,0:T(8,128)(2,1)S(1)}, bf16[1536,512]{1,0:T(8,128)(2,1)}) custom-call(s32[1]{0:T(128)} %bitcast.level_ref.here_ref.refs_0_, bf16[192,512]{1,0:T(8,128)(2,1)S(1)} %bitcast.62, ...), custom_call_target="tpu_custom_call" | custom-call | tf_op jit(solution)/shard_map/conv_forward/pallas_call | solution.py:274
  100.8 10.2 %collective-permute-done.21.refs_8_ = bf16[192,512]{1,0:T(8,128)(2,1)S(1)} collective-permute-done((bf16[192,512]{1,0:T(8,128)(2,1)S(1)}, bf16[192,512]{1,0:T(8,128)(2,1)S(1)}, u32[]{:S(2)}, u32[]{:S(2)}) %collective-permute-start.21) | collective-permute-done | bytes 196640 | tf_op jit(solution)/shard_map/ppermute | solution.py:368
  112.1 4.3 %collective-permute-done.31.refs_20_ = bf16[384,768]{1,0:T(8,128)(2,1)S(1)} collective-permute-done((bf16[384,768]{1,0:T(8,128)(2,1)S(1)}, bf16[384,768]{1,0:T(8,128)(2,1)S(1)}, u32[]{:S(2)}, u32[]{:S(2)}) %collective-permute-start.31) | collective-permute-done | bytes 589856 | tf_op jit(solution)/shard_map/ppermute | solution.py:368
  118.1 26.2 %feed_forward.1 = (bf16[768,512]{1,0:T(8,128)(2,1)S(1)}, bf16[512,768]{1,0:T(8,128)(2,1)}, f32[512,768]{1,0:T(8,128)}, bf16[512,768]{1,0:T(8,128)(2,1)S(1)}, f32...) custom-call(s32[1]{0:T(128)} %bitcast.level_ref.here_ref.refs_0_, ...), custom_call_target="tpu_custom_call" | custom-call | tf_op jit(solution)/shard_map/feed_forward/pallas_call | solution.py:894
  147.8 6.1 %collective-permute-done.35.late_in = bf16[4,192,768]{2,1,0:T(8,128)(2,1)S(1)} collective-permute-done((bf16[4,192,768]{2,1,0:T(8,128)(2,1)S(1)}, bf16[4,192,768]{2,1,0:T(8,128)(2,1)S(1)}, u32[]{:S(2)}, u32[]{:S(2)}) %collective-permute-start.35) | collective-permute-done | bytes 1179680 | tf_op jit(solution)/shard_map/ppermute | solution.py:368
  153.9 3.9 %kept.1 = (bf16[2,4,120,768]{3,2,1,0:T(8,128)(2,1)}, bf16[2,4,120,768]{3,2,1,0:T(8,128)(2,1)}, bf16[2,4,120,768]{3,2,1,0:T(8,128)(2,1)}, bf16[2,4,120,768]{3,2,1,0:T(8,128)(2,1)}) custom-call(bf16[1536,768]{1,0:T(8,128)(2,1)S(1)} %get-tuple-element.123.up_ref, bf16[1536,768]{1,0:T(8,128)(2,1)S(1)} %copy-done.8, ...), custom_call_target="tpu_custom_call" | custom-call | tf_op jit(solution)/shard_map/kept/pallas_call | solution.py:1239
  164.8 4.2 %collective-permute-done.37.refs_3_ = bf16[192,512]{1,0:T(8,128)(2,1)S(1)} collective-permute-done((bf16[192,512]{1,0:T(8,128)(2,1)S(1)}, bf16[192,512]{1,0:T(8,128)(2,1)S(1)}, u32[]{:S(2)}, u32[]{:S(2)}) %collective-permute-start.37) | collective-permute-done | bytes 196640 | tf_op jit(solution)/shard_map/ppermute | solution.py:368
  169.0 11.6 %collective-permute-done.36.refs_2_ = bf16[192,512]{1,0:T(8,128)(2,1)S(1)} collective-permute-done((bf16[192,512]{1,0:T(8,128)(2,1)S(1)}, bf16[192,512]{1,0:T(8,128)(2,1)S(1)}, u32[]{:S(2)}, u32[]{:S(2)}) %collective-permute-start.36) | collective-permute-done | bytes 196640 | tf_op jit(solution)/shard_map/ppermute | solution.py:368
  180.6 6.4 %conv_mixed.1 = (bf16[4,192,512]{2,1,0:T(8,128)(2,1)}, bf16[1536,512]{1,0:T(8,128)(2,1)}) custom-call(s32[1]{0:T(128)} %bitcast.level_ref.here_ref.refs_0_, bf16[192,512]{1,0:T(8,128)(2,1)S(1)} %get-tuple-element.121.refs_0_, bf16[192,512]{1,0:T(8,128)(2,1)S(1)} %collective-permute-done.33.refs_1_, bf16[192,512]{1,0:T(8,128)(2,1)S(1)} %collective-permute-done.36.refs_2_, ...), custom_call_target="tpu_custom_call" | custom-call | tf_op jit(solution)/shard_map/conv_mixed/pallas_call | solution.py:293
  187.0 3.7 %all-to-all-start.1 = ((bf16[4,192,512]{2,1,0:T(8,128)(2,1)}), bf16[4,192,512]{2,1,0:T(8,128)(2,1)S(1)}, u32[]{:S(2)}, u32[]{:S(2)}) async-start(bf16[4,192,512]{2,1,0:T(8,128)(2,1)} %get-tuple-element.137), calls=%async_computation.1 | async-start | bytes 1572864 | tf_op jit(solution)/shard_map/all_to_all | solution.py:437
  193.7 4.4 %kept_again.1 = (bf16[4,120,768]{2,1,0:T(8,128)(2,1)}, bf16[4,120,768]{2,1,0:T(8,128)(2,1)}, bf16[4,120,768]{2,1,0:T(8,128)(2,1)}, bf16[4,120,768]{2,1,0:T(8,128)(2,1)}) custom-call(bf16[2,4,120,768]{3,2,1,0:T(8,128)(2,1)} %get-tuple-element.131.up_ref, bf16[2,4,120,768]{3,2,1,0:T(8,128)(2,1)S(1)} %collective-permute-done.38.up_in, ...), custom_call_target="tpu_custom_call" | custom-call | tf_op jit(solution)/shard_map/kept_again/pallas_call | solution.py:1249
  203.2 7.9 %all-to-all-done.1 = bf16[4,192,512]{2,1,0:T(8,128)(2,1)S(1)} async-done(((bf16[4,192,512]{2,1,0:T(8,128)(2,1)}), bf16[4,192,512]{2,1,0:T(8,128)(2,1)S(1)}, u32[]{:S(2)}, u32[]{:S(2)}) %all-to-all-start.1) | async-done | bytes 786464 | tf_op jit(solution)/shard_map/all_to_all | solution.py:437
  211.1 5.7 %rest_grads.1 = (bf16[4,264,768]{2,1,0:T(8,128)(2,1)}, bf16[4,264,768]{2,1,0:T(8,128)(2,1)}, bf16[768,512]{1,0:T(8,128)(2,1)}, bf16[768,512]{1,0:T(8,128)(2,1)}) custom-call(bf16[768,512]{1,0:T(8,128)(2,1)S(1)} %bitcast.45, f32[768,512]{1,0:T(8,128)} %bitcast.65, f32[768,512]{1,0:T(8,128)} %bitcast.66, bf16[512,768]{1,0:T(8,128)(2,1)} %copy-done.3, ...), custom_call_target="tpu_custom_call" | custom-call | tf_op jit(solution)/shard_map/rest_grads/pallas_call | solution.py:1254
  216.8 3.2 %bulk_sum.1 = bf16[4,240,768]{2,1,0:T(8,128)(2,1)} custom-call(bf16[4,120,768]{2,1,0:T(8,128)(2,1)} %get-tuple-element.150.up_ref, bf16[4,120,768]{2,1,0:T(8,128)(2,1)} %collective-permute-done.40.up_in, bf16[4,120,768]{2,1,0:T(8,128)(2,1)} %get-tuple-element.154.down_ref, bf16[4,120,768]{2,1,0:T(8,128)(2,1)} %collective-permute-done.41.down_in), custom_call_target="tpu_custom_call" | custom-call | tf_op jit(solution)/shard_map/bulk_sum/pallas_call | solution.py:1265
  220.0 4.9 %all-to-all-start.2 = ((bf16[4,240,768]{2,1,0:T(8,128)(2,1)}), bf16[4,240,768]{2,1,0:T(8,128)(2,1)S(1)}, u32[]{:S(2)}, u32[]{:S(2)}) async-start(bf16[4,240,768]{2,1,0:T(8,128)(2,1)} %bulk_sum.1), calls=%async_computation.2 | async-start | bytes 2949120 | tf_op jit(solution)/shard_map/all_to_all | solution.py:437
  224.9 3.7 %collective-permute-done.42.far_ref = bf16[4,264,768]{2,1,0:T(8,128)(2,1)S(1)} collective-permute-done((bf16[4,264,768]{2,1,0:T(8,128)(2,1)}, bf16[4,264,768]{2,1,0:T(8,128)(2,1)S(1)}, u32[]{:S(2)}, u32[]{:S(2)}) %collective-permute-start.42) | collective-permute-done | bytes 1622048 | tf_op jit(solution)/shard_map/ppermute | solution.py:368
  234.0 9.1 %first_norm_back.1 = (f32[512,768]{1,0:T(8,128)}, f32[1,768]{1,0:T(1,128)S(1)}) custom-call(s32[1]{0:T(128)} %bitcast.level_ref.here_ref.refs_0_, bf16[4,192,512]{2,1,0:T(8,128)(2,1)} %bitcast.69, bf16[4,192,512]{2,1,0:T(8,128)(2,1)} %bitcast.70, bf16[4,192,512]{2,1,0:T(8,128)(2,1)} %bitcast.63, bf16[192,768]{1,0:T(8,128)(2,1)} %bitcast.51, ...), custom_call_target="tpu_custom_call" | custom-call | tf_op jit(solution)/shard_map/first_norm_back/pallas_call | solution.py:1270
  243.1 8.3 %collective-permute-done.44.p2 = bf16[264,768]{1,0:T(8,128)(2,1)S(1)} collective-permute-done((bf16[264,768]{1,0:T(8,128)(2,1)S(1)}, bf16[264,768]{1,0:T(8,128)(2,1)S(1)}, u32[]{:S(2)}, u32[]{:S(2)}) %collective-permute-start.44) | collective-permute-done | bytes 405536 | tf_op jit(solution)/shard_map/ppermute | solution.py:368
  256.3 3.8 %collective-permute-done.46.refs_1_ = bf16[56,768]{1,0:T(8,128)(2,1)S(1)} collective-permute-done((bf16[56,768]{1,0:T(8,128)(2,1)S(1)}, bf16[56,768]{1,0:T(8,128)(2,1)S(1)}, u32[]{:S(2)}, u32[]{:S(2)}) %collective-permute-start.46) | collective-permute-done | bytes 86048 | tf_op jit(solution)/shard_map/ppermute | solution.py:368
  260.1 4.4 %collective-permute-done.47.refs_2_ = bf16[56,768]{1,0:T(8,128)(2,1)S(1)} collective-permute-done((bf16[56,768]{1,0:T(8,128)(2,1)S(1)}, bf16[56,768]{1,0:T(8,128)(2,1)S(1)}, u32[]{:S(2)}, u32[]{:S(2)}) %collective-permute-start.47) | collective-permute-done | bytes 86048 | tf_op jit(solution)/shard_map/ppermute | solution.py:368
  268.3 13.1 %collective-permute-done.51.refs_3_ = bf16[368,768]{1,0:T(8,128)(2,1)S(1)} collective-permute-done((bf16[368,768]{1,0:T(8,128)(2,1)S(1)}, bf16[368,768]{1,0:T(8,128)(2,1)S(1)}, u32[]{:S(2)}, u32[]{:S(2)}) %collective-permute-start.51) | collective-permute-done | bytes 565280 | tf_op jit(solution)/shard_map/ppermute | solution.py:368
  281.5 8.3 %collective-permute-done.50.refs_2_ = bf16[368,768]{1,0:T(8,128)(2,1)S(1)} collective-permute-done((bf16[368,768]{1,0:T(8,128)(2,1)S(1)}, bf16[368,768]{1,0:T(8,128)(2,1)S(1)}, u32[]{:S(2)}, u32[]{:S(2)}) %collective-permute-start.50) | collective-permute-done | bytes 565280 | tf_op jit(solution)/shard_map/ppermute | solution.py:368
  292.8 4.4 %unpack.1 = (f32[768,768]{1,0:T(8,128)}, f32[768,768]{1,0:T(8,128)}, f32[192,768]{1,0:T(8,128)}, f32[3,192,768]{2,1,0:T(8,128)}, f32[192,2048]{1,0:T(8,128)}, /*index=5*/f32[2,768]{1,0:T(2,128)S(1)}) custom-call(s32[1]{0:T(128)} %bitcast.12.here_ref, bf16[368,768]{1,0:T(8,128)(2,1)S(1)} %mesh_sum.1.refs_0_, ...), custom_call_target="tpu_custom_call" | custom-call | tf_op jit(solution)/shard_map/unpack/pallas_call | solution.py:1304
  (173 shorter events, 85.5 us)
Async XLA Ops:
  9.4 12.5 %collective-permute-start.3 = (bf16[192,768]{1,0:T(8,128)(2,1)S(1)}, bf16[192,768]{1,0:T(8,128)(2,1)}, u32[]{:S(2)}, u32[]{:S(2)}) collective-permute-start(bf16[192,768]{1,0:T(8,128)(2,1)S(1)} %bitcast.46), channel_id=1, source_target_pairs={{0,24},{4,28},{8,16},{12,20},{16,8},{20,12},{24,0},{28,4},{1,25},{... | collective-permute-start | bytes 884744 | tf_op jit(solution)/shard_map/ppermute | solution.py:368
  12.1 13.0 %collective-permute-start.2 = (bf16[192,768]{1,0:T(8,128)(2,1)S(1)}, bf16[192,768]{1,0:T(8,128)(2,1)}, u32[]{:S(2)}, u32[]{:S(2)}) collective-permute-start(bf16[192,768]{1,0:T(8,128)(2,1)S(1)} %bitcast.47), channel_id=1, source_target_pairs={{0,16},{4,20},{8,24},{12,28},{16,0},{20,4},{24,8},{28,12},{1,17},{... | collective-permute-start | bytes 884744 | tf_op jit(solution)/shard_map/ppermute | solution.py:368
  12.6 12.6 %collective-permute-start.1 = (bf16[192,768]{1,0:T(8,128)(2,1)S(1)}, bf16[192,768]{1,0:T(8,128)(2,1)}, u32[]{:S(2)}, u32[]{:S(2)}) collective-permute-start(bf16[192,768]{1,0:T(8,128)(2,1)S(1)} %bitcast.48), channel_id=1, source_target_pairs={{0,8},{4,12},{8,0},{12,4},{16,24},{20,28},{24,16},{28,20},{1,9},{5... | collective-permute-start | bytes 884744 | tf_op jit(solution)/shard_map/ppermute | solution.py:368
  29.9 32.3 %all-to-all-start = ((bf16[4,2,96,768]{3,2,1,0:T(8,128)(2,1)}), bf16[4,2,96,768]{3,2,1,0:T(8,128)(2,1)}, u32[]{:S(2)}, u32[]{:S(2)}) async-start(bf16[4,2,96,768]{3,2,1,0:T(8,128)(2,1)} %broadcast_in_dim.39), calls=%async_computation | async-start | bytes 2359296 | tf_op jit(solution)/shard_map/all_to_all | solution.py:437
  37.4 14.1 %collective-permute-start.11 = (bf16[192,768]{1,0:T(8,128)(2,1)S(1)}, bf16[192,768]{1,0:T(8,128)(2,1)S(1)}, u32[]{:S(2)}, u32[]{:S(2)}) collective-permute-start(bf16[192,768]{1,0:T(8,128)(2,1)S(1)} %bitcast.53), channel_id=1, source_target_pairs={{0,16},{4,20},{8,24},{12,28},{16,0},{20,4},{24,8},{28,12},{1,17},{... | collective-permute-start | bytes 884744 | tf_op jit(solution)/shard_map/ppermute | solution.py:368
  37.9 13.7 %collective-permute-start.10 = (bf16[192,768]{1,0:T(8,128)(2,1)S(1)}, bf16[192,768]{1,0:T(8,128)(2,1)S(1)}, u32[]{:S(2)}, u32[]{:S(2)}) collective-permute-start(bf16[192,768]{1,0:T(8,128)(2,1)S(1)} %bitcast.54), channel_id=1, source_target_pairs={{0,8},{4,12},{8,0},{12,4},{16,24},{20,28},{24,16},{28,20},{1,9},{5... | collective-permute-start | bytes 884744 | tf_op jit(solution)/shard_map/ppermute | solution.py:368
  38.5 13.6 %collective-permute-start.13 = (bf16[192,768]{1,0:T(8,128)(2,1)S(1)}, bf16[192,768]{1,0:T(8,128)(2,1)}, u32[]{:S(2)}, u32[]{:S(2)}) collective-permute-start(bf16[192,768]{1,0:T(8,128)(2,1)S(1)} %bitcast.55), channel_id=1, source_target_pairs={{0,4},{4,0},{8,12},{12,8},{16,20},{20,16},{24,28},{28,24},{1,5},{5... | collective-permute-start | bytes 884744 | tf_op jit(solution)/shard_map/ppermute | solution.py:368
  38.5 13.6 %collective-permute-start.5 = (bf16[192,768]{1,0:T(8,128)(2,1)}, bf16[192,768]{1,0:T(8,128)(2,1)}, u32[]{:S(2)}, u32[]{:S(2)}) collective-permute-start(bf16[192,768]{1,0:T(8,128)(2,1)} %collective-permute-done.1.refs_1_.refs_4_), channel_id=1, source_target_pairs={{0,4},{4,0},{8,12},{12,8},{16,20},{20,16},{24,28},{28,24},{1,5},{5... | collective-permute-start | bytes 884744 | tf_op jit(solution)/shard_map/ppermute | solution.py:368
  63.6 20.1 %collective-permute-start.24 = (bf16[384,768]{1,0:T(8,128)(2,1)S(1)}, bf16[384,768]{1,0:T(8,128)(2,1)S(1)}, u32[]{:S(2)}, u32[]{:S(2)}) collective-permute-start(bf16[384,768]{1,0:T(8,128)(2,1)S(1)} %bitcast.37), channel_id=1, source_target_pairs={{0,16},{4,20},{8,24},{12,28},{16,0},{20,4},{24,8},{28,12},{1,17},{... | collective-permute-start | bytes 1769480 | tf_op jit(solution)/shard_map/ppermute | solution.py:368
  65.1 18.5 %collective-permute-start.23 = (bf16[384,768]{1,0:T(8,128)(2,1)S(1)}, bf16[384,768]{1,0:T(8,128)(2,1)S(1)}, u32[]{:S(2)}, u32[]{:S(2)}) collective-permute-start(bf16[384,768]{1,0:T(8,128)(2,1)S(1)} %bitcast.41), channel_id=1, source_target_pairs={{0,8},{4,12},{8,0},{12,4},{16,24},{20,28},{24,16},{28,20},{1,9},{5... | collective-permute-start | bytes 1769480 | tf_op jit(solution)/shard_map/ppermute | solution.py:368
  66.6 13.6 %collective-permute-start.17 = (bf16[192,512]{1,0:T(8,128)(2,1)}, bf16[192,512]{1,0:T(8,128)(2,1)S(1)}, u32[]{:S(2)}, u32[]{:S(2)}) collective-permute-start(bf16[192,512]{1,0:T(8,128)(2,1)} %bitcast.11), channel_id=1, source_target_pairs={{0,1},{1,0},{2,3},{3,2},{4,5},{5,4},{6,7},{7,6},{8,9},{9,8},{10,11... | collective-permute-start | bytes 589832 | tf_op jit(solution)/shard_map/ppermute | solution.py:368
  66.6 17.0 %collective-permute-start.18 = (bf16[192,512]{1,0:T(8,128)(2,1)}, bf16[192,512]{1,0:T(8,128)(2,1)S(1)}, u32[]{:S(2)}, u32[]{:S(2)}) collective-permute-start(bf16[192,512]{1,0:T(8,128)(2,1)} %bitcast.14), channel_id=1, source_target_pairs={{0,2},{1,3},{2,0},{3,1},{4,6},{5,7},{6,4},{7,5},{8,10},{9,11},{10,... | collective-permute-start | bytes 589832 | tf_op jit(solution)/shard_map/ppermute | solution.py:368
  68.7 15.0 %collective-permute-start.19 = (bf16[192,512]{1,0:T(8,128)(2,1)}, bf16[192,512]{1,0:T(8,128)(2,1)}, u32[]{:S(2)}, u32[]{:S(2)}) collective-permute-start(bf16[192,512]{1,0:T(8,128)(2,1)} %bitcast.15), channel_id=1, source_target_pairs={{0,3},{1,2},{2,1},{3,0},{4,7},{5,6},{6,5},{7,4},{8,11},{9,10},{10,... | collective-permute-start | bytes 589832 | tf_op jit(solution)/shard_map/ppermute | solution.py:368
  83.8 27.2 %collective-permute-start.25 = (bf16[2,384,768]{2,1,0:T(8,128)(2,1)S(1)}, bf16[2,384,768]{2,1,0:T(8,128)(2,1)S(1)}, u32[]{:S(2)}, u32[]{:S(2)}) collective-permute-start(bf16[2,384,768]{2,1,0:T(8,128)(2,1)S(1)} %get-tuple-element.116), channel_id=1, source_target_pairs={{0,16},{4,20},{8,24},{12,28},{16,0},{20,4},{24,8},{28,12},{1,17},{... | collective-permute-start | bytes 3538952 | tf_op jit(solution)/shard_map/ppermute | solution.py:368
  84.8 26.3 %collective-permute-start.27 = (bf16[2,384,768]{2,1,0:T(8,128)(2,1)S(1)}, bf16[2,384,768]{2,1,0:T(8,128)(2,1)S(1)}, u32[]{:S(2)}, u32[]{:S(2)}) collective-permute-start(bf16[2,384,768]{2,1,0:T(8,128)(2,1)S(1)} %get-tuple-element.118), channel_id=1, source_target_pairs={{0,8},{4,12},{8,0},{12,4},{16,24},{20,28},{24,16},{28,20},{1,9},{5... | collective-permute-start | bytes 3538952 | tf_op jit(solution)/shard_map/ppermute | solution.py:368
  95.4 15.6 %collective-permute-start.21 = (bf16[192,512]{1,0:T(8,128)(2,1)S(1)}, bf16[192,512]{1,0:T(8,128)(2,1)S(1)}, u32[]{:S(2)}, u32[]{:S(2)}) collective-permute-start(bf16[192,512]{1,0:T(8,128)(2,1)S(1)} %get-tuple-element.109), channel_id=1, source_target_pairs={{0,2},{1,3},{2,0},{3,1},{4,6},{5,7},{6,4},{7,5},{8,10},{9,11},{10,... | collective-permute-start | bytes 589832 | tf_op jit(solution)/shard_map/ppermute | solution.py:368
  96.3 14.7 %collective-permute-start.22 = (bf16[192,512]{1,0:T(8,128)(2,1)S(1)}, bf16[192,512]{1,0:T(8,128)(2,1)S(1)}, u32[]{:S(2)}, u32[]{:S(2)}) collective-permute-start(bf16[192,512]{1,0:T(8,128)(2,1)S(1)} %get-tuple-element.110), channel_id=1, source_target_pairs={{0,3},{1,2},{2,1},{3,0},{4,7},{5,6},{6,5},{7,4},{8,11},{9,10},{10,... | collective-permute-start | bytes 589832 | tf_op jit(solution)/shard_map/ppermute | solution.py:368
  157.8 34.5 %collective-permute-start.38 = (bf16[2,4,120,768]{3,2,1,0:T(8,128)(2,1)}, bf16[2,4,120,768]{3,2,1,0:T(8,128)(2,1)S(1)}, u32[]{:S(2)}, u32[]{:S(2)}) collective-permute-start(bf16[2,4,120,768]{3,2,1,0:T(8,128)(2,1)} %get-tuple-element.145), channel_id=1, source_target_pairs={{0,8},{4,12},{8,0},{12,4},{16,24},{20,28},{24,16},{28,20},{1,9},{5... | collective-permute-start | bytes 4423688 | tf_op jit(solution)/shard_map/ppermute | solution.py:368
  159.3 34.4 %collective-permute-start.39 = (bf16[2,4,120,768]{3,2,1,0:T(8,128)(2,1)}, bf16[2,4,120,768]{3,2,1,0:T(8,128)(2,1)}, u32[]{:S(2)}, u32[]{:S(2)}) collective-permute-start(bf16[2,4,120,768]{3,2,1,0:T(8,128)(2,1)} %get-tuple-element.148), channel_id=1, source_target_pairs={{0,16},{4,20},{8,24},{12,28},{16,0},{20,4},{24,8},{28,12},{1,17},{... | collective-permute-start | bytes 4423688 | tf_op jit(solution)/shard_map/ppermute | solution.py:368
  161.6 19.0 %collective-permute-start.36 = (bf16[192,512]{1,0:T(8,128)(2,1)S(1)}, bf16[192,512]{1,0:T(8,128)(2,1)S(1)}, u32[]{:S(2)}, u32[]{:S(2)}) collective-permute-start(bf16[192,512]{1,0:T(8,128)(2,1)S(1)} %get-tuple-element.133), channel_id=1, source_target_pairs={{0,2},{1,3},{2,0},{3,1},{4,6},{5,7},{6,4},{7,5},{8,10},{9,11},{10,... | collective-permute-start | bytes 589832 | tf_op jit(solution)/shard_map/ppermute | solution.py:368
  164.2 16.4 %collective-permute-start.33 = (bf16[192,512]{1,0:T(8,128)(2,1)S(1)}, bf16[192,512]{1,0:T(8,128)(2,1)S(1)}, u32[]{:S(2)}, u32[]{:S(2)}) collective-permute-start(bf16[192,512]{1,0:T(8,128)(2,1)S(1)} %get-tuple-element.122), channel_id=1, source_target_pairs={{0,1},{1,0},{2,3},{3,2},{4,5},{5,4},{6,7},{7,6},{8,9},{9,8},{10,11... | collective-permute-start | bytes 589832 | tf_op jit(solution)/shard_map/ppermute | solution.py:368
  187.0 24.0 %all-to-all-start.1 = ((bf16[4,192,512]{2,1,0:T(8,128)(2,1)}), bf16[4,192,512]{2,1,0:T(8,128)(2,1)S(1)}, u32[]{:S(2)}, u32[]{:S(2)}) async-start(bf16[4,192,512]{2,1,0:T(8,128)(2,1)} %get-tuple-element.137), calls=%async_computation.1 | async-start | bytes 1572864 | tf_op jit(solution)/shard_map/all_to_all | solution.py:437
  198.1 18.7 %collective-permute-start.40 = (bf16[4,120,768]{2,1,0:T(8,128)(2,1)}, bf16[4,120,768]{2,1,0:T(8,128)(2,1)}, u32[]{:S(2)}, u32[]{:S(2)}) collective-permute-start(bf16[4,120,768]{2,1,0:T(8,128)(2,1)} %get-tuple-element.151), channel_id=1, source_target_pairs={{0,16},{4,20},{8,24},{12,28},{16,0},{20,4},{24,8},{28,12},{1,17},{... | collective-permute-start | bytes 2211848 | tf_op jit(solution)/shard_map/ppermute | solution.py:368
  198.6 18.2 %collective-permute-start.41 = (bf16[4,120,768]{2,1,0:T(8,128)(2,1)}, bf16[4,120,768]{2,1,0:T(8,128)(2,1)}, u32[]{:S(2)}, u32[]{:S(2)}) collective-permute-start(bf16[4,120,768]{2,1,0:T(8,128)(2,1)} %get-tuple-element.155), channel_id=1, source_target_pairs={{0,8},{4,12},{8,0},{12,4},{16,24},{20,28},{24,16},{28,20},{1,9},{5... | collective-permute-start | bytes 2211848 | tf_op jit(solution)/shard_map/ppermute | solution.py:368
  220.0 44.5 %all-to-all-start.2 = ((bf16[4,240,768]{2,1,0:T(8,128)(2,1)}), bf16[4,240,768]{2,1,0:T(8,128)(2,1)S(1)}, u32[]{:S(2)}, u32[]{:S(2)}) async-start(bf16[4,240,768]{2,1,0:T(8,128)(2,1)} %bulk_sum.1), calls=%async_computation.2 | async-start | bytes 2949120 | tf_op jit(solution)/shard_map/all_to_all | solution.py:437
  230.4 12.7 %collective-permute-start.43 = (bf16[264,768]{1,0:T(8,128)(2,1)S(1)}, bf16[264,768]{1,0:T(8,128)(2,1)S(1)}, u32[]{:S(2)}, u32[]{:S(2)}) collective-permute-start(bf16[264,768]{1,0:T(8,128)(2,1)S(1)} %get-tuple-element.159), channel_id=1, source_target_pairs={{0,8},{4,12},{8,0},{12,4},{16,24},{20,28},{24,16},{28,20},{1,9},{5... | collective-permute-start | bytes 1216520 | tf_op jit(solution)/shard_map/ppermute | solution.py:368
  231.6 19.8 %collective-permute-start.44 = (bf16[264,768]{1,0:T(8,128)(2,1)S(1)}, bf16[264,768]{1,0:T(8,128)(2,1)S(1)}, u32[]{:S(2)}, u32[]{:S(2)}) collective-permute-start(bf16[264,768]{1,0:T(8,128)(2,1)S(1)} %get-tuple-element.161), channel_id=1, source_target_pairs={{0,16},{4,20},{8,24},{12,28},{16,0},{20,4},{24,8},{28,12},{1,17},{... | collective-permute-start | bytes 1216520 | tf_op jit(solution)/shard_map/ppermute | solution.py:368
  232.1 19.3 %collective-permute-start.45 = (bf16[264,768]{1,0:T(8,128)(2,1)S(1)}, bf16[264,768]{1,0:T(8,128)(2,1)S(1)}, u32[]{:S(2)}, u32[]{:S(2)}) collective-permute-start(bf16[264,768]{1,0:T(8,128)(2,1)S(1)} %get-tuple-element.163), channel_id=1, source_target_pairs={{0,24},{4,28},{8,16},{12,20},{16,8},{20,12},{24,0},{28,4},{1,25},{... | collective-permute-start | bytes 1216520 | tf_op jit(solution)/shard_map/ppermute | solution.py:368
  264.8 16.7 %collective-permute-start.51 = (bf16[368,768]{1,0:T(8,128)(2,1)S(1)}, bf16[368,768]{1,0:T(8,128)(2,1)S(1)}, u32[]{:S(2)}, u32[]{:S(2)}) collective-permute-start(bf16[368,768]{1,0:T(8,128)(2,1)S(1)} %mesh_sum.1.refs_0_), channel_id=1, source_target_pairs={{0,24},{4,28},{8,16},{12,20},{16,8},{20,12},{24,0},{28,4},{1,25},{... | collective-permute-start | bytes 1695752 | tf_op jit(solution)/shard_map/ppermute | solution.py:368
  266.3 23.4 %collective-permute-start.50 = (bf16[368,768]{1,0:T(8,128)(2,1)S(1)}, bf16[368,768]{1,0:T(8,128)(2,1)S(1)}, u32[]{:S(2)}, u32[]{:S(2)}) collective-permute-start(bf16[368,768]{1,0:T(8,128)(2,1)S(1)} %mesh_sum.1.refs_0_), channel_id=1, source_target_pairs={{0,16},{4,20},{8,24},{12,28},{16,0},{20,4},{24,8},{28,12},{1,17},{... | collective-permute-start | bytes 1695752 | tf_op jit(solution)/shard_map/ppermute | solution.py:368
  267.9 22.9 %collective-permute-start.49 = (bf16[368,768]{1,0:T(8,128)(2,1)S(1)}, bf16[368,768]{1,0:T(8,128)(2,1)S(1)}, u32[]{:S(2)}, u32[]{:S(2)}) collective-permute-start(bf16[368,768]{1,0:T(8,128)(2,1)S(1)} %mesh_sum.1.refs_0_), channel_id=1, source_target_pairs={{0,8},{4,12},{8,0},{12,4},{16,24},{20,28},{24,16},{28,20},{1,9},{5... | collective-permute-start | bytes 1695752 | tf_op jit(solution)/shard_map/ppermute | solution.py:368
  268.3 22.5 %collective-permute-start.52 = (bf16[368,768]{1,0:T(8,128)(2,1)S(1)}, bf16[368,768]{1,0:T(8,128)(2,1)S(1)}, u32[]{:S(2)}, u32[]{:S(2)}) collective-permute-start(bf16[368,768]{1,0:T(8,128)(2,1)S(1)} %mesh_sum.1.refs_0_), channel_id=1, source_target_pairs={{0,4},{4,0},{8,12},{12,8},{16,20},{20,16},{24,28},{28,24},{1,5},{5... | collective-permute-start | bytes 1695752 | tf_op jit(solution)/shard_map/ppermute | solution.py:368
  (52 other events, 483.8 us)

commit v3 on v2

--- a/solution.py
+++ b/solution.py
@@ -997,18 +997,32 @@
             out_ref[side, i, hidden:] = add_low(late_ref[chip, late[1], :], late_in[chip, late[1], :])
 
 
-def pair_kernel(up_ref, up_in, down_ref, down_in, up_keep, up_send, down_keep, down_send):
-    up_keep[...] = add_low(up_ref[0], up_in[0])
-    up_send[...] = add_low(up_ref[1], up_in[1])
-    down_keep[...] = add_low(down_ref[0], down_in[0])
-    down_send[...] = add_low(down_ref[1], down_in[1])
-
-
-def bulk_kernel(up_ref, up_in, down_ref, down_in, bulk_ref):
+def window_call(kernel, windows, outs, name, room):
+    def spec(x, lead):
+        shape = (None,) * len(lead) + x.shape[len(lead) :]
+        return pl.BlockSpec(shape, lambda n: tuple(lead) + (0,) * (len(x.shape) - len(lead)))
+
+    return pl.pallas_call(
+        kernel,
+        grid=(1,),
+        in_specs=[spec(x, lead) for x, lead in windows],
+        out_specs=[VM] * len(outs),
+        out_shape=list(outs),
+        compiler_params=pltpu.CompilerParams(vmem_limit_bytes=room << 20),
+        name=name,
+    )(*(x for x, _ in windows))
+
+
+def second_send_kernel(up_ref, up_in, down_ref, down_in, up_send, down_send):
+    up_send[...] = add_low(up_ref[...], up_in[...])
+    down_send[...] = add_low(down_ref[...], down_in[...])
+
+
+def bulk_kernel(up_ref, up_in, up_last, down_ref, down_in, down_last, bulk_ref):
     mesh_rows, size = up_ref.shape[:2]
     for i in range(mesh_rows):
-        bulk_ref[i, :size] = add_low(up_ref[i], up_in[i])
-        bulk_ref[i, size:] = add_low(down_ref[i], down_in[i])
+        bulk_ref[i, :size] = add_low(up_ref[i], up_in[i], up_last[i])
+        bulk_ref[i, size:] = add_low(down_ref[i], down_in[i], down_last[i])
 
 
 def split_kernel(near_ref, far_ref, *outs):
@@ -1089,18 +1103,14 @@
 
 
 def unpack_kernel(here_ref, *refs, hidden, rows):
-    pieces, outs, gains_ref = refs[:8], refs[8:13], refs[13]
-    held, (turned, gains, sems) = refs[14:19], refs[19:]
+    pieces, outs, gain_refs = refs[:8], refs[8:13], refs[13:15]
+    held, (turned, gains, sems) = refs[15:20], refs[20:]
     up, down, out, given, kernel = held
     copies = [pltpu.make_async_copy(source, to, sems.at[k]) for k, (source, to) in enumerate(zip(held, outs))]
     here = here_ref[0]
     width = given.shape[2]
     taps = kernel.shape[1]
     parts = -(-taps // width)
-    for slot, ref in enumerate(pieces):
-        turned[slice_at(here, slot, hidden), :] = ref[:hidden].astype(f32)
-    up[...] = turned[...].T
-    copies[0].start()
     for slot, ref in enumerate(pieces):
         start = hidden + rows
         down[slice_at(here, slot, hidden), :] = ref[start : start + hidden].astype(f32)
@@ -1122,7 +1132,13 @@
         gain = ref[start + (3 + parts) * rows :].astype(f32)
         gains[relative_index(here, slot, 8)] = gain[:2] + gain[2:4]
     copies[4].start()
-    gains_ref[...] = sum(gains[slot] for slot in range(8))
+    total = sum(gains[slot] for slot in range(8))
+    for row, ref in enumerate(gain_refs):
+        ref[...] = total[row]
+    for slot, ref in enumerate(pieces):
+        turned[slice_at(here, slot, hidden), :] = ref[:hidden].astype(f32)
+    up[...] = turned[...].T
+    copies[0].start()
     for copy in copies:
         copy.wait()
 
@@ -1189,7 +1205,7 @@
         first_norm_forward_kernel, [((spots, width), bf16)], name="first_norm", count=2, room=10
     )(x, gain_first[None])
     first_group = chips_of(stacked(own_mixer, next_mixer))
-    other_mixers = [after(part, *first_group[1:], normed_low, tables) for part in other_mixers]
+    other_mixers = [after(part, *first_group[1:], normed_low, tables, own_feed) for part in other_mixers]
     second_group = chips_of(stacked(*other_mixers))
     feed_rows = turn(after(own_feed, *other_mixers))
     mixer = [[far(piece) for piece in pair_of(group)] for group in (first_group, second_group)]
@@ -1245,11 +1261,15 @@
     mixed_out, gspec = conv_mixed(level, received, fspec, tables)
     mixed = turn(mixed_out).reshape(channels, spots)
     filt_grad = conv_filt(gspec, uspec, tables, taps, width, length)
-    quarter = (half[0][1:], bf16)
-    up_keep, up_send, down_keep, down_send = whole_call(
-        pair_kernel, [pltpu.HBM(*quarter), quarter] * 2, name="kept_again", count=4, room=12
-    )(far(up_keep), after(up_in, mixed_out), far(down_keep), after(down_in, mixed_out))
-    up_in, down_in = swap(up_send, "dp", 4), swap(down_send, "dp", 2)
+    up_in, down_in = after(up_in, mixed_out), after(down_in, mixed_out)
+    up_send, down_send = window_call(
+        second_send_kernel,
+        [(far(up_keep), (1,)), (up_in, (1,)), (far(down_keep), (1,)), (down_in, (1,))],
+        [jax.ShapeDtypeStruct(half[0][1:], bf16)] * 2,
+        "second_send",
+        12,
+    )
+    up_last, down_last = swap(up_send, "dp", 4), swap(down_send, "dp", 2)
     rest_rows = (2 * mesh_rows + filt_parts) * rows
     rest_near, rest_far, grad_value, grad_one = whole_call(
         partial(rest_kernel, **sizes),
@@ -1262,9 +1282,14 @@
     rest = whole_call(split_kernel, [((rest_rows, width), bf16)] * 4, name="rest_kept", count=2)(
         far(rest_near), swap(rest_far, "dp", 1)
     )
-    (bulk,) = whole_call(
-        bulk_kernel, [pltpu.HBM((mesh_rows, 2 * (hidden + rows), width), bf16)], name="bulk_sum", count=4
-    )(far(up_keep), after(up_in, rest_near), far(down_keep), after(down_in, rest_near))
+    (bulk,) = window_call(
+        bulk_kernel,
+        [(far(up_keep), (0,)), (up_in, (0,)), (after(up_last, rest_near), ())]
+        + [(far(down_keep), (0,)), (down_in, (0,)), (after(down_last, rest_near), ())],
+        [pltpu.HBM((mesh_rows, 2 * (hidden + rows), width), bf16)],
+        "bulk_sum",
+        16,
+    )
     bulk = turn(bulk)
     rest = [rest[0]] + [swap(rest[chip], "dp", 2 * chip) for chip in range(1, 4)]
     grad_tokens, gain_first_grad = whole_call(
@@ -1301,11 +1326,11 @@
         room=8,
     )(after(bulk, *rest[1:]), own_filt, *rest)
     shapes = [up_weight.shape, down_weight.shape, (own_channels, width), (3, own_channels, width), kernel.shape]
-    up_grad, down_grad, out_grad, in_grad, kernel_grad, gains = pl.pallas_call(
+    up_grad, down_grad, out_grad, in_grad, kernel_grad, gain_one, gain_two = pl.pallas_call(
         partial(unpack_kernel, hidden=hidden, rows=rows),
-        out_shape=[jax.ShapeDtypeStruct(shape, f32) for shape in shapes + [(2, width)]],
+        out_shape=[jax.ShapeDtypeStruct(shape, f32) for shape in shapes + [(width,)] * 2],
         in_specs=[SM] + [VM] * 8,
-        out_specs=[pl.BlockSpec(memory_space=pl.ANY)] * 5 + [VM],
+        out_specs=[pl.BlockSpec(memory_space=pl.ANY)] * 5 + [VM] * 2,
         scratch_shapes=[pltpu.VMEM(shape, f32) for shape in shapes + [down_weight.shape, (8, 2, width)]]
         + [pltpu.SemaphoreType.DMA((5,))],
         compiler_params=pltpu.CompilerParams(vmem_limit_bytes=24 << 20),
@@ -1314,11 +1339,11 @@
     return (
         block_out[None],
         grad_tokens[None],
-        gains[0],
+        gain_one,
         in_grad.transpose(2, 0, 1),
         kernel_grad,
         out_grad,
-        gains[1],
+        gain_two,
         up_grad,
         down_grad,
     )

time: 298 us -> 298 us (level)
  transfers between devices with their start and end apart: 59 -> 59, of which waited for: 32 -> 32; matrix products, arithmetic and copies ran while one was open for 2% -> 2% of each run, Pallas kernels for 19% -> 18%
where the time goes in v3:
time: 298 us; the launch traced here: 297 us
  waiting for transfers between devices  127 us (43%)
  Pallas kernels  93.4 us (31%)
  starting transfers between devices  64.8 us (22%)
  local copies, waits for them, and re-layouts  6.93 us (2%)
  other arithmetic  3.83 us (1%)
    ppermute x56, waiting for transfers between devices, swap(): lax.ppermute(x, axis, [(i, i ^ bit) for i in range(lax.axis_size(axis))])  115 us
    ppermute x56, starting transfers between devices, swap(): lax.ppermute(x, axis, [(i, i ^ bit) for i in range(lax.axis_size(axis))])  52.6 us
    pallas_call x1, Pallas kernels, feed_forward(): pl.pallas_call(partial(feed_kernel, mesh_rows=mesh_rows), grid=(8 // FEED...  26.2 us
    all_to_all x3, starting transfers between devices, turn(): return lax.all_to_all(x, 'mp', 0, 0)  12.2 us
    all_to_all x3, waiting for transfers between devices, turn(): return lax.all_to_all(x, 'mp', 0, 0)  12.1 us
    pallas_call x1, Pallas kernels, fast_body(): whole_call(partial(first_norm_kernel, **sizes), [wide, ((1, width), f32)]...  9.12 us
    pallas_call x1, Pallas kernels, filter_slices(): whole_call(partial(filter_slices_kernel, radix=radix, channels=channels,...  8.99 us
    pallas_call x2, Pallas kernels, window_call(): pl.pallas_call(kernel, grid=(1,), in_specs=[spec(x, lead) for x, lead in...  6.44 us
  transfers between devices with their start and end apart: 59, of which 32 were waited for; matrix products, arithmetic and copies ran while one was open for 2% of the time, Pallas kernels for 18%

profile of v3, /device:TPU:0, one launch (start us, length us, event | category | flops | bytes accessed | tf_op | source)
XLA Modules:
  0.0 297.3 jit_solution(8533327886750665734)
XLA Ops:
  2.5 3.1 %collective-permute-start = (bf16[96,768]{1,0:T(8,128)(2,1)S(1)}, bf16[96,768]{1,0:T(8,128)(2,1)S(1)}, u32[]{:S(2)}, u32[]{:S(2)}) collective-permute-start(bf16[96,768]{1,0:T(8,128)(2,1)S(1)} %bitcast.57), channel_id=1, source_target_pairs={{0,1},{1,0},{2,3},{3,2},{4,5},{5,4},{6,7},{7,6},{8,9},{9,8},{10,11... | collective-permute-start | bytes 442376 | tf_op jit(solution)/shard_map/ppermute | solution.py:368
  14.1 3.8 %collective-permute-start.9 = (bf16[96,768]{1,0:T(8,128)(2,1)S(1)}, bf16[96,768]{1,0:T(8,128)(2,1)S(1)}, u32[]{:S(2)}, u32[]{:S(2)}) collective-permute-start(bf16[96,768]{1,0:T(8,128)(2,1)S(1)} %bitcast.59), channel_id=1, source_target_pairs={{0,3},{1,2},{2,1},{3,0},{4,7},{5,6},{6,5},{7,4},{8,11},{9,10},{10,... | collective-permute-start | bytes 442376 | tf_op jit(solution)/shard_map/ppermute | solution.py:368
  21.9 3.2 %collective-permute-done.2.refs_2_.refs_5_ = bf16[192,768]{1,0:T(8,128)(2,1)} collective-permute-done((bf16[192,768]{1,0:T(8,128)(2,1)S(1)}, bf16[192,768]{1,0:T(8,128)(2,1)}, u32[]{:S(2)}, u32[]{:S(2)}) %collective-permute-start.2) | collective-permute-done | bytes 294944 | tf_op jit(solution)/shard_map/ppermute | solution.py:368
  28.8 4.3 %all-to-all-start = ((bf16[4,2,96,768]{3,2,1,0:T(8,128)(2,1)}), bf16[4,2,96,768]{3,2,1,0:T(8,128)(2,1)}, u32[]{:S(2)}, u32[]{:S(2)}) async-start(bf16[4,2,96,768]{3,2,1,0:T(8,128)(2,1)} %broadcast_in_dim.36), calls=%async_computation | async-start | bytes 2359296 | tf_op jit(solution)/shard_map/all_to_all | solution.py:437
  37.8 6.7 %collective-permute-done.12.refs_11_.refs_14_ = bf16[192,768]{1,0:T(8,128)(2,1)S(1)} collective-permute-done((bf16[192,768]{1,0:T(8,128)(2,1)S(1)}, bf16[192,768]{1,0:T(8,128)(2,1)S(1)}, u32[]{:S(2)}, u32[]{:S(2)}) %collective-permute-start.12) | collective-permute-done | bytes 294944 | tf_op jit(solution)/shard_map/ppermute | solution.py:368
  44.6 5.8 %collective-permute-done.11.refs_10_.refs_13_ = bf16[192,768]{1,0:T(8,128)(2,1)S(1)} collective-permute-done((bf16[192,768]{1,0:T(8,128)(2,1)S(1)}, bf16[192,768]{1,0:T(8,128)(2,1)S(1)}, u32[]{:S(2)}, u32[]{:S(2)}) %collective-permute-start.11) | collective-permute-done | bytes 294944 | tf_op jit(solution)/shard_map/ppermute | solution.py:368
  52.6 6.3 %project.1 = (bf16[2,4,24,512]{3,2,1,0:T(8,128)(2,1)}, bf16[2,4,24,512]{3,2,1,0:T(8,128)(2,1)}, bf16[2,4,24,512]{3,2,1,0:T(8,128)(2,1)}, bf16[2,4,24,512]{3,2,1,...) custom-call(s32[1]{0:T(128)} %bitcast.level_ref.here_ref.refs_0_, ...), custom_call_target="tpu_custom_call" | custom-call | tf_op jit(solution)/shard_map/project/pallas_call | solution.py:774
  70.0 9.0 %filter_spectrum.1.refs_4_ = f32[1536,512]{1,0:T(8,128)S(1)} custom-call(s32[1]{0:T(128)} %bitcast.15.here_ref, f32[192,2048]{1,0:T(8,128)} %kernel_ref.2, s32[192,1]{1,0:T(8,128)S(1)} %copy.27.pad_ref, bf16[512,512]{1,0:T(8,128)(2,1)} %fusion.high_ref.refs_5_, bf16[512,512]{1,0:T(8,128)(2,1)} %subtract_convert_fusion.low_ref, ...), custom_call_target="tpu_custom_call" | custom-call | tf_op jit(solution)/shard_map/filter_spectrum/pallas_call | solution.py:709
  84.2 6.2 %conv_forward.1 = (bf16[192,512]{1,0:T(8,128)(2,1)S(1)}, bf16[192,512]{1,0:T(8,128)(2,1)S(1)}, bf16[192,512]{1,0:T(8,128)(2,1)S(1)}, bf16[192,512]{1,0:T(8,128)(2,1)S(1)}, bf16[1536,512]{1,0:T(8,128)(2,1)}) custom-call(s32[1]{0:T(128)} %bitcast.level_ref.here_ref.refs_0_, bf16[192,512]{1,0:T(8,128)(2,1)S(1)} %bitcast.61, ...), custom_call_target="tpu_custom_call" | custom-call | tf_op jit(solution)/shard_map/conv_forward/pallas_call | solution.py:274
  98.5 10.2 %collective-permute-done.21.refs_8_ = bf16[192,512]{1,0:T(8,128)(2,1)S(1)} collective-permute-done((bf16[192,512]{1,0:T(8,128)(2,1)S(1)}, bf16[192,512]{1,0:T(8,128)(2,1)S(1)}, u32[]{:S(2)}, u32[]{:S(2)}) %collective-permute-start.21) | collective-permute-done | bytes 196640 | tf_op jit(solution)/shard_map/ppermute | solution.py:368
  109.8 4.3 %collective-permute-done.31.refs_20_ = bf16[384,768]{1,0:T(8,128)(2,1)S(1)} collective-permute-done((bf16[384,768]{1,0:T(8,128)(2,1)S(1)}, bf16[384,768]{1,0:T(8,128)(2,1)S(1)}, u32[]{:S(2)}, u32[]{:S(2)}) %collective-permute-start.31) | collective-permute-done | bytes 589856 | tf_op jit(solution)/shard_map/ppermute | solution.py:368
  115.8 26.2 %feed_forward.1 = (bf16[768,512]{1,0:T(8,128)(2,1)S(1)}, bf16[512,768]{1,0:T(8,128)(2,1)}, f32[512,768]{1,0:T(8,128)}, bf16[512,768]{1,0:T(8,128)(2,1)S(1)}, f32...) custom-call(s32[1]{0:T(128)} %bitcast.level_ref.here_ref.refs_0_, ...), custom_call_target="tpu_custom_call" | custom-call | tf_op jit(solution)/shard_map/feed_forward/pallas_call | solution.py:894
  145.6 6.1 %collective-permute-done.35.late_in = bf16[4,192,768]{2,1,0:T(8,128)(2,1)S(1)} collective-permute-done((bf16[4,192,768]{2,1,0:T(8,128)(2,1)S(1)}, bf16[4,192,768]{2,1,0:T(8,128)(2,1)S(1)}, u32[]{:S(2)}, u32[]{:S(2)}) %collective-permute-start.35) | collective-permute-done | bytes 1179680 | tf_op jit(solution)/shard_map/ppermute | solution.py:368
  151.7 3.9 %kept.1 = (bf16[2,4,120,768]{3,2,1,0:T(8,128)(2,1)}, bf16[2,4,120,768]{3,2,1,0:T(8,128)(2,1)}, bf16[2,4,120,768]{3,2,1,0:T(8,128)(2,1)}, bf16[2,4,120,768]{3,2,1,0:T(8,128)(2,1)}) custom-call(bf16[1536,768]{1,0:T(8,128)(2,1)S(1)} %get-tuple-element.122.up_ref, bf16[1536,768]{1,0:T(8,128)(2,1)S(1)} %copy-done.12, ...), custom_call_target="tpu_custom_call" | custom-call | tf_op jit(solution)/shard_map/kept/pallas_call | solution.py:1255
  162.5 4.2 %collective-permute-done.37.refs_3_ = bf16[192,512]{1,0:T(8,128)(2,1)S(1)} collective-permute-done((bf16[192,512]{1,0:T(8,128)(2,1)S(1)}, bf16[192,512]{1,0:T(8,128)(2,1)S(1)}, u32[]{:S(2)}, u32[]{:S(2)}) %collective-permute-start.37) | collective-permute-done | bytes 196640 | tf_op jit(solution)/shard_map/ppermute | solution.py:368
  166.7 11.6 %collective-permute-done.36.refs_2_ = bf16[192,512]{1,0:T(8,128)(2,1)S(1)} collective-permute-done((bf16[192,512]{1,0:T(8,128)(2,1)S(1)}, bf16[192,512]{1,0:T(8,128)(2,1)S(1)}, u32[]{:S(2)}, u32[]{:S(2)}) %collective-permute-start.36) | collective-permute-done | bytes 196640 | tf_op jit(solution)/shard_map/ppermute | solution.py:368
  178.3 6.4 %conv_mixed.1 = (bf16[4,192,512]{2,1,0:T(8,128)(2,1)}, bf16[1536,512]{1,0:T(8,128)(2,1)}) custom-call(s32[1]{0:T(128)} %bitcast.level_ref.here_ref.refs_0_, bf16[192,512]{1,0:T(8,128)(2,1)S(1)} %get-tuple-element.120.refs_0_, bf16[192,512]{1,0:T(8,128)(2,1)S(1)} %collective-permute-done.33.refs_1_, bf16[192,512]{1,0:T(8,128)(2,1)S(1)} %collective-permute-done.36.refs_2_, ...), custom_call_target="tpu_custom_call" | custom-call | tf_op jit(solution)/shard_map/conv_mixed/pallas_call | solution.py:293
  184.7 4.4 %all-to-all-start.1 = ((bf16[4,192,512]{2,1,0:T(8,128)(2,1)}), bf16[4,192,512]{2,1,0:T(8,128)(2,1)}, u32[]{:S(2)}, u32[]{:S(2)}) async-start(bf16[4,192,512]{2,1,0:T(8,128)(2,1)} %get-tuple-element.136), calls=%async_computation.1 | async-start | bytes 1572864 | tf_op jit(solution)/shard_map/all_to_all | solution.py:437
  191.3 3.2 %second_send.1 = (bf16[4,120,768]{2,1,0:T(8,128)(2,1)}, bf16[4,120,768]{2,1,0:T(8,128)(2,1)}) custom-call(bf16[2,4,120,768]{3,2,1,0:T(8,128)(2,1)} %get-tuple-element.130.up_ref, bf16[2,4,120,768]{3,2,1,0:T(8,128)(2,1)S(1)} %collective-permute-done.38.up_in, bf16[2,4,120,768]{3,2,1,0:T(8,128)(2,1)} %get-tuple-element.146.down_ref, ...), custom_call_target="tpu_custom_call" | custom-call | tf_op jit(solution)/shard_map/second_send/pallas_call | solution.py:1005
  196.6 3.1 %conv_filt.1.filt_ref = f32[3,192,768]{2,1,0:T(8,128)S(1)} custom-call(bf16[1536,512]{1,0:T(8,128)(2,1)S(1)} %copy-done.14, bf16[1536,512]{1,0:T(8,128)(2,1)S(1)} %copy-done.13, bf16[512,512]{1,0:T(8,128)(2,1)S(1)} %copy-done.2, f32[2,8,256]{2,1,0:T(8,128)S(1)} %copy-done.17), custom_call_target="tpu_custom_call" | custom-call | tf_op jit(solution)/shard_map/conv_filt/pallas_call | solution.py:313
  199.7 9.9 %all-to-all-done.1 = bf16[4,192,512]{2,1,0:T(8,128)(2,1)} async-done(((bf16[4,192,512]{2,1,0:T(8,128)(2,1)}), bf16[4,192,512]{2,1,0:T(8,128)(2,1)}, u32[]{:S(2)}, u32[]{:S(2)}) %all-to-all-start.1) | async-done | bytes 786464 | tf_op jit(solution)/shard_map/all_to_all | solution.py:437
  209.5 5.8 %rest_grads.1 = (bf16[4,264,768]{2,1,0:T(8,128)(2,1)}, bf16[4,264,768]{2,1,0:T(8,128)(2,1)}, bf16[768,512]{1,0:T(8,128)(2,1)}, bf16[768,512]{1,0:T(8,128)(2,1)}) custom-call(bf16[768,512]{1,0:T(8,128)(2,1)} %bitcast.23.mixed_ref, f32[768,512]{1,0:T(8,128)} %bitcast.64, f32[768,512]{1,0:T(8,128)} %bitcast.65, bf16[512,768]{1,0:T(8,128)(2,1)} %copy-done.3, ...), custom_call_target="tpu_custom_call" | custom-call | tf_op jit(solution)/shard_map/rest_grads/pallas_call | solution.py:1274
  215.4 3.2 %bulk_sum.1 = bf16[4,240,768]{2,1,0:T(8,128)(2,1)} custom-call(bf16[2,4,120,768]{3,2,1,0:T(8,128)(2,1)} %get-tuple-element.130.up_ref, bf16[2,4,120,768]{3,2,1,0:T(8,128)(2,1)S(1)} %copy-done.7, bf16[4,120,768]{2,1,0:T(8,128)(2,1)S(1)} %collective-permute-done.40.up_last, bf16[2,4,120,768]{3,2,1,0:T(8,128)(2,1)} %get-tuple-element.146.down_ref, ...), custom_call_target="tpu_custom_call" | custom-call | tf_op jit(solution)/shard_map/bulk_sum/pallas_call | solution.py:1005
  218.6 3.6 %all-to-all-start.2 = ((bf16[4,240,768]{2,1,0:T(8,128)(2,1)}), bf16[4,240,768]{2,1,0:T(8,128)(2,1)S(1)}, u32[]{:S(2)}, u32[]{:S(2)}) async-start(bf16[4,240,768]{2,1,0:T(8,128)(2,1)} %bulk_sum.1), calls=%async_computation.2 | async-start | bytes 2949120 | tf_op jit(solution)/shard_map/all_to_all | solution.py:437
  222.2 3.7 %collective-permute-done.42.far_ref = bf16[4,264,768]{2,1,0:T(8,128)(2,1)S(1)} collective-permute-done((bf16[4,264,768]{2,1,0:T(8,128)(2,1)}, bf16[4,264,768]{2,1,0:T(8,128)(2,1)S(1)}, u32[]{:S(2)}, u32[]{:S(2)}) %collective-permute-start.42) | collective-permute-done | bytes 1622048 | tf_op jit(solution)/shard_map/ppermute | solution.py:368
  231.3 9.1 %first_norm_back.1 = (f32[512,768]{1,0:T(8,128)}, f32[1,768]{1,0:T(1,128)S(1)}) custom-call(s32[1]{0:T(128)} %bitcast.level_ref.here_ref.refs_0_, bf16[4,192,512]{2,1,0:T(8,128)(2,1)} %bitcast.68, bf16[4,192,512]{2,1,0:T(8,128)(2,1)} %bitcast.69, bf16[4,192,512]{2,1,0:T(8,128)(2,1)} %bitcast.62, bf16[192,768]{1,0:T(8,128)(2,1)} %bitcast.50, ...), custom_call_target="tpu_custom_call" | custom-call | tf_op jit(solution)/shard_map/first_norm_back/pallas_call | solution.py:1295
  240.4 8.8 %collective-permute-done.44.p2 = bf16[264,768]{1,0:T(8,128)(2,1)S(1)} collective-permute-done((bf16[264,768]{1,0:T(8,128)(2,1)S(1)}, bf16[264,768]{1,0:T(8,128)(2,1)S(1)}, u32[]{:S(2)}, u32[]{:S(2)}) %collective-permute-start.44) | collective-permute-done | bytes 405536 | tf_op jit(solution)/shard_map/ppermute | solution.py:368
  254.0 3.7 %collective-permute-done.46.refs_1_ = bf16[56,768]{1,0:T(8,128)(2,1)S(1)} collective-permute-done((bf16[56,768]{1,0:T(8,128)(2,1)S(1)}, bf16[56,768]{1,0:T(8,128)(2,1)S(1)}, u32[]{:S(2)}, u32[]{:S(2)}) %collective-permute-start.46) | collective-permute-done | bytes 86048 | tf_op jit(solution)/shard_map/ppermute | solution.py:368
  257.7 5.3 %collective-permute-done.47.refs_2_ = bf16[56,768]{1,0:T(8,128)(2,1)S(1)} collective-permute-done((bf16[56,768]{1,0:T(8,128)(2,1)S(1)}, bf16[56,768]{1,0:T(8,128)(2,1)S(1)}, u32[]{:S(2)}, u32[]{:S(2)}) %collective-permute-start.47) | collective-permute-done | bytes 86048 | tf_op jit(solution)/shard_map/ppermute | solution.py:368
  266.9 13.1 %collective-permute-done.51.refs_3_ = bf16[368,768]{1,0:T(8,128)(2,1)S(1)} collective-permute-done((bf16[368,768]{1,0:T(8,128)(2,1)S(1)}, bf16[368,768]{1,0:T(8,128)(2,1)S(1)}, u32[]{:S(2)}, u32[]{:S(2)}) %collective-permute-start.51) | collective-permute-done | bytes 565280 | tf_op jit(solution)/shard_map/ppermute | solution.py:368
  280.1 9.2 %collective-permute-done.50.refs_2_ = bf16[368,768]{1,0:T(8,128)(2,1)S(1)} collective-permute-done((bf16[368,768]{1,0:T(8,128)(2,1)S(1)}, bf16[368,768]{1,0:T(8,128)(2,1)S(1)}, u32[]{:S(2)}, u32[]{:S(2)}) %collective-permute-start.50) | collective-permute-done | bytes 565280 | tf_op jit(solution)/shard_map/ppermute | solution.py:368
  292.0 5.0 %unpack.1 = (f32[768,768]{1,0:T(8,128)}, f32[768,768]{1,0:T(8,128)}, f32[192,768]{1,0:T(8,128)}, f32[3,192,768]{2,1,0:T(8,128)}, f32[192,2048]{1,0:T(8,128)}, /*index=5*/f32[768]{0:T(1024)}, f32[768]{0:T(1024)}) custom-call(s32[1]{0:T(128)} %bitcast.15.here_ref, bf16[368,768]{1,0:T(8,128)(2,1)S(1)} %mesh_sum.1.refs_0_, ...), custom_call_target="tpu_custom_call" | custom-call | tf_op jit(solution)/shard_map/unpack/pallas_call | solution.py:1329
  (184 shorter events, 83.6 us)
Async XLA Ops:
  9.4 12.5 %collective-permute-start.3 = (bf16[192,768]{1,0:T(8,128)(2,1)S(1)}, bf16[192,768]{1,0:T(8,128)(2,1)S(1)}, u32[]{:S(2)}, u32[]{:S(2)}) collective-permute-start(bf16[192,768]{1,0:T(8,128)(2,1)S(1)} %bitcast.45), channel_id=1, source_target_pairs={{0,24},{4,28},{8,16},{12,20},{16,8},{20,12},{24,0},{28,4},{1,25},{... | collective-permute-start | bytes 884744 | tf_op jit(solution)/shard_map/ppermute | solution.py:368
  12.1 13.0 %collective-permute-start.2 = (bf16[192,768]{1,0:T(8,128)(2,1)S(1)}, bf16[192,768]{1,0:T(8,128)(2,1)}, u32[]{:S(2)}, u32[]{:S(2)}) collective-permute-start(bf16[192,768]{1,0:T(8,128)(2,1)S(1)} %bitcast.46), channel_id=1, source_target_pairs={{0,16},{4,20},{8,24},{12,28},{16,0},{20,4},{24,8},{28,12},{1,17},{... | collective-permute-start | bytes 884744 | tf_op jit(solution)/shard_map/ppermute | solution.py:368
  12.6 12.6 %collective-permute-start.1 = (bf16[192,768]{1,0:T(8,128)(2,1)S(1)}, bf16[192,768]{1,0:T(8,128)(2,1)}, u32[]{:S(2)}, u32[]{:S(2)}) collective-permute-start(bf16[192,768]{1,0:T(8,128)(2,1)S(1)} %bitcast.47), channel_id=1, source_target_pairs={{0,8},{4,12},{8,0},{12,4},{16,24},{20,28},{24,16},{28,20},{1,9},{5... | collective-permute-start | bytes 884744 | tf_op jit(solution)/shard_map/ppermute | solution.py:368
  28.8 32.3 %all-to-all-start = ((bf16[4,2,96,768]{3,2,1,0:T(8,128)(2,1)}), bf16[4,2,96,768]{3,2,1,0:T(8,128)(2,1)}, u32[]{:S(2)}, u32[]{:S(2)}) async-start(bf16[4,2,96,768]{3,2,1,0:T(8,128)(2,1)} %broadcast_in_dim.36), calls=%async_computation | async-start | bytes 2359296 | tf_op jit(solution)/shard_map/all_to_all | solution.py:437
  36.3 14.1 %collective-permute-start.11 = (bf16[192,768]{1,0:T(8,128)(2,1)S(1)}, bf16[192,768]{1,0:T(8,128)(2,1)S(1)}, u32[]{:S(2)}, u32[]{:S(2)}) collective-permute-start(bf16[192,768]{1,0:T(8,128)(2,1)S(1)} %bitcast.52), channel_id=1, source_target_pairs={{0,16},{4,20},{8,24},{12,28},{16,0},{20,4},{24,8},{28,12},{1,17},{... | collective-permute-start | bytes 884744 | tf_op jit(solution)/shard_map/ppermute | solution.py:368
  36.8 13.7 %collective-permute-start.10 = (bf16[192,768]{1,0:T(8,128)(2,1)S(1)}, bf16[192,768]{1,0:T(8,128)(2,1)S(1)}, u32[]{:S(2)}, u32[]{:S(2)}) collective-permute-start(bf16[192,768]{1,0:T(8,128)(2,1)S(1)} %bitcast.53), channel_id=1, source_target_pairs={{0,8},{4,12},{8,0},{12,4},{16,24},{20,28},{24,16},{28,20},{1,9},{5... | collective-permute-start | bytes 884744 | tf_op jit(solution)/shard_map/ppermute | solution.py:368
  37.3 13.6 %collective-permute-start.13 = (bf16[192,768]{1,0:T(8,128)(2,1)S(1)}, bf16[192,768]{1,0:T(8,128)(2,1)S(1)}, u32[]{:S(2)}, u32[]{:S(2)}) collective-permute-start(bf16[192,768]{1,0:T(8,128)(2,1)S(1)} %bitcast.54), channel_id=1, source_target_pairs={{0,4},{4,0},{8,12},{12,8},{16,20},{20,16},{24,28},{28,24},{1,5},{5... | collective-permute-start | bytes 884744 | tf_op jit(solution)/shard_map/ppermute | solution.py:368
  37.3 13.6 %collective-permute-start.5 = (bf16[192,768]{1,0:T(8,128)(2,1)}, bf16[192,768]{1,0:T(8,128)(2,1)}, u32[]{:S(2)}, u32[]{:S(2)}) collective-permute-start(bf16[192,768]{1,0:T(8,128)(2,1)} %collective-permute-done.1.refs_1_.refs_4_), channel_id=1, source_target_pairs={{0,4},{4,0},{8,12},{12,8},{16,20},{20,16},{24,28},{28,24},{1,5},{5... | collective-permute-start | bytes 884744 | tf_op jit(solution)/shard_map/ppermute | solution.py:368
  62.4 20.1 %collective-permute-start.24 = (bf16[384,768]{1,0:T(8,128)(2,1)S(1)}, bf16[384,768]{1,0:T(8,128)(2,1)S(1)}, u32[]{:S(2)}, u32[]{:S(2)}) collective-permute-start(bf16[384,768]{1,0:T(8,128)(2,1)S(1)} %bitcast.37), channel_id=1, source_target_pairs={{0,16},{4,20},{8,24},{12,28},{16,0},{20,4},{24,8},{28,12},{1,17},{... | collective-permute-start | bytes 1769480 | tf_op jit(solution)/shard_map/ppermute | solution.py:368
  64.0 18.5 %collective-permute-start.23 = (bf16[384,768]{1,0:T(8,128)(2,1)S(1)}, bf16[384,768]{1,0:T(8,128)(2,1)S(1)}, u32[]{:S(2)}, u32[]{:S(2)}) collective-permute-start(bf16[384,768]{1,0:T(8,128)(2,1)S(1)} %bitcast.41), channel_id=1, source_target_pairs={{0,8},{4,12},{8,0},{12,4},{16,24},{20,28},{24,16},{28,20},{1,9},{5... | collective-permute-start | bytes 1769480 | tf_op jit(solution)/shard_map/ppermute | solution.py:368
  65.5 14.2 %collective-permute-start.17 = (bf16[192,512]{1,0:T(8,128)(2,1)}, bf16[192,512]{1,0:T(8,128)(2,1)S(1)}, u32[]{:S(2)}, u32[]{:S(2)}) collective-permute-start(bf16[192,512]{1,0:T(8,128)(2,1)} %bitcast.14), channel_id=1, source_target_pairs={{0,1},{1,0},{2,3},{3,2},{4,5},{5,4},{6,7},{7,6},{8,9},{9,8},{10,11... | collective-permute-start | bytes 589832 | tf_op jit(solution)/shard_map/ppermute | solution.py:368
  65.5 17.0 %collective-permute-start.18 = (bf16[192,512]{1,0:T(8,128)(2,1)}, bf16[192,512]{1,0:T(8,128)(2,1)S(1)}, u32[]{:S(2)}, u32[]{:S(2)}) collective-permute-start(bf16[192,512]{1,0:T(8,128)(2,1)} %bitcast.17), channel_id=1, source_target_pairs={{0,2},{1,3},{2,0},{3,1},{4,6},{5,7},{6,4},{7,5},{8,10},{9,11},{10,... | collective-permute-start | bytes 589832 | tf_op jit(solution)/shard_map/ppermute | solution.py:368
  67.5 15.0 %collective-permute-start.19 = (bf16[192,512]{1,0:T(8,128)(2,1)}, bf16[192,512]{1,0:T(8,128)(2,1)S(1)}, u32[]{:S(2)}, u32[]{:S(2)}) collective-permute-start(bf16[192,512]{1,0:T(8,128)(2,1)} %bitcast.18), channel_id=1, source_target_pairs={{0,3},{1,2},{2,1},{3,0},{4,7},{5,6},{6,5},{7,4},{8,11},{9,10},{10,... | collective-permute-start | bytes 589832 | tf_op jit(solution)/shard_map/ppermute | solution.py:368
  82.6 26.1 %collective-permute-start.25 = (bf16[2,384,768]{2,1,0:T(8,128)(2,1)S(1)}, bf16[2,384,768]{2,1,0:T(8,128)(2,1)S(1)}, u32[]{:S(2)}, u32[]{:S(2)}) collective-permute-start(bf16[2,384,768]{2,1,0:T(8,128)(2,1)S(1)} %get-tuple-element.115), channel_id=1, source_target_pairs={{0,16},{4,20},{8,24},{12,28},{16,0},{20,4},{24,8},{28,12},{1,17},{... | collective-permute-start | bytes 3538952 | tf_op jit(solution)/shard_map/ppermute | solution.py:368
  83.6 25.1 %collective-permute-start.27 = (bf16[2,384,768]{2,1,0:T(8,128)(2,1)S(1)}, bf16[2,384,768]{2,1,0:T(8,128)(2,1)S(1)}, u32[]{:S(2)}, u32[]{:S(2)}) collective-permute-start(bf16[2,384,768]{2,1,0:T(8,128)(2,1)S(1)} %get-tuple-element.117), channel_id=1, source_target_pairs={{0,8},{4,12},{8,0},{12,4},{16,24},{20,28},{24,16},{28,20},{1,9},{5... | collective-permute-start | bytes 3538952 | tf_op jit(solution)/shard_map/ppermute | solution.py:368
  93.2 15.5 %collective-permute-start.21 = (bf16[192,512]{1,0:T(8,128)(2,1)S(1)}, bf16[192,512]{1,0:T(8,128)(2,1)S(1)}, u32[]{:S(2)}, u32[]{:S(2)}) collective-permute-start(bf16[192,512]{1,0:T(8,128)(2,1)S(1)} %get-tuple-element.108), channel_id=1, source_target_pairs={{0,2},{1,3},{2,0},{3,1},{4,6},{5,7},{6,4},{7,5},{8,10},{9,11},{10,... | collective-permute-start | bytes 589832 | tf_op jit(solution)/shard_map/ppermute | solution.py:368
  94.1 14.6 %collective-permute-start.22 = (bf16[192,512]{1,0:T(8,128)(2,1)S(1)}, bf16[192,512]{1,0:T(8,128)(2,1)S(1)}, u32[]{:S(2)}, u32[]{:S(2)}) collective-permute-start(bf16[192,512]{1,0:T(8,128)(2,1)S(1)} %get-tuple-element.109), channel_id=1, source_target_pairs={{0,3},{1,2},{2,1},{3,0},{4,7},{5,6},{6,5},{7,4},{8,11},{9,10},{10,... | collective-permute-start | bytes 589832 | tf_op jit(solution)/shard_map/ppermute | solution.py:368
  155.5 34.5 %collective-permute-start.38 = (bf16[2,4,120,768]{3,2,1,0:T(8,128)(2,1)}, bf16[2,4,120,768]{3,2,1,0:T(8,128)(2,1)S(1)}, u32[]{:S(2)}, u32[]{:S(2)}) collective-permute-start(bf16[2,4,120,768]{3,2,1,0:T(8,128)(2,1)} %get-tuple-element.144), channel_id=1, source_target_pairs={{0,8},{4,12},{8,0},{12,4},{16,24},{20,28},{24,16},{28,20},{1,9},{5... | collective-permute-start | bytes 4423688 | tf_op jit(solution)/shard_map/ppermute | solution.py:368
  157.0 34.3 %collective-permute-start.39 = (bf16[2,4,120,768]{3,2,1,0:T(8,128)(2,1)}, bf16[2,4,120,768]{3,2,1,0:T(8,128)(2,1)S(1)}, u32[]{:S(2)}, u32[]{:S(2)}) collective-permute-start(bf16[2,4,120,768]{3,2,1,0:T(8,128)(2,1)} %get-tuple-element.147), channel_id=1, source_target_pairs={{0,16},{4,20},{8,24},{12,28},{16,0},{20,4},{24,8},{28,12},{1,17},{... | collective-permute-start | bytes 4423688 | tf_op jit(solution)/shard_map/ppermute | solution.py:368
  159.4 18.9 %collective-permute-start.36 = (bf16[192,512]{1,0:T(8,128)(2,1)S(1)}, bf16[192,512]{1,0:T(8,128)(2,1)S(1)}, u32[]{:S(2)}, u32[]{:S(2)}) collective-permute-start(bf16[192,512]{1,0:T(8,128)(2,1)S(1)} %get-tuple-element.132), channel_id=1, source_target_pairs={{0,2},{1,3},{2,0},{3,1},{4,6},{5,7},{6,4},{7,5},{8,10},{9,11},{10,... | collective-permute-start | bytes 589832 | tf_op jit(solution)/shard_map/ppermute | solution.py:368
  162.0 16.4 %collective-permute-start.33 = (bf16[192,512]{1,0:T(8,128)(2,1)S(1)}, bf16[192,512]{1,0:T(8,128)(2,1)S(1)}, u32[]{:S(2)}, u32[]{:S(2)}) collective-permute-start(bf16[192,512]{1,0:T(8,128)(2,1)S(1)} %get-tuple-element.121), channel_id=1, source_target_pairs={{0,1},{1,0},{2,3},{3,2},{4,5},{5,4},{6,7},{7,6},{8,9},{9,8},{10,11... | collective-permute-start | bytes 589832 | tf_op jit(solution)/shard_map/ppermute | solution.py:368
  184.7 24.8 %all-to-all-start.1 = ((bf16[4,192,512]{2,1,0:T(8,128)(2,1)}), bf16[4,192,512]{2,1,0:T(8,128)(2,1)}, u32[]{:S(2)}, u32[]{:S(2)}) async-start(bf16[4,192,512]{2,1,0:T(8,128)(2,1)} %get-tuple-element.136), calls=%async_computation.1 | async-start | bytes 1572864 | tf_op jit(solution)/shard_map/all_to_all | solution.py:437
  194.5 20.8 %collective-permute-start.40 = (bf16[4,120,768]{2,1,0:T(8,128)(2,1)}, bf16[4,120,768]{2,1,0:T(8,128)(2,1)S(1)}, u32[]{:S(2)}, u32[]{:S(2)}) collective-permute-start(bf16[4,120,768]{2,1,0:T(8,128)(2,1)} %get-tuple-element.149), channel_id=1, source_target_pairs={{0,16},{4,20},{8,24},{12,28},{16,0},{20,4},{24,8},{28,12},{1,17},{... | collective-permute-start | bytes 2211848 | tf_op jit(solution)/shard_map/ppermute | solution.py:368
  195.4 20.0 %collective-permute-start.41 = (bf16[4,120,768]{2,1,0:T(8,128)(2,1)}, bf16[4,120,768]{2,1,0:T(8,128)(2,1)}, u32[]{:S(2)}, u32[]{:S(2)}) collective-permute-start(bf16[4,120,768]{2,1,0:T(8,128)(2,1)} %get-tuple-element.152), channel_id=1, source_target_pairs={{0,8},{4,12},{8,0},{12,4},{16,24},{20,28},{24,16},{28,20},{1,9},{5... | collective-permute-start | bytes 2211848 | tf_op jit(solution)/shard_map/ppermute | solution.py:368
  218.6 44.5 %all-to-all-start.2 = ((bf16[4,240,768]{2,1,0:T(8,128)(2,1)}), bf16[4,240,768]{2,1,0:T(8,128)(2,1)S(1)}, u32[]{:S(2)}, u32[]{:S(2)}) async-start(bf16[4,240,768]{2,1,0:T(8,128)(2,1)} %bulk_sum.1), calls=%async_computation.2 | async-start | bytes 2949120 | tf_op jit(solution)/shard_map/all_to_all | solution.py:437
  227.7 12.7 %collective-permute-start.43 = (bf16[264,768]{1,0:T(8,128)(2,1)S(1)}, bf16[264,768]{1,0:T(8,128)(2,1)S(1)}, u32[]{:S(2)}, u32[]{:S(2)}) collective-permute-start(bf16[264,768]{1,0:T(8,128)(2,1)S(1)} %get-tuple-element.156), channel_id=1, source_target_pairs={{0,8},{4,12},{8,0},{12,4},{16,24},{20,28},{24,16},{28,20},{1,9},{5... | collective-permute-start | bytes 1216520 | tf_op jit(solution)/shard_map/ppermute | solution.py:368
  229.3 19.8 %collective-permute-start.44 = (bf16[264,768]{1,0:T(8,128)(2,1)S(1)}, bf16[264,768]{1,0:T(8,128)(2,1)S(1)}, u32[]{:S(2)}, u32[]{:S(2)}) collective-permute-start(bf16[264,768]{1,0:T(8,128)(2,1)S(1)} %get-tuple-element.158), channel_id=1, source_target_pairs={{0,16},{4,20},{8,24},{12,28},{16,0},{20,4},{24,8},{28,12},{1,17},{... | collective-permute-start | bytes 1216520 | tf_op jit(solution)/shard_map/ppermute | solution.py:368
  229.8 19.3 %collective-permute-start.45 = (bf16[264,768]{1,0:T(8,128)(2,1)S(1)}, bf16[264,768]{1,0:T(8,128)(2,1)S(1)}, u32[]{:S(2)}, u32[]{:S(2)}) collective-permute-start(bf16[264,768]{1,0:T(8,128)(2,1)S(1)} %get-tuple-element.160), channel_id=1, source_target_pairs={{0,24},{4,28},{8,16},{12,20},{16,8},{20,12},{24,0},{28,4},{1,25},{... | collective-permute-start | bytes 1216520 | tf_op jit(solution)/shard_map/ppermute | solution.py:368
  263.4 16.7 %collective-permute-start.51 = (bf16[368,768]{1,0:T(8,128)(2,1)S(1)}, bf16[368,768]{1,0:T(8,128)(2,1)S(1)}, u32[]{:S(2)}, u32[]{:S(2)}) collective-permute-start(bf16[368,768]{1,0:T(8,128)(2,1)S(1)} %mesh_sum.1.refs_0_), channel_id=1, source_target_pairs={{0,24},{4,28},{8,16},{12,20},{16,8},{20,12},{24,0},{28,4},{1,25},{... | collective-permute-start | bytes 1695752 | tf_op jit(solution)/shard_map/ppermute | solution.py:368
  264.9 24.3 %collective-permute-start.50 = (bf16[368,768]{1,0:T(8,128)(2,1)S(1)}, bf16[368,768]{1,0:T(8,128)(2,1)S(1)}, u32[]{:S(2)}, u32[]{:S(2)}) collective-permute-start(bf16[368,768]{1,0:T(8,128)(2,1)S(1)} %mesh_sum.1.refs_0_), channel_id=1, source_target_pairs={{0,16},{4,20},{8,24},{12,28},{16,0},{20,4},{24,8},{28,12},{1,17},{... | collective-permute-start | bytes 1695752 | tf_op jit(solution)/shard_map/ppermute | solution.py:368
  266.4 22.9 %collective-permute-start.49 = (bf16[368,768]{1,0:T(8,128)(2,1)S(1)}, bf16[368,768]{1,0:T(8,128)(2,1)S(1)}, u32[]{:S(2)}, u32[]{:S(2)}) collective-permute-start(bf16[368,768]{1,0:T(8,128)(2,1)S(1)} %mesh_sum.1.refs_0_), channel_id=1, source_target_pairs={{0,8},{4,12},{8,0},{12,4},{16,24},{20,28},{24,16},{28,20},{1,9},{5... | collective-permute-start | bytes 1695752 | tf_op jit(solution)/shard_map/ppermute | solution.py:368
  266.9 22.9 %collective-permute-start.52 = (bf16[368,768]{1,0:T(8,128)(2,1)S(1)}, bf16[368,768]{1,0:T(8,128)(2,1)S(1)}, u32[]{:S(2)}, u32[]{:S(2)}) collective-permute-start(bf16[368,768]{1,0:T(8,128)(2,1)S(1)} %mesh_sum.1.refs_0_), channel_id=1, source_target_pairs={{0,4},{4,0},{8,12},{12,8},{16,20},{20,16},{24,28},{28,24},{1,5},{5... | collective-permute-start | bytes 1695752 | tf_op jit(solution)/shard_map/ppermute | solution.py:368
  (58 other events, 520.2 us)

commit v4 on v3

--- a/solution.py
+++ b/solution.py
@@ -1112,6 +1112,10 @@
     taps = kernel.shape[1]
     parts = -(-taps // width)
     for slot, ref in enumerate(pieces):
+        turned[slice_at(here, slot, hidden), :] = ref[:hidden].astype(f32)
+    up[...] = turned[...].T
+    copies[0].start()
+    for slot, ref in enumerate(pieces):
         start = hidden + rows
         down[slice_at(here, slot, hidden), :] = ref[start : start + hidden].astype(f32)
     copies[1].start()
@@ -1135,10 +1139,6 @@
     total = sum(gains[slot] for slot in range(8))
     for row, ref in enumerate(gain_refs):
         ref[...] = total[row]
-    for slot, ref in enumerate(pieces):
-        turned[slice_at(here, slot, hidden), :] = ref[:hidden].astype(f32)
-    up[...] = turned[...].T
-    copies[0].start()
     for copy in copies:
         copy.wait()
 

time: 298 us -> 298 us (level)
  no operation moved by 1% of the time
where the time goes in v4:
time: 298 us; the launch traced here: 297 us
  waiting for transfers between devices  127 us (43%)
  Pallas kernels  93.3 us (31%)
  starting transfers between devices  64.8 us (22%)
  local copies, waits for them, and re-layouts  6.93 us (2%)
  other arithmetic  3.83 us (1%)
    ppermute x56, waiting for transfers between devices, swap(): lax.ppermute(x, axis, [(i, i ^ bit) for i in range(lax.axis_size(axis))])  115 us
    ppermute x56, starting transfers between devices, swap(): lax.ppermute(x, axis, [(i, i ^ bit) for i in range(lax.axis_size(axis))])  52.6 us
    pallas_call x1, Pallas kernels, feed_forward(): pl.pallas_call(partial(feed_kernel, mesh_rows=mesh_rows), grid=(8 // FEED...  26.2 us
    all_to_all x3, starting transfers between devices, turn(): return lax.all_to_all(x, 'mp', 0, 0)  12.2 us
    all_to_all x3, waiting for transfers between devices, turn(): return lax.all_to_all(x, 'mp', 0, 0)  12.1 us
    pallas_call x1, Pallas kernels, fast_body(): whole_call(partial(first_norm_kernel, **sizes), [wide, ((1, width), f32)]...  9.12 us
    pallas_call x1, Pallas kernels, filter_slices(): whole_call(partial(filter_slices_kernel, radix=radix, channels=channels,...  8.99 us
    pallas_call x2, Pallas kernels, window_call(): pl.pallas_call(kernel, grid=(1,), in_specs=[spec(x, lead) for x, lead in...  6.44 us
  transfers between devices with their start and end apart: 59, of which 32 were waited for; matrix products, arithmetic and copies ran while one was open for 2% of the time, Pallas kernels for 18%

profile of v4, /device:TPU:0, one launch (start us, length us, event | category | flops | bytes accessed | tf_op | source)
XLA Modules:
  0.0 297.2 jit_solution(9784314310071284880)
XLA Ops:
  2.5 3.1 %collective-permute-start = (bf16[96,768]{1,0:T(8,128)(2,1)S(1)}, bf16[96,768]{1,0:T(8,128)(2,1)S(1)}, u32[]{:S(2)}, u32[]{:S(2)}) collective-permute-start(bf16[96,768]{1,0:T(8,128)(2,1)S(1)} %bitcast.57), channel_id=1, source_target_pairs={{0,1},{1,0},{2,3},{3,2},{4,5},{5,4},{6,7},{7,6},{8,9},{9,8},{10,11... | collective-permute-start | bytes 442376 | tf_op jit(solution)/shard_map/ppermute | solution.py:368
  14.1 3.8 %collective-permute-start.9 = (bf16[96,768]{1,0:T(8,128)(2,1)S(1)}, bf16[96,768]{1,0:T(8,128)(2,1)S(1)}, u32[]{:S(2)}, u32[]{:S(2)}) collective-permute-start(bf16[96,768]{1,0:T(8,128)(2,1)S(1)} %bitcast.59), channel_id=1, source_target_pairs={{0,3},{1,2},{2,1},{3,0},{4,7},{5,6},{6,5},{7,4},{8,11},{9,10},{10,... | collective-permute-start | bytes 442376 | tf_op jit(solution)/shard_map/ppermute | solution.py:368
  21.9 3.2 %collective-permute-done.2.refs_2_.refs_5_ = bf16[192,768]{1,0:T(8,128)(2,1)} collective-permute-done((bf16[192,768]{1,0:T(8,128)(2,1)S(1)}, bf16[192,768]{1,0:T(8,128)(2,1)}, u32[]{:S(2)}, u32[]{:S(2)}) %collective-permute-start.2) | collective-permute-done | bytes 294944 | tf_op jit(solution)/shard_map/ppermute | solution.py:368
  28.8 4.3 %all-to-all-start = ((bf16[4,2,96,768]{3,2,1,0:T(8,128)(2,1)}), bf16[4,2,96,768]{3,2,1,0:T(8,128)(2,1)}, u32[]{:S(2)}, u32[]{:S(2)}) async-start(bf16[4,2,96,768]{3,2,1,0:T(8,128)(2,1)} %broadcast_in_dim.36), calls=%async_computation | async-start | bytes 2359296 | tf_op jit(solution)/shard_map/all_to_all | solution.py:437
  37.8 6.7 %collective-permute-done.12.refs_11_.refs_14_ = bf16[192,768]{1,0:T(8,128)(2,1)S(1)} collective-permute-done((bf16[192,768]{1,0:T(8,128)(2,1)S(1)}, bf16[192,768]{1,0:T(8,128)(2,1)S(1)}, u32[]{:S(2)}, u32[]{:S(2)}) %collective-permute-start.12) | collective-permute-done | bytes 294944 | tf_op jit(solution)/shard_map/ppermute | solution.py:368
  44.6 5.8 %collective-permute-done.11.refs_10_.refs_13_ = bf16[192,768]{1,0:T(8,128)(2,1)S(1)} collective-permute-done((bf16[192,768]{1,0:T(8,128)(2,1)S(1)}, bf16[192,768]{1,0:T(8,128)(2,1)S(1)}, u32[]{:S(2)}, u32[]{:S(2)}) %collective-permute-start.11) | collective-permute-done | bytes 294944 | tf_op jit(solution)/shard_map/ppermute | solution.py:368
  52.6 6.3 %project.1 = (bf16[2,4,24,512]{3,2,1,0:T(8,128)(2,1)}, bf16[2,4,24,512]{3,2,1,0:T(8,128)(2,1)}, bf16[2,4,24,512]{3,2,1,0:T(8,128)(2,1)}, bf16[2,4,24,512]{3,2,1,...) custom-call(s32[1]{0:T(128)} %bitcast.level_ref.here_ref.refs_0_, ...), custom_call_target="tpu_custom_call" | custom-call | tf_op jit(solution)/shard_map/project/pallas_call | solution.py:774
  70.0 9.0 %filter_spectrum.1.refs_4_ = f32[1536,512]{1,0:T(8,128)S(1)} custom-call(s32[1]{0:T(128)} %bitcast.15.here_ref, f32[192,2048]{1,0:T(8,128)} %kernel_ref.2, s32[192,1]{1,0:T(8,128)S(1)} %copy.27.pad_ref, bf16[512,512]{1,0:T(8,128)(2,1)} %fusion.high_ref.refs_5_, bf16[512,512]{1,0:T(8,128)(2,1)} %subtract_convert_fusion.low_ref, ...), custom_call_target="tpu_custom_call" | custom-call | tf_op jit(solution)/shard_map/filter_spectrum/pallas_call | solution.py:709
  84.2 6.2 %conv_forward.1 = (bf16[192,512]{1,0:T(8,128)(2,1)S(1)}, bf16[192,512]{1,0:T(8,128)(2,1)S(1)}, bf16[192,512]{1,0:T(8,128)(2,1)S(1)}, bf16[192,512]{1,0:T(8,128)(2,1)S(1)}, bf16[1536,512]{1,0:T(8,128)(2,1)}) custom-call(s32[1]{0:T(128)} %bitcast.level_ref.here_ref.refs_0_, bf16[192,512]{1,0:T(8,128)(2,1)S(1)} %bitcast.61, ...), custom_call_target="tpu_custom_call" | custom-call | tf_op jit(solution)/shard_map/conv_forward/pallas_call | solution.py:274
  98.5 10.2 %collective-permute-done.21.refs_8_ = bf16[192,512]{1,0:T(8,128)(2,1)S(1)} collective-permute-done((bf16[192,512]{1,0:T(8,128)(2,1)S(1)}, bf16[192,512]{1,0:T(8,128)(2,1)S(1)}, u32[]{:S(2)}, u32[]{:S(2)}) %collective-permute-start.21) | collective-permute-done | bytes 196640 | tf_op jit(solution)/shard_map/ppermute | solution.py:368
  109.8 4.3 %collective-permute-done.31.refs_20_ = bf16[384,768]{1,0:T(8,128)(2,1)S(1)} collective-permute-done((bf16[384,768]{1,0:T(8,128)(2,1)S(1)}, bf16[384,768]{1,0:T(8,128)(2,1)S(1)}, u32[]{:S(2)}, u32[]{:S(2)}) %collective-permute-start.31) | collective-permute-done | bytes 589856 | tf_op jit(solution)/shard_map/ppermute | solution.py:368
  115.8 26.2 %feed_forward.1 = (bf16[768,512]{1,0:T(8,128)(2,1)S(1)}, bf16[512,768]{1,0:T(8,128)(2,1)}, f32[512,768]{1,0:T(8,128)}, bf16[512,768]{1,0:T(8,128)(2,1)S(1)}, f32...) custom-call(s32[1]{0:T(128)} %bitcast.level_ref.here_ref.refs_0_, ...), custom_call_target="tpu_custom_call" | custom-call | tf_op jit(solution)/shard_map/feed_forward/pallas_call | solution.py:894
  145.6 6.1 %collective-permute-done.35.late_in = bf16[4,192,768]{2,1,0:T(8,128)(2,1)S(1)} collective-permute-done((bf16[4,192,768]{2,1,0:T(8,128)(2,1)S(1)}, bf16[4,192,768]{2,1,0:T(8,128)(2,1)S(1)}, u32[]{:S(2)}, u32[]{:S(2)}) %collective-permute-start.35) | collective-permute-done | bytes 1179680 | tf_op jit(solution)/shard_map/ppermute | solution.py:368
  151.7 3.9 %kept.1 = (bf16[2,4,120,768]{3,2,1,0:T(8,128)(2,1)}, bf16[2,4,120,768]{3,2,1,0:T(8,128)(2,1)}, bf16[2,4,120,768]{3,2,1,0:T(8,128)(2,1)}, bf16[2,4,120,768]{3,2,1,0:T(8,128)(2,1)}) custom-call(bf16[1536,768]{1,0:T(8,128)(2,1)S(1)} %get-tuple-element.122.up_ref, bf16[1536,768]{1,0:T(8,128)(2,1)S(1)} %copy-done.12, ...), custom_call_target="tpu_custom_call" | custom-call | tf_op jit(solution)/shard_map/kept/pallas_call | solution.py:1255
  162.5 4.2 %collective-permute-done.37.refs_3_ = bf16[192,512]{1,0:T(8,128)(2,1)S(1)} collective-permute-done((bf16[192,512]{1,0:T(8,128)(2,1)S(1)}, bf16[192,512]{1,0:T(8,128)(2,1)S(1)}, u32[]{:S(2)}, u32[]{:S(2)}) %collective-permute-start.37) | collective-permute-done | bytes 196640 | tf_op jit(solution)/shard_map/ppermute | solution.py:368
  166.7 11.6 %collective-permute-done.36.refs_2_ = bf16[192,512]{1,0:T(8,128)(2,1)S(1)} collective-permute-done((bf16[192,512]{1,0:T(8,128)(2,1)S(1)}, bf16[192,512]{1,0:T(8,128)(2,1)S(1)}, u32[]{:S(2)}, u32[]{:S(2)}) %collective-permute-start.36) | collective-permute-done | bytes 196640 | tf_op jit(solution)/shard_map/ppermute | solution.py:368
  178.3 6.4 %conv_mixed.1 = (bf16[4,192,512]{2,1,0:T(8,128)(2,1)}, bf16[1536,512]{1,0:T(8,128)(2,1)}) custom-call(s32[1]{0:T(128)} %bitcast.level_ref.here_ref.refs_0_, bf16[192,512]{1,0:T(8,128)(2,1)S(1)} %get-tuple-element.120.refs_0_, bf16[192,512]{1,0:T(8,128)(2,1)S(1)} %collective-permute-done.33.refs_1_, bf16[192,512]{1,0:T(8,128)(2,1)S(1)} %collective-permute-done.36.refs_2_, ...), custom_call_target="tpu_custom_call" | custom-call | tf_op jit(solution)/shard_map/conv_mixed/pallas_call | solution.py:293
  184.7 4.4 %all-to-all-start.1 = ((bf16[4,192,512]{2,1,0:T(8,128)(2,1)}), bf16[4,192,512]{2,1,0:T(8,128)(2,1)}, u32[]{:S(2)}, u32[]{:S(2)}) async-start(bf16[4,192,512]{2,1,0:T(8,128)(2,1)} %get-tuple-element.136), calls=%async_computation.1 | async-start | bytes 1572864 | tf_op jit(solution)/shard_map/all_to_all | solution.py:437
  191.3 3.2 %second_send.1 = (bf16[4,120,768]{2,1,0:T(8,128)(2,1)}, bf16[4,120,768]{2,1,0:T(8,128)(2,1)}) custom-call(bf16[2,4,120,768]{3,2,1,0:T(8,128)(2,1)} %get-tuple-element.130.up_ref, bf16[2,4,120,768]{3,2,1,0:T(8,128)(2,1)S(1)} %collective-permute-done.38.up_in, bf16[2,4,120,768]{3,2,1,0:T(8,128)(2,1)} %get-tuple-element.146.down_ref, ...), custom_call_target="tpu_custom_call" | custom-call | tf_op jit(solution)/shard_map/second_send/pallas_call | solution.py:1005
  196.6 3.1 %conv_filt.1.filt_ref = f32[3,192,768]{2,1,0:T(8,128)S(1)} custom-call(bf16[1536,512]{1,0:T(8,128)(2,1)S(1)} %copy-done.14, bf16[1536,512]{1,0:T(8,128)(2,1)S(1)} %copy-done.13, bf16[512,512]{1,0:T(8,128)(2,1)S(1)} %copy-done.2, f32[2,8,256]{2,1,0:T(8,128)S(1)} %copy-done.17), custom_call_target="tpu_custom_call" | custom-call | tf_op jit(solution)/shard_map/conv_filt/pallas_call | solution.py:313
  199.7 9.9 %all-to-all-done.1 = bf16[4,192,512]{2,1,0:T(8,128)(2,1)} async-done(((bf16[4,192,512]{2,1,0:T(8,128)(2,1)}), bf16[4,192,512]{2,1,0:T(8,128)(2,1)}, u32[]{:S(2)}, u32[]{:S(2)}) %all-to-all-start.1) | async-done | bytes 786464 | tf_op jit(solution)/shard_map/all_to_all | solution.py:437
  209.5 5.8 %rest_grads.1 = (bf16[4,264,768]{2,1,0:T(8,128)(2,1)}, bf16[4,264,768]{2,1,0:T(8,128)(2,1)}, bf16[768,512]{1,0:T(8,128)(2,1)}, bf16[768,512]{1,0:T(8,128)(2,1)}) custom-call(bf16[768,512]{1,0:T(8,128)(2,1)} %bitcast.23.mixed_ref, f32[768,512]{1,0:T(8,128)} %bitcast.64, f32[768,512]{1,0:T(8,128)} %bitcast.65, bf16[512,768]{1,0:T(8,128)(2,1)} %copy-done.3, ...), custom_call_target="tpu_custom_call" | custom-call | tf_op jit(solution)/shard_map/rest_grads/pallas_call | solution.py:1274
  215.4 3.2 %bulk_sum.1 = bf16[4,240,768]{2,1,0:T(8,128)(2,1)} custom-call(bf16[2,4,120,768]{3,2,1,0:T(8,128)(2,1)} %get-tuple-element.130.up_ref, bf16[2,4,120,768]{3,2,1,0:T(8,128)(2,1)S(1)} %copy-done.7, bf16[4,120,768]{2,1,0:T(8,128)(2,1)S(1)} %collective-permute-done.40.up_last, bf16[2,4,120,768]{3,2,1,0:T(8,128)(2,1)} %get-tuple-element.146.down_ref, ...), custom_call_target="tpu_custom_call" | custom-call | tf_op jit(solution)/shard_map/bulk_sum/pallas_call | solution.py:1005
  218.6 3.6 %all-to-all-start.2 = ((bf16[4,240,768]{2,1,0:T(8,128)(2,1)}), bf16[4,240,768]{2,1,0:T(8,128)(2,1)S(1)}, u32[]{:S(2)}, u32[]{:S(2)}) async-start(bf16[4,240,768]{2,1,0:T(8,128)(2,1)} %bulk_sum.1), calls=%async_computation.2 | async-start | bytes 2949120 | tf_op jit(solution)/shard_map/all_to_all | solution.py:437
  222.2 3.7 %collective-permute-done.42.far_ref = bf16[4,264,768]{2,1,0:T(8,128)(2,1)S(1)} collective-permute-done((bf16[4,264,768]{2,1,0:T(8,128)(2,1)}, bf16[4,264,768]{2,1,0:T(8,128)(2,1)S(1)}, u32[]{:S(2)}, u32[]{:S(2)}) %collective-permute-start.42) | collective-permute-done | bytes 1622048 | tf_op jit(solution)/shard_map/ppermute | solution.py:368
  231.3 9.1 %first_norm_back.1 = (f32[512,768]{1,0:T(8,128)}, f32[1,768]{1,0:T(1,128)S(1)}) custom-call(s32[1]{0:T(128)} %bitcast.level_ref.here_ref.refs_0_, bf16[4,192,512]{2,1,0:T(8,128)(2,1)} %bitcast.68, bf16[4,192,512]{2,1,0:T(8,128)(2,1)} %bitcast.69, bf16[4,192,512]{2,1,0:T(8,128)(2,1)} %bitcast.62, bf16[192,768]{1,0:T(8,128)(2,1)} %bitcast.50, ...), custom_call_target="tpu_custom_call" | custom-call | tf_op jit(solution)/shard_map/first_norm_back/pallas_call | solution.py:1295
  240.4 8.8 %collective-permute-done.44.p2 = bf16[264,768]{1,0:T(8,128)(2,1)S(1)} collective-permute-done((bf16[264,768]{1,0:T(8,128)(2,1)S(1)}, bf16[264,768]{1,0:T(8,128)(2,1)S(1)}, u32[]{:S(2)}, u32[]{:S(2)}) %collective-permute-start.44) | collective-permute-done | bytes 405536 | tf_op jit(solution)/shard_map/ppermute | solution.py:368
  254.0 3.7 %collective-permute-done.46.refs_1_ = bf16[56,768]{1,0:T(8,128)(2,1)S(1)} collective-permute-done((bf16[56,768]{1,0:T(8,128)(2,1)S(1)}, bf16[56,768]{1,0:T(8,128)(2,1)S(1)}, u32[]{:S(2)}, u32[]{:S(2)}) %collective-permute-start.46) | collective-permute-done | bytes 86048 | tf_op jit(solution)/shard_map/ppermute | solution.py:368
  257.7 5.3 %collective-permute-done.47.refs_2_ = bf16[56,768]{1,0:T(8,128)(2,1)S(1)} collective-permute-done((bf16[56,768]{1,0:T(8,128)(2,1)S(1)}, bf16[56,768]{1,0:T(8,128)(2,1)S(1)}, u32[]{:S(2)}, u32[]{:S(2)}) %collective-permute-start.47) | collective-permute-done | bytes 86048 | tf_op jit(solution)/shard_map/ppermute | solution.py:368
  266.9 13.1 %collective-permute-done.51.refs_3_ = bf16[368,768]{1,0:T(8,128)(2,1)S(1)} collective-permute-done((bf16[368,768]{1,0:T(8,128)(2,1)S(1)}, bf16[368,768]{1,0:T(8,128)(2,1)S(1)}, u32[]{:S(2)}, u32[]{:S(2)}) %collective-permute-start.51) | collective-permute-done | bytes 565280 | tf_op jit(solution)/shard_map/ppermute | solution.py:368
  280.1 9.2 %collective-permute-done.50.refs_2_ = bf16[368,768]{1,0:T(8,128)(2,1)S(1)} collective-permute-done((bf16[368,768]{1,0:T(8,128)(2,1)S(1)}, bf16[368,768]{1,0:T(8,128)(2,1)S(1)}, u32[]{:S(2)}, u32[]{:S(2)}) %collective-permute-start.50) | collective-permute-done | bytes 565280 | tf_op jit(solution)/shard_map/ppermute | solution.py:368
  292.0 5.0 %unpack.1 = (f32[768,768]{1,0:T(8,128)}, f32[768,768]{1,0:T(8,128)}, f32[192,768]{1,0:T(8,128)}, f32[3,192,768]{2,1,0:T(8,128)}, f32[192,2048]{1,0:T(8,128)}, /*index=5*/f32[768]{0:T(1024)}, f32[768]{0:T(1024)}) custom-call(s32[1]{0:T(128)} %bitcast.15.here_ref, bf16[368,768]{1,0:T(8,128)(2,1)S(1)} %mesh_sum.1.refs_0_, ...), custom_call_target="tpu_custom_call" | custom-call | tf_op jit(solution)/shard_map/unpack/pallas_call | solution.py:1329
  (184 shorter events, 83.6 us)
Async XLA Ops:
  9.4 12.5 %collective-permute-start.3 = (bf16[192,768]{1,0:T(8,128)(2,1)S(1)}, bf16[192,768]{1,0:T(8,128)(2,1)S(1)}, u32[]{:S(2)}, u32[]{:S(2)}) collective-permute-start(bf16[192,768]{1,0:T(8,128)(2,1)S(1)} %bitcast.45), channel_id=1, source_target_pairs={{0,24},{4,28},{8,16},{12,20},{16,8},{20,12},{24,0},{28,4},{1,25},{... | collective-permute-start | bytes 884744 | tf_op jit(solution)/shard_map/ppermute | solution.py:368
  12.1 13.0 %collective-permute-start.2 = (bf16[192,768]{1,0:T(8,128)(2,1)S(1)}, bf16[192,768]{1,0:T(8,128)(2,1)}, u32[]{:S(2)}, u32[]{:S(2)}) collective-permute-start(bf16[192,768]{1,0:T(8,128)(2,1)S(1)} %bitcast.46), channel_id=1, source_target_pairs={{0,16},{4,20},{8,24},{12,28},{16,0},{20,4},{24,8},{28,12},{1,17},{... | collective-permute-start | bytes 884744 | tf_op jit(solution)/shard_map/ppermute | solution.py:368
  12.6 12.6 %collective-permute-start.1 = (bf16[192,768]{1,0:T(8,128)(2,1)S(1)}, bf16[192,768]{1,0:T(8,128)(2,1)}, u32[]{:S(2)}, u32[]{:S(2)}) collective-permute-start(bf16[192,768]{1,0:T(8,128)(2,1)S(1)} %bitcast.47), channel_id=1, source_target_pairs={{0,8},{4,12},{8,0},{12,4},{16,24},{20,28},{24,16},{28,20},{1,9},{5... | collective-permute-start | bytes 884744 | tf_op jit(solution)/shard_map/ppermute | solution.py:368
  28.8 32.3 %all-to-all-start = ((bf16[4,2,96,768]{3,2,1,0:T(8,128)(2,1)}), bf16[4,2,96,768]{3,2,1,0:T(8,128)(2,1)}, u32[]{:S(2)}, u32[]{:S(2)}) async-start(bf16[4,2,96,768]{3,2,1,0:T(8,128)(2,1)} %broadcast_in_dim.36), calls=%async_computation | async-start | bytes 2359296 | tf_op jit(solution)/shard_map/all_to_all | solution.py:437
  36.3 14.1 %collective-permute-start.11 = (bf16[192,768]{1,0:T(8,128)(2,1)S(1)}, bf16[192,768]{1,0:T(8,128)(2,1)S(1)}, u32[]{:S(2)}, u32[]{:S(2)}) collective-permute-start(bf16[192,768]{1,0:T(8,128)(2,1)S(1)} %bitcast.52), channel_id=1, source_target_pairs={{0,16},{4,20},{8,24},{12,28},{16,0},{20,4},{24,8},{28,12},{1,17},{... | collective-permute-start | bytes 884744 | tf_op jit(solution)/shard_map/ppermute | solution.py:368
  36.8 13.7 %collective-permute-start.10 = (bf16[192,768]{1,0:T(8,128)(2,1)S(1)}, bf16[192,768]{1,0:T(8,128)(2,1)S(1)}, u32[]{:S(2)}, u32[]{:S(2)}) collective-permute-start(bf16[192,768]{1,0:T(8,128)(2,1)S(1)} %bitcast.53), channel_id=1, source_target_pairs={{0,8},{4,12},{8,0},{12,4},{16,24},{20,28},{24,16},{28,20},{1,9},{5... | collective-permute-start | bytes 884744 | tf_op jit(solution)/shard_map/ppermute | solution.py:368
  37.3 13.6 %collective-permute-start.13 = (bf16[192,768]{1,0:T(8,128)(2,1)S(1)}, bf16[192,768]{1,0:T(8,128)(2,1)S(1)}, u32[]{:S(2)}, u32[]{:S(2)}) collective-permute-start(bf16[192,768]{1,0:T(8,128)(2,1)S(1)} %bitcast.54), channel_id=1, source_target_pairs={{0,4},{4,0},{8,12},{12,8},{16,20},{20,16},{24,28},{28,24},{1,5},{5... | collective-permute-start | bytes 884744 | tf_op jit(solution)/shard_map/ppermute | solution.py:368
  37.3 13.6 %collective-permute-start.5 = (bf16[192,768]{1,0:T(8,128)(2,1)}, bf16[192,768]{1,0:T(8,128)(2,1)}, u32[]{:S(2)}, u32[]{:S(2)}) collective-permute-start(bf16[192,768]{1,0:T(8,128)(2,1)} %collective-permute-done.1.refs_1_.refs_4_), channel_id=1, source_target_pairs={{0,4},{4,0},{8,12},{12,8},{16,20},{20,16},{24,28},{28,24},{1,5},{5... | collective-permute-start | bytes 884744 | tf_op jit(solution)/shard_map/ppermute | solution.py:368
  62.4 20.1 %collective-permute-start.24 = (bf16[384,768]{1,0:T(8,128)(2,1)S(1)}, bf16[384,768]{1,0:T(8,128)(2,1)S(1)}, u32[]{:S(2)}, u32[]{:S(2)}) collective-permute-start(bf16[384,768]{1,0:T(8,128)(2,1)S(1)} %bitcast.37), channel_id=1, source_target_pairs={{0,16},{4,20},{8,24},{12,28},{16,0},{20,4},{24,8},{28,12},{1,17},{... | collective-permute-start | bytes 1769480 | tf_op jit(solution)/shard_map/ppermute | solution.py:368
  64.0 18.5 %collective-permute-start.23 = (bf16[384,768]{1,0:T(8,128)(2,1)S(1)}, bf16[384,768]{1,0:T(8,128)(2,1)S(1)}, u32[]{:S(2)}, u32[]{:S(2)}) collective-permute-start(bf16[384,768]{1,0:T(8,128)(2,1)S(1)} %bitcast.41), channel_id=1, source_target_pairs={{0,8},{4,12},{8,0},{12,4},{16,24},{20,28},{24,16},{28,20},{1,9},{5... | collective-permute-start | bytes 1769480 | tf_op jit(solution)/shard_map/ppermute | solution.py:368
  65.5 14.2 %collective-permute-start.17 = (bf16[192,512]{1,0:T(8,128)(2,1)}, bf16[192,512]{1,0:T(8,128)(2,1)S(1)}, u32[]{:S(2)}, u32[]{:S(2)}) collective-permute-start(bf16[192,512]{1,0:T(8,128)(2,1)} %bitcast.14), channel_id=1, source_target_pairs={{0,1},{1,0},{2,3},{3,2},{4,5},{5,4},{6,7},{7,6},{8,9},{9,8},{10,11... | collective-permute-start | bytes 589832 | tf_op jit(solution)/shard_map/ppermute | solution.py:368
  65.5 17.0 %collective-permute-start.18 = (bf16[192,512]{1,0:T(8,128)(2,1)}, bf16[192,512]{1,0:T(8,128)(2,1)S(1)}, u32[]{:S(2)}, u32[]{:S(2)}) collective-permute-start(bf16[192,512]{1,0:T(8,128)(2,1)} %bitcast.17), channel_id=1, source_target_pairs={{0,2},{1,3},{2,0},{3,1},{4,6},{5,7},{6,4},{7,5},{8,10},{9,11},{10,... | collective-permute-start | bytes 589832 | tf_op jit(solution)/shard_map/ppermute | solution.py:368
  67.5 15.0 %collective-permute-start.19 = (bf16[192,512]{1,0:T(8,128)(2,1)}, bf16[192,512]{1,0:T(8,128)(2,1)S(1)}, u32[]{:S(2)}, u32[]{:S(2)}) collective-permute-start(bf16[192,512]{1,0:T(8,128)(2,1)} %bitcast.18), channel_id=1, source_target_pairs={{0,3},{1,2},{2,1},{3,0},{4,7},{5,6},{6,5},{7,4},{8,11},{9,10},{10,... | collective-permute-start | bytes 589832 | tf_op jit(solution)/shard_map/ppermute | solution.py:368
  82.6 26.1 %collective-permute-start.25 = (bf16[2,384,768]{2,1,0:T(8,128)(2,1)S(1)}, bf16[2,384,768]{2,1,0:T(8,128)(2,1)S(1)}, u32[]{:S(2)}, u32[]{:S(2)}) collective-permute-start(bf16[2,384,768]{2,1,0:T(8,128)(2,1)S(1)} %get-tuple-element.115), channel_id=1, source_target_pairs={{0,16},{4,20},{8,24},{12,28},{16,0},{20,4},{24,8},{28,12},{1,17},{... | collective-permute-start | bytes 3538952 | tf_op jit(solution)/shard_map/ppermute | solution.py:368
  83.6 25.1 %collective-permute-start.27 = (bf16[2,384,768]{2,1,0:T(8,128)(2,1)S(1)}, bf16[2,384,768]{2,1,0:T(8,128)(2,1)S(1)}, u32[]{:S(2)}, u32[]{:S(2)}) collective-permute-start(bf16[2,384,768]{2,1,0:T(8,128)(2,1)S(1)} %get-tuple-element.117), channel_id=1, source_target_pairs={{0,8},{4,12},{8,0},{12,4},{16,24},{20,28},{24,16},{28,20},{1,9},{5... | collective-permute-start | bytes 3538952 | tf_op jit(solution)/shard_map/ppermute | solution.py:368
  93.2 15.5 %collective-permute-start.21 = (bf16[192,512]{1,0:T(8,128)(2,1)S(1)}, bf16[192,512]{1,0:T(8,128)(2,1)S(1)}, u32[]{:S(2)}, u32[]{:S(2)}) collective-permute-start(bf16[192,512]{1,0:T(8,128)(2,1)S(1)} %get-tuple-element.108), channel_id=1, source_target_pairs={{0,2},{1,3},{2,0},{3,1},{4,6},{5,7},{6,4},{7,5},{8,10},{9,11},{10,... | collective-permute-start | bytes 589832 | tf_op jit(solution)/shard_map/ppermute | solution.py:368
  94.1 14.6 %collective-permute-start.22 = (bf16[192,512]{1,0:T(8,128)(2,1)S(1)}, bf16[192,512]{1,0:T(8,128)(2,1)S(1)}, u32[]{:S(2)}, u32[]{:S(2)}) collective-permute-start(bf16[192,512]{1,0:T(8,128)(2,1)S(1)} %get-tuple-element.109), channel_id=1, source_target_pairs={{0,3},{1,2},{2,1},{3,0},{4,7},{5,6},{6,5},{7,4},{8,11},{9,10},{10,... | collective-permute-start | bytes 589832 | tf_op jit(solution)/shard_map/ppermute | solution.py:368
  155.5 34.5 %collective-permute-start.38 = (bf16[2,4,120,768]{3,2,1,0:T(8,128)(2,1)}, bf16[2,4,120,768]{3,2,1,0:T(8,128)(2,1)S(1)}, u32[]{:S(2)}, u32[]{:S(2)}) collective-permute-start(bf16[2,4,120,768]{3,2,1,0:T(8,128)(2,1)} %get-tuple-element.144), channel_id=1, source_target_pairs={{0,8},{4,12},{8,0},{12,4},{16,24},{20,28},{24,16},{28,20},{1,9},{5... | collective-permute-start | bytes 4423688 | tf_op jit(solution)/shard_map/ppermute | solution.py:368
  157.0 34.3 %collective-permute-start.39 = (bf16[2,4,120,768]{3,2,1,0:T(8,128)(2,1)}, bf16[2,4,120,768]{3,2,1,0:T(8,128)(2,1)S(1)}, u32[]{:S(2)}, u32[]{:S(2)}) collective-permute-start(bf16[2,4,120,768]{3,2,1,0:T(8,128)(2,1)} %get-tuple-element.147), channel_id=1, source_target_pairs={{0,16},{4,20},{8,24},{12,28},{16,0},{20,4},{24,8},{28,12},{1,17},{... | collective-permute-start | bytes 4423688 | tf_op jit(solution)/shard_map/ppermute | solution.py:368
  159.4 18.9 %collective-permute-start.36 = (bf16[192,512]{1,0:T(8,128)(2,1)S(1)}, bf16[192,512]{1,0:T(8,128)(2,1)S(1)}, u32[]{:S(2)}, u32[]{:S(2)}) collective-permute-start(bf16[192,512]{1,0:T(8,128)(2,1)S(1)} %get-tuple-element.132), channel_id=1, source_target_pairs={{0,2},{1,3},{2,0},{3,1},{4,6},{5,7},{6,4},{7,5},{8,10},{9,11},{10,... | collective-permute-start | bytes 589832 | tf_op jit(solution)/shard_map/ppermute | solution.py:368
  162.0 16.4 %collective-permute-start.33 = (bf16[192,512]{1,0:T(8,128)(2,1)S(1)}, bf16[192,512]{1,0:T(8,128)(2,1)S(1)}, u32[]{:S(2)}, u32[]{:S(2)}) collective-permute-start(bf16[192,512]{1,0:T(8,128)(2,1)S(1)} %get-tuple-element.121), channel_id=1, source_target_pairs={{0,1},{1,0},{2,3},{3,2},{4,5},{5,4},{6,7},{7,6},{8,9},{9,8},{10,11... | collective-permute-start | bytes 589832 | tf_op jit(solution)/shard_map/ppermute | solution.py:368
  184.7 24.8 %all-to-all-start.1 = ((bf16[4,192,512]{2,1,0:T(8,128)(2,1)}), bf16[4,192,512]{2,1,0:T(8,128)(2,1)}, u32[]{:S(2)}, u32[]{:S(2)}) async-start(bf16[4,192,512]{2,1,0:T(8,128)(2,1)} %get-tuple-element.136), calls=%async_computation.1 | async-start | bytes 1572864 | tf_op jit(solution)/shard_map/all_to_all | solution.py:437
  194.5 20.8 %collective-permute-start.40 = (bf16[4,120,768]{2,1,0:T(8,128)(2,1)}, bf16[4,120,768]{2,1,0:T(8,128)(2,1)S(1)}, u32[]{:S(2)}, u32[]{:S(2)}) collective-permute-start(bf16[4,120,768]{2,1,0:T(8,128)(2,1)} %get-tuple-element.149), channel_id=1, source_target_pairs={{0,16},{4,20},{8,24},{12,28},{16,0},{20,4},{24,8},{28,12},{1,17},{... | collective-permute-start | bytes 2211848 | tf_op jit(solution)/shard_map/ppermute | solution.py:368
  195.4 20.0 %collective-permute-start.41 = (bf16[4,120,768]{2,1,0:T(8,128)(2,1)}, bf16[4,120,768]{2,1,0:T(8,128)(2,1)}, u32[]{:S(2)}, u32[]{:S(2)}) collective-permute-start(bf16[4,120,768]{2,1,0:T(8,128)(2,1)} %get-tuple-element.152), channel_id=1, source_target_pairs={{0,8},{4,12},{8,0},{12,4},{16,24},{20,28},{24,16},{28,20},{1,9},{5... | collective-permute-start | bytes 2211848 | tf_op jit(solution)/shard_map/ppermute | solution.py:368
  218.6 44.5 %all-to-all-start.2 = ((bf16[4,240,768]{2,1,0:T(8,128)(2,1)}), bf16[4,240,768]{2,1,0:T(8,128)(2,1)S(1)}, u32[]{:S(2)}, u32[]{:S(2)}) async-start(bf16[4,240,768]{2,1,0:T(8,128)(2,1)} %bulk_sum.1), calls=%async_computation.2 | async-start | bytes 2949120 | tf_op jit(solution)/shard_map/all_to_all | solution.py:437
  227.7 12.7 %collective-permute-start.43 = (bf16[264,768]{1,0:T(8,128)(2,1)S(1)}, bf16[264,768]{1,0:T(8,128)(2,1)S(1)}, u32[]{:S(2)}, u32[]{:S(2)}) collective-permute-start(bf16[264,768]{1,0:T(8,128)(2,1)S(1)} %get-tuple-element.156), channel_id=1, source_target_pairs={{0,8},{4,12},{8,0},{12,4},{16,24},{20,28},{24,16},{28,20},{1,9},{5... | collective-permute-start | bytes 1216520 | tf_op jit(solution)/shard_map/ppermute | solution.py:368
  229.3 19.8 %collective-permute-start.44 = (bf16[264,768]{1,0:T(8,128)(2,1)S(1)}, bf16[264,768]{1,0:T(8,128)(2,1)S(1)}, u32[]{:S(2)}, u32[]{:S(2)}) collective-permute-start(bf16[264,768]{1,0:T(8,128)(2,1)S(1)} %get-tuple-element.158), channel_id=1, source_target_pairs={{0,16},{4,20},{8,24},{12,28},{16,0},{20,4},{24,8},{28,12},{1,17},{... | collective-permute-start | bytes 1216520 | tf_op jit(solution)/shard_map/ppermute | solution.py:368
  229.8 19.3 %collective-permute-start.45 = (bf16[264,768]{1,0:T(8,128)(2,1)S(1)}, bf16[264,768]{1,0:T(8,128)(2,1)S(1)}, u32[]{:S(2)}, u32[]{:S(2)}) collective-permute-start(bf16[264,768]{1,0:T(8,128)(2,1)S(1)} %get-tuple-element.160), channel_id=1, source_target_pairs={{0,24},{4,28},{8,16},{12,20},{16,8},{20,12},{24,0},{28,4},{1,25},{... | collective-permute-start | bytes 1216520 | tf_op jit(solution)/shard_map/ppermute | solution.py:368
  263.4 16.7 %collective-permute-start.51 = (bf16[368,768]{1,0:T(8,128)(2,1)S(1)}, bf16[368,768]{1,0:T(8,128)(2,1)S(1)}, u32[]{:S(2)}, u32[]{:S(2)}) collective-permute-start(bf16[368,768]{1,0:T(8,128)(2,1)S(1)} %mesh_sum.1.refs_0_), channel_id=1, source_target_pairs={{0,24},{4,28},{8,16},{12,20},{16,8},{20,12},{24,0},{28,4},{1,25},{... | collective-permute-start | bytes 1695752 | tf_op jit(solution)/shard_map/ppermute | solution.py:368
  264.9 24.3 %collective-permute-start.50 = (bf16[368,768]{1,0:T(8,128)(2,1)S(1)}, bf16[368,768]{1,0:T(8,128)(2,1)S(1)}, u32[]{:S(2)}, u32[]{:S(2)}) collective-permute-start(bf16[368,768]{1,0:T(8,128)(2,1)S(1)} %mesh_sum.1.refs_0_), channel_id=1, source_target_pairs={{0,16},{4,20},{8,24},{12,28},{16,0},{20,4},{24,8},{28,12},{1,17},{... | collective-permute-start | bytes 1695752 | tf_op jit(solution)/shard_map/ppermute | solution.py:368
  266.4 22.9 %collective-permute-start.49 = (bf16[368,768]{1,0:T(8,128)(2,1)S(1)}, bf16[368,768]{1,0:T(8,128)(2,1)S(1)}, u32[]{:S(2)}, u32[]{:S(2)}) collective-permute-start(bf16[368,768]{1,0:T(8,128)(2,1)S(1)} %mesh_sum.1.refs_0_), channel_id=1, source_target_pairs={{0,8},{4,12},{8,0},{12,4},{16,24},{20,28},{24,16},{28,20},{1,9},{5... | collective-permute-start | bytes 1695752 | tf_op jit(solution)/shard_map/ppermute | solution.py:368
  266.9 22.9 %collective-permute-start.52 = (bf16[368,768]{1,0:T(8,128)(2,1)S(1)}, bf16[368,768]{1,0:T(8,128)(2,1)S(1)}, u32[]{:S(2)}, u32[]{:S(2)}) collective-permute-start(bf16[368,768]{1,0:T(8,128)(2,1)S(1)} %mesh_sum.1.refs_0_), channel_id=1, source_target_pairs={{0,4},{4,0},{8,12},{12,8},{16,20},{20,16},{24,28},{28,24},{1,5},{5... | collective-permute-start | bytes 1695752 | tf_op jit(solution)/shard_map/ppermute | solution.py:368
  (58 other events, 520.1 us)
